TPU v7x, 32 devices: a whole 2x2x4 slice. The times are simulated.
32 devices in a mesh: fsdp: 2 (over y), context: 4 (over z), tensor: 4 (over x, core).
Axes of the slice: x: 2, y: 2, z: 4, core: 2. Of those that a mesh axis runs over, the one named last changes fastest.
Arguments:
- frames: bfloat16 [1536, 4, 1536], P(('context', 'tensor'), 'fsdp'), may hold values from -6 to 6
- text_states: bfloat16 [64, 4, 1536], P(None, 'fsdp'), may hold values from -6 to 6
- cotangent: bfloat16 [1536, 4, 1536], P(('context', 'tensor'), 'fsdp'), may hold values from -6 to 6
- self_query: bfloat16 [1536, 1536], P(('fsdp', 'context'), 'tensor'), may hold values from -0.15625 to 0.15625
- self_key: bfloat16 [1536, 1536], P(('fsdp', 'context'), 'tensor'), may hold values from -0.15625 to 0.15625
- self_value: bfloat16 [1536, 1536], P(('fsdp', 'context'), 'tensor'), may hold values from -0.15625 to 0.15625
- self_out: bfloat16 [1536, 1536], P(('fsdp', 'context'), 'tensor'), may hold values from -1.25 to 1.25
- cross_query: bfloat16 [1536, 1536], P(('fsdp', 'context'), 'tensor'), may hold values from -0.15625 to 0.15625
- cross_key: bfloat16 [1536, 1536], P(('fsdp', 'context'), 'tensor'), may hold values from -0.15625 to 0.15625
- cross_value: bfloat16 [1536, 1536], P(('fsdp', 'context'), 'tensor'), may hold values from -0.15625 to 0.15625
- cross_out: bfloat16 [1536, 1536], P(('fsdp', 'context'), 'tensor'), may hold values from -0.875 to 0.875
- feed_in: bfloat16 [1536, 6144], P(('fsdp', 'context'), 'tensor'), may hold values from -0.15625 to 0.15625
- feed_out: bfloat16 [1536, 6144], P(('fsdp', 'context'), 'tensor'), may hold values from -0.078125 to 0.078125
- first_gain: bfloat16 [1536], P(('fsdp', 'context')), may hold values from 0.25 to 1.75
- first_shift: bfloat16 [1536], P(('fsdp', 'context')), may hold values from -3 to 3
- second_gain: bfloat16 [1536], P(('fsdp', 'context')), may hold values from 0.25 to 1.75
- second_shift: bfloat16 [1536], P(('fsdp', 'context')), may hold values from -3 to 3
- third_gain: bfloat16 [1536], P(('fsdp', 'context')), may hold values from 0.25 to 1.75
- third_shift: bfloat16 [1536], P(('fsdp', 'context')), may hold values from -3 to 3
Outputs:
- layer_out: bfloat16 [1536, 4, 1536], P(('context', 'tensor'), 'fsdp')
- frames_grad: float32 [1536, 4, 1536], P(('context', 'tensor'), 'fsdp')
- text_grad: float32 [64, 4, 1536], P(None, 'fsdp')
- self_query_grad: float32 [1536, 1536], P(('fsdp', 'context'), 'tensor')
- self_key_grad: float32 [1536, 1536], P(('fsdp', 'context'), 'tensor')
- self_value_grad: float32 [1536, 1536], P(('fsdp', 'context'), 'tensor')
- self_out_grad: float32 [1536, 1536], P(('fsdp', 'context'), 'tensor')
- cross_query_grad: float32 [1536, 1536], P(('fsdp', 'context'), 'tensor')
- cross_key_grad: float32 [1536, 1536], P(('fsdp', 'context'), 'tensor')
- cross_value_grad: float32 [1536, 1536], P(('fsdp', 'context'), 'tensor')
- cross_out_grad: float32 [1536, 1536], P(('fsdp', 'context'), 'tensor')
- feed_in_grad: float32 [1536, 6144], P(('fsdp', 'context'), 'tensor')
- feed_out_grad: float32 [1536, 6144], P(('fsdp', 'context'), 'tensor')
- first_gain_grad: float32 [1536], P(('fsdp', 'context'))
- first_shift_grad: float32 [1536], P(('fsdp', 'context'))
- second_gain_grad: float32 [1536], P(('fsdp', 'context'))
- second_shift_grad: float32 [1536], P(('fsdp', 'context'))
- third_gain_grad: float32 [1536], P(('fsdp', 'context'))
- third_shift_grad: float32 [1536], P(('fsdp', 'context'))
All inputs are finite; a program needn't handle non-finite values.
Results may differ from a plain program's by a relative error of at most 0.015.
Values may be sent and summed in bfloat16 or wider, within the bound.
No kernel may reach another device: no remote copies, remote signals or barrier semaphores. Data moves between devices by JAX's collectives and lax.ppermute only.
A program may use at most 192 MiB of HBM per device.

v0:
```python
import functools

import jax
import jax.numpy as jnp
from jax import lax
from jax.experimental import pallas as pl
from jax.experimental.pallas import tpu as pltpu
from jax.sharding import PartitionSpec as P

HEAD = 64
low = jnp.bfloat16
wide = jnp.float32
masked_score = -1e30
scale = HEAD**-0.5


def dot(left, right, left_dim, right_dim):
    return lax.dot_general(
        left, right, (((left_dim,), (right_dim,)), ((), ())), preferred_element_type=wide
    )


def from_context(values, step, size):
    return lax.ppermute(values, "context", [((i + step) % size, i) for i in range(size)])


def from_fsdp(values, step, size):
    return lax.ppermute(values, "fsdp", [((i + step) % size, i) for i in range(size)])


def swap_tensor(values, mask, size):
    return lax.ppermute(values, "tensor", [(i, i ^ mask) for i in range(size)])


def shift_order(size):
    order = []
    for step in range(1, size // 2 + 1):
        order.append(step)
        if size - step != step:
            order.append(size - step)
    return order


def gather_group(shard, fsdp_size, context_size, axis=0):
    arrived = {0: shard}
    for step in shift_order(context_size):
        arrived[step] = from_context(shard, step, context_size)
    pieces = [arrived[step] for step in range(context_size)]
    for far in range(1, fsdp_size):
        there = {0: from_fsdp(shard, far, fsdp_size)}
        for step in shift_order(context_size):
            there[step] = from_fsdp(arrived[step], far, fsdp_size)
        pieces += [there[step] for step in range(context_size)]
    return jnp.concatenate(pieces, axis=axis)


def reduce_fsdp(near, far_blocks, fsdp_size):
    total = near
    for step in range(1, fsdp_size):
        total = total + from_fsdp(far_blocks[step - 1], fsdp_size - step, fsdp_size).astype(wide)
    return total


def reduce_context(total, context_size):
    rows = total.shape[0] // context_size
    result = total[:rows]
    for step in shift_order(context_size):
        piece = total[step * rows : (step + 1) * rows].astype(low)
        result = result + from_context(piece, context_size - step, context_size).astype(wide)
    return result


def weight_grad(left_rows, right_rows, fsdp_size, context_size):
    half = left_rows.shape[-1] // fsdp_size
    far = [
        dot(left_rows[:, step * half : (step + 1) * half], right_rows, 0, 0).astype(low)
        for step in range(1, fsdp_size)
    ]
    near = dot(left_rows[:, :half], right_rows, 0, 0)
    return reduce_context(reduce_fsdp(near, far, fsdp_size), context_size)


def gather_rows(values, tensor_size):
    blocks = [values]
    mask = tensor_size // 2
    while mask:
        blocks = blocks + [swap_tensor(block, mask, tensor_size) for block in blocks]
        mask //= 2
    return jnp.concatenate(blocks, axis=1)


def mask_order(tensor_size):
    order = [0]
    mask = tensor_size // 2
    while mask:
        order = order + [item ^ mask for item in order]
        mask //= 2
    return order


def scatter_rows(parts, tensor_size):
    mask = 1
    while mask < tensor_size:
        half = parts.shape[1] // 2
        arrived = swap_tensor(parts[:, half:].astype(low), mask, tensor_size)
        parts = parts[:, :half] + arrived.astype(wide)
        mask *= 2
    return parts


def norm_stats(values):
    centre = jnp.mean(values, axis=-1, keepdims=True)
    centred = values - centre
    spread = jnp.mean(centred * centred, axis=-1, keepdims=True)
    root = lax.rsqrt(spread + 1e-05)
    return centred * root, root


def layer_norm(values, gain, shift):
    scaled, unused = norm_stats(values)
    return (scaled * gain + shift).astype(low)


def norm_back(values, gain, grad):
    scaled, root = norm_stats(values)
    weighted = grad * gain
    inner = jnp.mean(weighted * scaled, axis=-1, keepdims=True)
    outer = jnp.mean(weighted, axis=-1, keepdims=True)
    piece = root * (weighted - outer - scaled * inner)
    return piece, jnp.sum(grad * scaled, axis=(0, 1)), jnp.sum(grad, axis=(0, 1))


def frame_places(shape, axis, frames, order, own):
    row = lax.broadcasted_iota(jnp.int32, shape, axis)
    place = jnp.zeros(shape, jnp.int32)
    for slot, mask in enumerate(order):
        inside = (row >= slot * frames) & (row < (slot + 1) * frames)
        place = jnp.where(inside, (own ^ mask) * frames + row - slot * frames, place)
    return place


def fill_bias(bias_ref, frames, order, own):
    shape = bias_ref.shape
    keys = frame_places(shape, 0, frames, order, own)
    queries = frame_places(shape, 1, frames, order, own)
    bias_ref[...] = jnp.where(keys <= queries, 0.0, masked_score).astype(wide)


def self_forward_kernel(frames, order, place_ref, rows_ref, out_ref, top_ref, bias_ref):
    blocks, block_rows = rows_ref.shape[0], rows_ref.shape[1]
    width = out_ref.shape[2]
    heads = width // HEAD
    own_block = place_ref[0]
    fill_bias(bias_ref, frames, order, place_ref[1])

    def slot_of(block):
        return lax.rem(own_block - block + blocks, blocks)

    def query_block(block, unused):
        slot = slot_of(block)
        outs = []
        for head in range(heads):
            lanes = head * HEAD
            query = rows_ref[slot, :, lanes : lanes + HEAD] * scale

            def key_value(where, lanes=lanes):
                key = rows_ref[where, :, width + lanes : width + lanes + HEAD]
                value = rows_ref[where, :, 2 * width + lanes : 2 * width + lanes + HEAD]
                return key, value

            key, value = key_value(slot)
            scores = dot(key, query, 1, 1) + bias_ref[...]
            top = jnp.max(scores, axis=0, keepdims=True)
            weights = jnp.exp(scores - top)
            total = jnp.sum(weights, axis=0, keepdims=True)
            acc = dot(value, weights.astype(low), 0, 0)

            def step(past, carry, query=query, key_value=key_value):
                top, total, acc = carry
                key, value = key_value(slot_of(past))
                scores = dot(key, query, 1, 1)
                new_top = jnp.maximum(top, jnp.max(scores, axis=0, keepdims=True))
                weights = jnp.exp(scores - new_top)
                shrink = jnp.exp(top - new_top)
                total = total * shrink + jnp.sum(weights, axis=0, keepdims=True)
                acc = acc * shrink + dot(value, weights.astype(low), 0, 0)
                return new_top, total, acc

            top, total, acc = lax.fori_loop(0, block, step, (top, total, acc))
            outs.append((acc / total).T)
            top_ref[slot, head : head + 1, :] = top + jnp.log(total)
        out_ref[slot] = jnp.concatenate(outs, axis=1).astype(low)
        return unused

    lax.fori_loop(0, blocks, query_block, 0)


def self_backward_kernel(
    frames,
    order,
    place_ref,
    rows_ref,
    out_ref,
    top_ref,
    grad_ref,
    result_ref,
    bias_ref,
    delta_ref,
    query_acc,
    key_acc,
    value_acc,
):
    blocks, block_rows = rows_ref.shape[0], rows_ref.shape[1]
    width = out_ref.shape[2]
    heads = width // HEAD
    own_block = place_ref[0]
    fill_bias(bias_ref, frames, order, place_ref[1])
    query_acc[...] = jnp.zeros_like(query_acc)

    def slot_of(block):
        return lax.rem(own_block - block + blocks, blocks)

    def fill_delta(slot, unused):
        for head in range(heads):
            lanes = head * HEAD
            product = out_ref[slot, :, lanes : lanes + HEAD].astype(wide) * grad_ref[
                slot, :, lanes : lanes + HEAD
            ].astype(wide)
            delta_ref[slot, head : head + 1, :] = jnp.sum(product.T, axis=0, keepdims=True)
        return unused

    lax.fori_loop(0, blocks, fill_delta, 0)

    def key_block(block, unused):
        slot = slot_of(block)
        for head in range(heads):
            lanes = head * HEAD
            key = rows_ref[slot, :, width + lanes : width + lanes + HEAD]
            value = rows_ref[slot, :, 2 * width + lanes : 2 * width + lanes + HEAD]

            def terms(where, bias, lanes=lanes, head=head, key=key, value=value):
                query = rows_ref[where, :, lanes : lanes + HEAD] * scale
                grad = grad_ref[where, :, lanes : lanes + HEAD]
                scores = dot(key, query, 1, 1)
                if bias is not None:
                    scores = scores + bias
                weights = jnp.exp(scores - top_ref[where, head : head + 1, :])
                grad_weights = dot(value, grad, 1, 1)
                grad_scores = (weights * (grad_weights - delta_ref[where, head : head + 1, :])).astype(low)
                query_acc[head, where] += dot(key, grad_scores, 0, 0)
                return dot(grad_scores, query, 1, 0), dot(weights.astype(low), grad, 1, 0)

            start = terms(slot, bias_ref[...])

            def step(later, carry, terms=terms):
                key_part, value_part = terms(slot_of(later), None)
                return carry[0] + key_part, carry[1] + value_part

            key_grad, value_grad = lax.fori_loop(block + 1, blocks, step, start)
            key_acc[head, slot] = key_grad
            value_acc[head, slot] = value_grad
        return unused

    lax.fori_loop(0, blocks, key_block, 0)

    def write(slot, unused):
        parts = [(query_acc[head, slot] * scale).T for head in range(heads)]
        parts += [key_acc[head, slot] for head in range(heads)]
        parts += [value_acc[head, slot] for head in range(heads)]
        rest = result_ref.shape[2] - 3 * width
        if rest:
            parts.append(jnp.zeros((block_rows, rest), wide))
        result_ref[slot] = jnp.concatenate(parts, axis=1).astype(low)
        return unused

    lax.fori_loop(0, blocks, write, 0)


smem = pl.BlockSpec(memory_space=pltpu.SMEM)
vmem = pl.BlockSpec(memory_space=pltpu.VMEM)
kernel_params = pltpu.CompilerParams(vmem_limit_bytes=40 * 1024 * 1024)


def self_forward(place, rows, width, frames, order):
    blocks, block_rows, unused = rows.shape
    heads = width // HEAD
    work = blocks * block_rows * blocks * block_rows * heads * 5 // 8
    return pl.pallas_call(
        functools.partial(self_forward_kernel, frames, order),
        out_shape=(
            jax.ShapeDtypeStruct((blocks, block_rows, width), low),
            jax.ShapeDtypeStruct((blocks, heads, block_rows), wide),
        ),
        in_specs=[smem, vmem],
        out_specs=(vmem, vmem),
        scratch_shapes=[pltpu.VMEM((block_rows, block_rows), wide)],
        compiler_params=kernel_params,
        cost_estimate=pl.CostEstimate(
            flops=work * 64 * 4, bytes_accessed=rows.size * 4, transcendentals=work
        ),
    )(place, rows)


def self_backward(place, rows, out, top, grad, frames, order):
    blocks, block_rows, full = rows.shape
    width = out.shape[2]
    heads = width // HEAD
    work = blocks * block_rows * blocks * block_rows * heads * 5 // 8
    return pl.pallas_call(
        functools.partial(self_backward_kernel, frames, order),
        out_shape=jax.ShapeDtypeStruct((blocks, block_rows, full), low),
        in_specs=[smem, vmem, vmem, vmem, vmem],
        out_specs=vmem,
        scratch_shapes=[
            pltpu.VMEM((block_rows, block_rows), wide),
            pltpu.VMEM((blocks, heads, block_rows), wide),
            pltpu.VMEM((heads, blocks, HEAD, block_rows), wide),
            pltpu.VMEM((heads, blocks, block_rows, HEAD), wide),
            pltpu.VMEM((heads, blocks, block_rows, HEAD), wide),
        ],
        compiler_params=kernel_params,
        cost_estimate=pl.CostEstimate(
            flops=work * 64 * 10, bytes_accessed=rows.size * 8, transcendentals=work
        ),
    )(place, rows, out, top, grad)


def cross_weights(query, key):
    scores = dot(key, query * scale, 1, 1)
    top = jnp.max(scores, axis=0, keepdims=True)
    weights = jnp.exp(scores - top)
    return weights / jnp.sum(weights, axis=0, keepdims=True)


def cross_forward_kernel(query_ref, key_ref, value_ref, out_ref):
    outs = []
    for head in range(query_ref.shape[2] // HEAD):
        lanes = slice(head * HEAD, (head + 1) * HEAD)
        weights = cross_weights(query_ref[0, :, lanes], key_ref[0, :, lanes])
        outs.append(dot(value_ref[0, :, lanes], weights.astype(low), 0, 0).T)
    out_ref[0] = jnp.concatenate(outs, axis=1).astype(low)


def cross_backward_kernel(query_ref, key_ref, value_ref, grad_ref, query_out, key_out, value_out):
    queries, keys, values = [], [], []
    for head in range(query_ref.shape[2] // HEAD):
        lanes = slice(head * HEAD, (head + 1) * HEAD)
        query, key, value = query_ref[0, :, lanes], key_ref[0, :, lanes], value_ref[0, :, lanes]
        grad = grad_ref[0, :, lanes]
        weights = cross_weights(query, key)
        grad_weights = dot(value, grad, 1, 1)
        inner = jnp.sum(weights * grad_weights, axis=0, keepdims=True)
        grad_scores = (weights * (grad_weights - inner)).astype(low)
        queries.append((dot(key, grad_scores, 0, 0) * scale).T)
        keys.append(dot(grad_scores, query * scale, 1, 0))
        values.append(dot(weights.astype(low), grad, 1, 0))
    query_out[0] = jnp.concatenate(queries, axis=1).astype(low)
    key_out[0] = jnp.concatenate(keys, axis=1)
    value_out[0] = jnp.concatenate(values, axis=1)


def clip_spec(shape):
    return pl.BlockSpec((1,) + tuple(shape[1:]), lambda clip: (clip, 0, 0))


def cross_forward(query, key, value):
    work = query.shape[0] * query.shape[1] * query.shape[2] * key.shape[1]
    return pl.pallas_call(
        cross_forward_kernel,
        grid=(query.shape[0],),
        out_shape=jax.ShapeDtypeStruct(query.shape, low),
        in_specs=[clip_spec(query.shape), clip_spec(key.shape), clip_spec(value.shape)],
        out_specs=clip_spec(query.shape),
        compiler_params=kernel_params,
        cost_estimate=pl.CostEstimate(
            flops=4 * work, bytes_accessed=4 * query.size, transcendentals=work // 64
        ),
    )(query, key, value)


def cross_backward(query, key, value, grad):
    work = query.shape[0] * query.shape[1] * query.shape[2] * key.shape[1]
    return pl.pallas_call(
        cross_backward_kernel,
        grid=(query.shape[0],),
        out_shape=(
            jax.ShapeDtypeStruct(query.shape, low),
            jax.ShapeDtypeStruct(key.shape, wide),
            jax.ShapeDtypeStruct(value.shape, wide),
        ),
        in_specs=[
            clip_spec(query.shape),
            clip_spec(key.shape),
            clip_spec(value.shape),
            clip_spec(grad.shape),
        ],
        out_specs=(clip_spec(query.shape), clip_spec(key.shape), clip_spec(value.shape)),
        compiler_params=kernel_params,
        cost_estimate=pl.CostEstimate(
            flops=10 * work, bytes_accessed=8 * query.size, transcendentals=work // 64
        ),
    )(query, key, value, grad)


def pick(values, index):
    return lax.dynamic_index_in_dim(values, index, 0, keepdims=False)


def to_heads(chunks, own, size):
    slots = {0: pick(chunks, own)}
    for step in shift_order(size):
        chunk = pick(chunks, lax.rem(own + step, size))
        slots[step] = from_context(chunk, size - step, size)
    return jnp.stack([slots[step] for step in range(size)])


def to_frames(slots, own, size):
    arrived = {0: slots[0]}
    for step in shift_order(size):
        arrived[step] = from_context(slots[step], step, size)
    stacked = jnp.stack([arrived[step] for step in range(size)])
    return jnp.stack([pick(stacked, lax.rem(j - own + size, size)) for j in range(size)])


def relative_columns(own_fsdp, own_context, fsdp_size, context_size, width):
    block = width // (fsdp_size * context_size)
    there = lax.broadcasted_iota(jnp.int32, (width, width), 0)
    here = lax.broadcasted_iota(jnp.int32, (width, width), 1)
    far = lax.rem(here // (block * context_size) + own_fsdp, fsdp_size)
    step = lax.rem(lax.rem(here // block, context_size) + own_context, context_size)
    source = (far * context_size + step) * block + lax.rem(here, block)
    return (there == source).astype(low)


def on_device(sizes, frames, text_states, cotangent, *parameters):
    nf, nc, nt = sizes
    (
        self_query,
        self_key,
        self_value,
        self_out,
        cross_query,
        cross_key,
        cross_value,
        cross_out,
        feed_in,
        feed_out,
    ) = parameters[:10]
    own_fsdp = lax.axis_index("fsdp")
    own_context = lax.axis_index("context")
    own_tensor = lax.axis_index("tensor")
    frame_count, clips, features = frames.shape
    order = mask_order(nt)
    block = features // (nf * nc)
    columns = self_query.shape[1]
    halves = nc // clips
    width = columns // halves
    padded = -(-3 * width // 128) * 128
    gather = functools.partial(gather_group, fsdp_size=nf, context_size=nc)
    place = jnp.stack([own_context, own_tensor]).astype(jnp.int32)

    vectors = gather(jnp.stack(parameters[10:16] + parameters[10:12]), axis=1).astype(wide)
    pieces = []
    for part in range(halves):
        lanes = slice(part * width, (part + 1) * width)
        pieces += [self_query[:, lanes], self_key[:, lanes], self_value[:, lanes]]
        if padded > 3 * width:
            pieces.append(jnp.zeros((block, padded - 3 * width), low))
    qkv_all = gather(jnp.concatenate(pieces, axis=1))
    second_all = gather(jnp.concatenate([self_out, cross_query], axis=1))
    third_all = gather(jnp.concatenate([cross_key, cross_value, cross_out], axis=1))
    feed_in_all = gather(feed_in)
    feed_out_all = gather(feed_out)
    self_out_all, cross_query_all = second_all[:, :columns], second_all[:, columns:]
    cross_key_value = third_all[:, : 2 * columns]
    cross_out_all = third_all[:, 2 * columns :]

    relative = relative_columns(own_fsdp, own_context, nf, nc, features)
    residual = jnp.einsum("fcd,de->cfe", frames, relative, preferred_element_type=wide)
    incoming = jnp.einsum("fcd,de->cfe", cotangent, relative, preferred_element_type=wide)
    text = jnp.einsum("tcd,de->cte", text_states, relative, preferred_element_type=wide).astype(low)

    def by_row(values):
        return values.reshape(-1, values.shape[-1])

    def by_clip(values):
        return values.reshape(clips, -1, values.shape[-1])

    def to_chunks(values, lanes):
        parts = [values[..., j * lanes : (j + 1) * lanes] for j in range(halves)]
        return jnp.stack(parts, axis=1).reshape(clips * halves, values.shape[1], lanes)

    def from_chunks(chunks):
        chunks = chunks.reshape((clips, halves) + chunks.shape[1:])
        return jnp.concatenate([chunks[:, j] for j in range(halves)], axis=-1)

    normed_one = by_row(gather_rows(layer_norm(residual, vectors[0], vectors[1]), nt))
    projected = by_clip(dot(normed_one, qkv_all, 1, 0).astype(low))
    head_rows = to_heads(to_chunks(projected, padded), own_context, nc)
    head_out, head_top = self_forward(place, head_rows, width, frame_count, order)
    attended = by_row(from_chunks(to_frames(head_out, own_context, nc)))
    after_self = residual + scatter_rows(by_clip(dot(attended, self_out_all, 1, 1)), nt)

    normed_two = by_row(gather_rows(layer_norm(after_self, vectors[2], vectors[3]), nt))
    cross_queries = by_clip(dot(normed_two, cross_query_all, 1, 0).astype(low))
    text_projected = by_clip(dot(by_row(text), cross_key_value, 1, 0).astype(low))
    cross_keys, cross_values = text_projected[..., :columns], text_projected[..., columns:]
    crossed = cross_forward(cross_queries, cross_keys, cross_values)
    after_cross = after_self + scatter_rows(by_clip(dot(by_row(crossed), cross_out_all, 1, 1)), nt)

    normed_three = by_row(gather_rows(layer_norm(after_cross, vectors[4], vectors[5]), nt))
    hidden = dot(normed_three, feed_in_all, 1, 0)
    gate = 0.5 + 0.5 * lax.erf(hidden * (0.5**0.5))
    active = (hidden * gate).astype(low)
    layer_out = after_cross + scatter_rows(by_clip(dot(active, feed_out_all, 1, 1)), nt)
    layer_out = jnp.einsum("cfe,de->fcd", layer_out.astype(low), relative, preferred_element_type=wide).astype(low)

    grad_rows = by_row(gather_rows(incoming.astype(low), nt))
    grad_active = dot(grad_rows, feed_out_all, 1, 0)
    feed_out_grad = weight_grad(grad_rows, active, nf, nc)
    slope = gate + hidden * jnp.exp(-0.5 * hidden * hidden) * ((2.0 * jnp.pi) ** -0.5)
    grad_hidden = (grad_active * slope).astype(low)
    feed_in_grad = weight_grad(normed_three, grad_hidden, nf, nc)
    grad_normed = scatter_rows(by_clip(dot(grad_hidden, feed_in_all, 1, 1)), nt)
    piece, third_gain, third_shift = norm_back(after_cross, vectors[4], grad_normed)
    grad_after_cross = incoming + piece

    grad_rows = by_row(gather_rows(grad_after_cross.astype(low), nt))
    grad_crossed = by_clip(dot(grad_rows, cross_out_all, 1, 0).astype(low))
    cross_out_grad = weight_grad(grad_rows, by_row(crossed), nf, nc)
    grad_cross_queries, grad_cross_keys, grad_cross_values = cross_backward(
        cross_queries, cross_keys, cross_values, grad_crossed
    )
    grad_cross_queries = by_row(grad_cross_queries)
    cross_query_grad = weight_grad(normed_two, grad_cross_queries, nf, nc)
    grad_normed = scatter_rows(by_clip(dot(grad_cross_queries, cross_query_all, 1, 1)), nt)
    piece, second_gain, second_shift = norm_back(after_self, vectors[2], grad_normed)
    grad_after_self = grad_after_cross + piece

    text_grads = by_row(jnp.concatenate([grad_cross_keys, grad_cross_values], axis=-1))
    mask = 1
    while mask < nc:
        text_grads = text_grads + lax.ppermute(
            text_grads, "context", [(i, i ^ mask) for i in range(nc)]
        )
        mask *= 2
    text_low = text_grads.astype(low)
    near_columns = by_row(text[..., :block])
    far_blocks = [
        dot(by_row(text[..., far * nc * block : far * nc * block + block]), text_low, 0, 0).astype(low)
        for far in range(1, nf)
    ]
    key_value_grad = reduce_fsdp(dot(near_columns, text_low, 0, 0), far_blocks, nf)
    text_part = dot(text_low, cross_key_value, 1, 1)
    mask = 1
    while mask < nt:
        text_part = text_part + swap_tensor(text_part, mask, nt)
        mask *= 2
    text_grad = jnp.einsum(
        "cte,de->tcd", by_clip(text_part), relative.astype(wide), precision=lax.Precision.HIGHEST
    )

    grad_rows = by_row(gather_rows(grad_after_self.astype(low), nt))
    grad_attended = by_clip(dot(grad_rows, self_out_all, 1, 0).astype(low))
    self_out_grad = weight_grad(grad_rows, attended, nf, nc)
    head_grad = to_heads(to_chunks(grad_attended, width), own_context, nc)
    head_back = self_backward(place, head_rows, head_out, head_top, head_grad, frame_count, order)
    grad_projected = by_row(from_chunks(to_frames(head_back, own_context, nc)))
    qkv_grad = weight_grad(normed_one, grad_projected, nf, nc)
    grad_normed = scatter_rows(by_clip(dot(grad_projected, qkv_all, 1, 1)), nt)
    piece, first_gain, first_shift = norm_back(residual, vectors[0], grad_normed)
    frames_grad = jnp.einsum(
        "cfe,de->fcd",
        grad_after_self + piece,
        relative.astype(wide),
        precision=lax.Precision.HIGHEST,
    )

    norm_grads = jnp.stack(
        [first_gain, first_shift, second_gain, second_shift, third_gain, third_shift]
    )
    mask = 1
    while mask < nt:
        norm_grads = norm_grads + swap_tensor(norm_grads, mask, nt)
        mask *= 2
    half = nc * block
    total = norm_grads[:, :half]
    for step in range(1, nf):
        total = total + from_fsdp(norm_grads[:, step * half : (step + 1) * half], nf - step, nf)
    norm_result = total[:, :block]
    for step in shift_order(nc):
        norm_result = norm_result + from_context(
            total[:, step * block : (step + 1) * block], nc - step, nc
        )

    qkv_parts = []
    for kind in range(3):
        parts = [
            qkv_grad[:, part * padded + kind * width : part * padded + (kind + 1) * width]
            for part in range(halves)
        ]
        qkv_parts.append(jnp.concatenate(parts, axis=1))
    return (
        layer_out,
        frames_grad,
        text_grad,
        qkv_parts[0],
        qkv_parts[1],
        qkv_parts[2],
        self_out_grad,
        cross_query_grad,
        key_value_grad[:, :columns],
        key_value_grad[:, columns:],
        cross_out_grad,
        feed_in_grad,
        feed_out_grad,
        norm_result[0],
        norm_result[1],
        norm_result[2],
        norm_result[3],
        norm_result[4],
        norm_result[5],
    )


def solution(mesh):
    sizes = (mesh.shape["fsdp"], mesh.shape["context"], mesh.shape["tensor"])
    rows = P(("context", "tensor"), "fsdp", None)
    texts = P(None, "fsdp", None)
    matrix = P(("fsdp", "context"), "tensor")
    vector = P(("fsdp", "context"))
    return jax.shard_map(
        functools.partial(on_device, sizes),
        mesh=mesh,
        in_specs=(rows, texts, rows) + (matrix,) * 10 + (vector,) * 6,
        out_specs=(rows, rows, texts) + (matrix,) * 10 + (vector,) * 6,
        check_vma=False,
    )
```

profile of v0, /device:TPU:8, one launch (start us, length us, event | category | flops | bytes accessed | tf_op | source)
XLA Modules:
  0.0 922.2 jit_solution(17161036591774747517)
XLA Ops:
  29.0 3.5 collective-permute-start.11
  38.1 34.4 %collective-permute-done.10 = bf16[192,1280]{1,0:T(8,128)(2,1)} collective-permute-done((bf16[192,1280]{1,0:T(8,128)(2,1)S(1)}, bf16[192,1280]{1,0:T(8,128)(2,1)}, u32[]{:S(2)}, u32[]{:S(2)}) %collective-permute-start.10) | collective-permute-done | bytes 491552 | tf_op jit(solution)/shard_map/ppermute | solution.py:24
  82.2 5.0 collective-permute-done.7
  90.9 9.7 %collective-permute-done.15 = bf16[192,1280]{1,0:T(8,128)(2,1)S(1)} collective-permute-done((bf16[192,1280]{1,0:T(8,128)(2,1)}, bf16[192,1280]{1,0:T(8,128)(2,1)S(1)}, u32[]{:S(2)}, u32[]{:S(2)}) %collective-permute-start.15) | collective-permute-done | bytes 491552 | tf_op jit(solution)/shard_map/ppermute | solution.py:28
  101.5 8.0 collective-permute-done.16
  120.1 9.3 %collective-permute-done.23 = bf16[192,768]{1,0:T(8,128)(2,1)S(1)} collective-permute-done((bf16[192,768]{1,0:T(8,128)(2,1)S(1)}, bf16[192,768]{1,0:T(8,128)(2,1)S(1)}, u32[]{:S(2)}, u32[]{:S(2)}) %collective-permute-start.23) | collective-permute-done | bytes 294944 | tf_op jit(solution)/shard_map/ppermute | solution.py:24
  129.4 19.0 %collective-permute-done.24 = bf16[192,768]{1,0:T(8,128)(2,1)S(1)} collective-permute-done((bf16[192,768]{1,0:T(8,128)(2,1)S(1)}, bf16[192,768]{1,0:T(8,128)(2,1)S(1)}, u32[]{:S(2)}, u32[]{:S(2)}) %collective-permute-start.24) | collective-permute-done | bytes 294944 | tf_op jit(solution)/shard_map/ppermute | solution.py:24
  150.4 6.8 collective-permute-done.27
  158.8 14.9 %collective-permute-done.19 = bf16[384,640]{1,0:T(8,128)(2,1)S(1)} collective-permute-done((bf16[384,640]{1,0:T(8,128)(2,1)S(1)}, bf16[384,640]{1,0:T(8,128)(2,1)S(1)}, u32[]{:S(2)}, u32[]{:S(2)}) %collective-permute-start.19) | collective-permute-done | bytes 491552 | tf_op jit(solution)/shard_map/ppermute | solution.py:24
  175.1 18.0 %shard_map.330 = (bf16[4,384,192]{2,1,0:T(8,128)(2,1)S(1)}, f32[4,3,384]{2,1,0:T(4,128)S(1)}) custom-call(s32[2]{0:T(128)S(1)} %pad_add_fusion.place_ref, bf16[4,384,640]{2,1,0:T(8,128)(2,1)S(1)} %pad_maximum_fusion.7.rows_ref), custom_call_target="tpu_custom_call" | custom-call | flops 1132462080 | bytes 3932160 | tf_op jit(solution)/shard_map/pallas_call | solution.py:288
  193.2 6.6 collective-permute-start.22
  199.8 4.3 collective-permute-start.21
  204.9 20.6 %collective-permute-done.22 = bf16[384,192]{1,0:T(8,128)(2,1)S(1)} collective-permute-done((bf16[384,192]{1,0:T(8,128)(2,1)S(1)}, bf16[384,192]{1,0:T(8,128)(2,1)S(1)}, u32[]{:S(2)}, u32[]{:S(2)}) %collective-permute-start.22) | collective-permute-done | bytes 147488 | tf_op jit(solution)/shard_map/ppermute | solution.py:24
  225.5 4.2 collective-permute-done.21
  239.8 23.1 %collective-permute-done.35 = bf16[192,1152]{1,0:T(8,128)(2,1)S(1)} collective-permute-done((bf16[192,1152]{1,0:T(8,128)(2,1)S(1)}, bf16[192,1152]{1,0:T(8,128)(2,1)S(1)}, u32[]{:S(2)}, u32[]{:S(2)}) %collective-permute-start.35) | collective-permute-done | bytes 442400 | tf_op jit(solution)/shard_map/ppermute | solution.py:24
  263.5 27.5 %collective-permute-done.36 = bf16[192,1152]{1,0:T(8,128)(2,1)S(1)} collective-permute-done((bf16[192,1152]{1,0:T(8,128)(2,1)S(1)}, bf16[192,1152]{1,0:T(8,128)(2,1)S(1)}, u32[]{:S(2)}, u32[]{:S(2)}) %collective-permute-start.36) | collective-permute-done | bytes 442400 | tf_op jit(solution)/shard_map/ppermute | solution.py:24
  292.8 12.0 %collective-permute-done.31 = bf16[2,96,1536]{2,1,0:T(8,128)(2,1)S(1)} collective-permute-done((bf16[2,96,1536]{2,1,0:T(8,128)(2,1)S(1)}, bf16[2,96,1536]{2,1,0:T(8,128)(2,1)S(1)}, u32[]{:S(2)}, u32[]{:S(2)}) %collective-permute-start.31) | collective-permute-done | bytes 589856 | tf_op jit(solution)/shard_map/ppermute | solution.py:32
  307.5 7.6 collective-permute-done.39
  317.3 10.8 %collective-permute-done.41 = bf16[192,1152]{1,0:T(8,128)(2,1)S(1)} collective-permute-done((bf16[192,1152]{1,0:T(8,128)(2,1)S(1)}, bf16[192,1152]{1,0:T(8,128)(2,1)S(1)}, u32[]{:S(2)}, u32[]{:S(2)}) %collective-permute-start.41) | collective-permute-done | bytes 442400 | tf_op jit(solution)/shard_map/ppermute | solution.py:28
  345.1 15.7 %collective-permute-done.54 = bf16[192,1536]{1,0:T(8,128)(2,1)S(1)} collective-permute-done((bf16[192,1536]{1,0:T(8,128)(2,1)S(1)}, bf16[192,1536]{1,0:T(8,128)(2,1)S(1)}, u32[]{:S(2)}, u32[]{:S(2)}) %collective-permute-start.54) | collective-permute-done | bytes 589856 | tf_op jit(solution)/shard_map/ppermute | solution.py:24
  362.2 19.6 %collective-permute-done.55 = bf16[192,1536]{1,0:T(8,128)(2,1)S(1)} collective-permute-done((bf16[192,1536]{1,0:T(8,128)(2,1)S(1)}, bf16[192,1536]{1,0:T(8,128)(2,1)S(1)}, u32[]{:S(2)}, u32[]{:S(2)}) %collective-permute-start.55) | collective-permute-done | bytes 589856 | tf_op jit(solution)/shard_map/ppermute | solution.py:24
  385.3 25.3 %collective-permute-done.51 = bf16[192,1536]{1,0:T(8,128)(2,1)S(1)} collective-permute-done((bf16[192,1536]{1,0:T(8,128)(2,1)S(1)}, bf16[192,1536]{1,0:T(8,128)(2,1)S(1)}, u32[]{:S(2)}, u32[]{:S(2)}) %collective-permute-start.51) | collective-permute-done | bytes 589856 | tf_op jit(solution)/shard_map/ppermute | solution.py:28
  413.6 9.6 %collective-permute-done.52 = bf16[192,1536]{1,0:T(8,128)(2,1)S(1)} collective-permute-done((bf16[192,1536]{1,0:T(8,128)(2,1)S(1)}, bf16[192,1536]{1,0:T(8,128)(2,1)S(1)}, u32[]{:S(2)}, u32[]{:S(2)}) %collective-permute-start.52) | collective-permute-done | bytes 589856 | tf_op jit(solution)/shard_map/ppermute | solution.py:28
  424.2 24.3 %collective-permute-done.58 = bf16[192,1536]{1,0:T(8,128)(2,1)S(1)} collective-permute-done((bf16[192,1536]{1,0:T(8,128)(2,1)S(1)}, bf16[192,1536]{1,0:T(8,128)(2,1)S(1)}, u32[]{:S(2)}, u32[]{:S(2)}) %collective-permute-start.58) | collective-permute-done | bytes 589856 | tf_op jit(solution)/shard_map/ppermute | solution.py:28
  449.3 10.8 %collective-permute-done.60 = bf16[192,1536]{1,0:T(8,128)(2,1)S(1)} collective-permute-done((bf16[192,1536]{1,0:T(8,128)(2,1)S(1)}, bf16[192,1536]{1,0:T(8,128)(2,1)S(1)}, u32[]{:S(2)}, u32[]{:S(2)}) %collective-permute-start.60) | collective-permute-done | bytes 589856 | tf_op jit(solution)/shard_map/ppermute | solution.py:28
  460.5 6.0 multiply_convert_fusion
  466.5 6.7 fusion.15
  473.2 6.6 fusion.136
  481.5 5.9 fusion.135
  489.2 3.5 convolution_convert_fusion
  495.9 13.7 %collective-permute-done.67 = bf16[2,96,1536]{2,1,0:T(8,128)(2,1)S(1)} collective-permute-done((bf16[2,96,1536]{2,1,0:T(8,128)(2,1)S(1)}, bf16[2,96,1536]{2,1,0:T(8,128)(2,1)S(1)}, u32[]{:S(2)}, u32[]{:S(2)}) %collective-permute-start.67) | collective-permute-done | bytes 589856 | tf_op jit(solution)/shard_map/ppermute | solution.py:32
  511.9 3.5 convolution_convert_fusion.1
  517.2 5.0 collective-permute-done.62
  526.6 7.5 collective-permute-done.68
  534.1 12.9 %collective-permute-done.109 = bf16[768,1536]{1,0:T(8,128)(2,1)} collective-permute-done((bf16[768,1536]{1,0:T(8,128)(2,1)}, bf16[768,1536]{1,0:T(8,128)(2,1)}, u32[]{:S(2)}, u32[]{:S(2)}) %collective-permute-start.109) | collective-permute-done | bytes 2359328 | tf_op jit(solution)/shard_map/ppermute | solution.py:28
  547.1 5.9 fusion.134
  556.1 4.3 collective-permute-start.112
  562.0 4.4 shard_map.332
  568.0 29.1 %collective-permute-done.105 = bf16[768,1536]{1,0:T(8,128)(2,1)} collective-permute-done((bf16[768,1536]{1,0:T(8,128)(2,1)}, bf16[768,1536]{1,0:T(8,128)(2,1)}, u32[]{:S(2)}, u32[]{:S(2)}) %collective-permute-start.105) | collective-permute-done | bytes 2359328 | tf_op jit(solution)/shard_map/ppermute | solution.py:28
  597.2 3.8 fusion.133
  607.3 4.3 collective-permute-start.108
  611.6 24.7 %collective-permute-done.111 = bf16[192,1536]{1,0:T(8,128)(2,1)} collective-permute-done((bf16[192,1536]{1,0:T(8,128)(2,1)S(1)}, bf16[192,1536]{1,0:T(8,128)(2,1)}, u32[]{:S(2)}, u32[]{:S(2)}) %collective-permute-start.111) | collective-permute-done | bytes 589856 | tf_op jit(solution)/shard_map/ppermute | solution.py:24
  640.8 4.9 collective-permute-done.106
  646.0 10.5 %collective-permute-done.108 = bf16[192,1536]{1,0:T(8,128)(2,1)S(1)} collective-permute-done((bf16[192,1536]{1,0:T(8,128)(2,1)S(1)}, bf16[192,1536]{1,0:T(8,128)(2,1)S(1)}, u32[]{:S(2)}, u32[]{:S(2)}) %collective-permute-start.108) | collective-permute-done | bytes 589856 | tf_op jit(solution)/shard_map/ppermute | solution.py:24
  664.0 6.0 collective-permute-done.73
  670.2 3.4 collective-permute-start.99
  675.5 6.4 collective-permute-done.85
  684.0 6.0 collective-permute-start.78
  692.5 8.4 collective-permute-done.78
  702.4 5.7 collective-permute-done.76
  708.2 24.5 %shard_map.333 = bf16[4,384,640]{2,1,0:T(8,128)(2,1)S(1)} custom-call(s32[2]{0:T(128)S(1)} %pad_add_fusion.place_ref, bf16[4,384,640]{2,1,0:T(8,128)(2,1)S(1)} %pad_maximum_fusion.7.rows_ref, bf16[4,384,192]{2,1,0:T(8,128)(2,1)S(1)} %get-tuple-element.24.out_ref, f32[4,3,384]{2,1,0:T(4,128)S(1)} %get-tuple-element.26.top_ref, ...), custom_call_target="tpu_custom_call" | custom-call | flops 2831155200 | bytes 7864320 | tf_op jit(solution)/shard_map/pallas_call | solution.py:309
  738.7 4.7 collective-permute-start.104
  743.5 24.7 %collective-permute-done.81 = bf16[384,640]{1,0:T(8,128)(2,1)S(1)} collective-permute-done((bf16[384,640]{1,0:T(8,128)(2,1)S(1)}, bf16[384,640]{1,0:T(8,128)(2,1)S(1)}, u32[]{:S(2)}, u32[]{:S(2)}) %collective-permute-start.81) | collective-permute-done | bytes 491552 | tf_op jit(solution)/shard_map/ppermute | solution.py:24
  768.3 16.7 %collective-permute-done.80 = bf16[384,640]{1,0:T(8,128)(2,1)S(1)} collective-permute-done((bf16[384,640]{1,0:T(8,128)(2,1)S(1)}, bf16[384,640]{1,0:T(8,128)(2,1)S(1)}, u32[]{:S(2)}, u32[]{:S(2)}) %collective-permute-start.80) | collective-permute-done | bytes 491552 | tf_op jit(solution)/shard_map/ppermute | solution.py:24
  797.4 6.8 collective-permute-done.87
  804.4 4.7 convolution_bitcast_fusion.3
  818.2 9.6 %collective-permute-done.92 = bf16[768,384]{1,0:T(8,128)(2,1)S(1)} collective-permute-done((bf16[768,384]{1,0:T(8,128)(2,1)S(1)}, bf16[768,384]{1,0:T(8,128)(2,1)S(1)}, u32[]{:S(2)}, u32[]{:S(2)}) %collective-permute-start.92) | collective-permute-done | bytes 589856 | tf_op jit(solution)/shard_map/ppermute | solution.py:28
  835.9 3.5 collective-permute-done.95
  848.0 20.2 %collective-permute-done.115 = f32[6,768]{1,0:T(8,128)S(1)} collective-permute-done((f32[6,768]{1,0:T(8,128)S(1)}, f32[6,768]{1,0:T(8,128)S(1)}, u32[]{:S(2)}, u32[]{:S(2)}) %collective-permute-start.115) | collective-permute-done | bytes 18464 | tf_op jit(solution)/shard_map/ppermute | solution.py:28
  870.3 4.4 fusion.129
  876.4 3.3 collective-permute-start.91
  879.9 5.2 convolution_bitcast_fusion.2
  887.6 21.4 %collective-permute-done.89 = bf16[192,1280]{1,0:T(8,128)(2,1)S(1)} collective-permute-done((bf16[192,1280]{1,0:T(8,128)(2,1)S(1)}, bf16[192,1280]{1,0:T(8,128)(2,1)S(1)}, u32[]{:S(2)}, u32[]{:S(2)}) %collective-permute-start.89) | collective-permute-done | bytes 491552 | tf_op jit(solution)/shard_map/ppermute | solution.py:24
  909.0 6.9 collective-permute-done.91
  (506 shorter events, 212.8 us)
Async XLA Ops:
  13.6 67.0 %collective-permute-start.13 = (bf16[192,1280]{1,0:T(8,128)(2,1)S(1)}, bf16[192,1280]{1,0:T(8,128)(2,1)S(1)}, u32[]{:S(2)}, u32[]{:S(2)}) collective-permute-start(bf16[192,1280]{1,0:T(8,128)(2,1)S(1)} %concatenate.89), channel_id=1, source_target_pairs={{16,0},{0,16},{17,1},{1,17},{18,2},{2,18},{19,3},{3,19},{20,4},{4,... | collective-permute-start | bytes 1474568 | tf_op jit(solution)/shard_map/ppermute | solution.py:28
  28.8 49.7 %collective-permute-start.12 = (bf16[192,1280]{1,0:T(8,128)(2,1)S(1)}, bf16[192,1280]{1,0:T(8,128)(2,1)S(1)}, u32[]{:S(2)}, u32[]{:S(2)}) collective-permute-start(bf16[192,1280]{1,0:T(8,128)(2,1)S(1)} %concatenate.89), channel_id=1, source_target_pairs={{12,0},{0,4},{4,8},{8,12},{13,1},{1,5},{5,9},{9,13},{14,2},{2,6},{... | collective-permute-start | bytes 1474568 | tf_op jit(solution)/shard_map/ppermute | solution.py:24
  29.0 46.8 %collective-permute-start.11 = (bf16[192,1280]{1,0:T(8,128)(2,1)S(1)}, bf16[192,1280]{1,0:T(8,128)(2,1)}, u32[]{:S(2)}, u32[]{:S(2)}) collective-permute-start(bf16[192,1280]{1,0:T(8,128)(2,1)S(1)} %concatenate.89), channel_id=1, source_target_pairs={{8,0},{12,4},{0,8},{4,12},{9,1},{13,5},{1,9},{5,13},{10,2},{14,6},... | collective-permute-start | bytes 1474568 | tf_op jit(solution)/shard_map/ppermute | solution.py:24
  32.5 39.9 %collective-permute-start.10 = (bf16[192,1280]{1,0:T(8,128)(2,1)S(1)}, bf16[192,1280]{1,0:T(8,128)(2,1)}, u32[]{:S(2)}, u32[]{:S(2)}) collective-permute-start(bf16[192,1280]{1,0:T(8,128)(2,1)S(1)} %concatenate.89), channel_id=1, source_target_pairs={{4,0},{8,4},{12,8},{0,12},{5,1},{9,5},{13,9},{1,13},{6,2},{10,6},{... | collective-permute-start | bytes 1474568 | tf_op jit(solution)/shard_map/ppermute | solution.py:24
  33.7 116.4 %collective-permute-start.26 = (bf16[192,768]{1,0:T(8,128)(2,1)}, bf16[192,768]{1,0:T(8,128)(2,1)S(1)}, u32[]{:S(2)}, u32[]{:S(2)}) collective-permute-start(bf16[192,768]{1,0:T(8,128)(2,1)} %copy-done.32), channel_id=1, source_target_pairs={{16,0},{0,16},{17,1},{1,17},{18,2},{2,18},{19,3},{3,19},{20,4},{4,... | collective-permute-start | bytes 884744 | tf_op jit(solution)/shard_map/ppermute | solution.py:28
  80.5 28.9 %collective-permute-start.16 = (bf16[192,1280]{1,0:T(8,128)(2,1)S(1)}, bf16[192,1280]{1,0:T(8,128)(2,1)S(1)}, u32[]{:S(2)}, u32[]{:S(2)}) collective-permute-start(bf16[192,1280]{1,0:T(8,128)(2,1)S(1)} %collective-permute-done.12), channel_id=1, source_target_pairs={{16,0},{0,16},{17,1},{1,17},{18,2},{2,18},{19,3},{3,19},{20,4},{4,... | collective-permute-start | bytes 1474568 | tf_op jit(solution)/shard_map/ppermute | solution.py:28
  109.5 39.0 %collective-permute-start.24 = (bf16[192,768]{1,0:T(8,128)(2,1)S(1)}, bf16[192,768]{1,0:T(8,128)(2,1)S(1)}, u32[]{:S(2)}, u32[]{:S(2)}) collective-permute-start(bf16[192,768]{1,0:T(8,128)(2,1)S(1)} %copy-done.33), channel_id=1, source_target_pairs={{8,0},{12,4},{0,8},{4,12},{9,1},{13,5},{1,9},{5,13},{10,2},{14,6},... | collective-permute-start | bytes 884744 | tf_op jit(solution)/shard_map/ppermute | solution.py:24
  116.4 57.2 %collective-permute-start.19 = (bf16[384,640]{1,0:T(8,128)(2,1)S(1)}, bf16[384,640]{1,0:T(8,128)(2,1)S(1)}, u32[]{:S(2)}, u32[]{:S(2)}) collective-permute-start(bf16[384,640]{1,0:T(8,128)(2,1)S(1)} %get-tuple-element.96), channel_id=1, source_target_pairs={{4,0},{8,4},{12,8},{0,12},{5,1},{9,5},{13,9},{1,13},{6,2},{10,6},{... | collective-permute-start | bytes 1474568 | tf_op jit(solution)/shard_map/ppermute | solution.py:24
  118.7 56.1 %collective-permute-start.18 = (bf16[384,640]{1,0:T(8,128)(2,1)S(1)}, bf16[384,640]{1,0:T(8,128)(2,1)S(1)}, u32[]{:S(2)}, u32[]{:S(2)}) collective-permute-start(bf16[384,640]{1,0:T(8,128)(2,1)S(1)} %get-tuple-element.97), channel_id=1, source_target_pairs={{8,0},{12,4},{0,8},{4,12},{9,1},{13,5},{1,9},{5,13},{10,2},{14,6},... | collective-permute-start | bytes 1474568 | tf_op jit(solution)/shard_map/ppermute | solution.py:24
  129.4 45.5 %collective-permute-start.17 = (bf16[384,640]{1,0:T(8,128)(2,1)S(1)}, bf16[384,640]{1,0:T(8,128)(2,1)S(1)}, u32[]{:S(2)}, u32[]{:S(2)}) collective-permute-start(bf16[384,640]{1,0:T(8,128)(2,1)S(1)} %get-tuple-element.98), channel_id=1, source_target_pairs={{12,0},{0,4},{4,8},{8,12},{13,1},{1,5},{5,9},{9,13},{14,2},{2,6},{... | collective-permute-start | bytes 1474568 | tf_op jit(solution)/shard_map/ppermute | solution.py:24
  150.1 190.0 %collective-permute-start.49 = (bf16[192,1536]{1,0:T(8,128)(2,1)S(1)}, bf16[192,1536]{1,0:T(8,128)(2,1)S(1)}, u32[]{:S(2)}, u32[]{:S(2)}) collective-permute-start(bf16[192,1536]{1,0:T(8,128)(2,1)S(1)} %copy-done.18), channel_id=1, source_target_pairs={{12,0},{0,4},{4,8},{8,12},{13,1},{1,5},{5,9},{9,13},{14,2},{2,6},{... | collective-permute-start | bytes 1769480 | tf_op jit(solution)/shard_map/ppermute | solution.py:24
  157.2 47.0 %collective-permute-start.29 = (bf16[192,768]{1,0:T(8,128)(2,1)S(1)}, bf16[192,768]{1,0:T(8,128)(2,1)S(1)}, u32[]{:S(2)}, u32[]{:S(2)}) collective-permute-start(bf16[192,768]{1,0:T(8,128)(2,1)S(1)} %collective-permute-done.25), channel_id=1, source_target_pairs={{16,0},{0,16},{17,1},{1,17},{18,2},{2,18},{19,3},{3,19},{20,4},{4,... | collective-permute-start | bytes 884744 | tf_op jit(solution)/shard_map/ppermute | solution.py:28
  173.6 30.5 %collective-permute-start.28 = (bf16[192,768]{1,0:T(8,128)(2,1)S(1)}, bf16[192,768]{1,0:T(8,128)(2,1)S(1)}, u32[]{:S(2)}, u32[]{:S(2)}) collective-permute-start(bf16[192,768]{1,0:T(8,128)(2,1)S(1)} %collective-permute-done.24), channel_id=1, source_target_pairs={{16,0},{0,16},{17,1},{1,17},{18,2},{2,18},{19,3},{3,19},{20,4},{4,... | collective-permute-start | bytes 884744 | tf_op jit(solution)/shard_map/ppermute | solution.py:28
  193.2 32.3 %collective-permute-start.22 = (bf16[384,192]{1,0:T(8,128)(2,1)S(1)}, bf16[384,192]{1,0:T(8,128)(2,1)S(1)}, u32[]{:S(2)}, u32[]{:S(2)}) collective-permute-start(bf16[384,192]{1,0:T(8,128)(2,1)S(1)} %get-tuple-element.120), channel_id=1, source_target_pairs={{12,0},{0,4},{4,8},{8,12},{13,1},{1,5},{5,9},{9,13},{14,2},{2,6},{... | collective-permute-start | bytes 442376 | tf_op jit(solution)/shard_map/ppermute | solution.py:24
  199.8 29.9 %collective-permute-start.21 = (bf16[384,192]{1,0:T(8,128)(2,1)S(1)}, bf16[384,192]{1,0:T(8,128)(2,1)S(1)}, u32[]{:S(2)}, u32[]{:S(2)}) collective-permute-start(bf16[384,192]{1,0:T(8,128)(2,1)S(1)} %get-tuple-element.121), channel_id=1, source_target_pairs={{8,0},{12,4},{0,8},{4,12},{9,1},{13,5},{1,9},{5,13},{10,2},{14,6},... | collective-permute-start | bytes 442376 | tf_op jit(solution)/shard_map/ppermute | solution.py:24
  204.1 28.0 %collective-permute-start.20 = (bf16[384,192]{1,0:T(8,128)(2,1)S(1)}, bf16[384,192]{1,0:T(8,128)(2,1)S(1)}, u32[]{:S(2)}, u32[]{:S(2)}) collective-permute-start(bf16[384,192]{1,0:T(8,128)(2,1)S(1)} %get-tuple-element.122), channel_id=1, source_target_pairs={{4,0},{8,4},{12,8},{0,12},{5,1},{9,5},{13,9},{1,13},{6,2},{10,6},{... | collective-permute-start | bytes 442376 | tf_op jit(solution)/shard_map/ppermute | solution.py:24
  204.2 134.9 %collective-permute-start.48 = (bf16[192,1536]{1,0:T(8,128)(2,1)S(1)}, bf16[192,1536]{1,0:T(8,128)(2,1)S(1)}, u32[]{:S(2)}, u32[]{:S(2)}) collective-permute-start(bf16[192,1536]{1,0:T(8,128)(2,1)S(1)} %copy-done.18), channel_id=1, source_target_pairs={{8,0},{12,4},{0,8},{4,12},{9,1},{13,5},{1,9},{5,13},{10,2},{14,6},... | collective-permute-start | bytes 1769480 | tf_op jit(solution)/shard_map/ppermute | solution.py:24
  225.5 66.2 %collective-permute-start.38 = (bf16[192,1152]{1,0:T(8,128)(2,1)S(1)}, bf16[192,1152]{1,0:T(8,128)(2,1)S(1)}, u32[]{:S(2)}, u32[]{:S(2)}) collective-permute-start(bf16[192,1152]{1,0:T(8,128)(2,1)S(1)} %copy-done.39), channel_id=1, source_target_pairs={{16,0},{0,16},{17,1},{1,17},{18,2},{2,18},{19,3},{3,19},{20,4},{4,... | collective-permute-start | bytes 1327112 | tf_op jit(solution)/shard_map/ppermute | solution.py:28
  229.7 33.2 %collective-permute-start.35 = (bf16[192,1152]{1,0:T(8,128)(2,1)S(1)}, bf16[192,1152]{1,0:T(8,128)(2,1)S(1)}, u32[]{:S(2)}, u32[]{:S(2)}) collective-permute-start(bf16[192,1152]{1,0:T(8,128)(2,1)S(1)} %copy-done.39), channel_id=1, source_target_pairs={{4,0},{8,4},{12,8},{0,12},{5,1},{9,5},{13,9},{1,13},{6,2},{10,6},{... | collective-permute-start | bytes 1327112 | tf_op jit(solution)/shard_map/ppermute | solution.py:24
  235.3 27.7 %collective-permute-start.30 = (bf16[2,192,1536]{2,1,0:T(8,128)(2,1)S(1)}, bf16[2,192,1536]{2,1,0:T(8,128)(2,1)S(1)}, u32[]{:S(2)}, u32[]{:S(2)}) collective-permute-start(bf16[2,192,1536]{2,1,0:T(8,128)(2,1)S(1)} %slice.776), channel_id=1, source_target_pairs={{0,1},{1,0},{2,3},{3,2},{4,5},{5,4},{6,7},{7,6},{8,9},{9,8},{10,11... | collective-permute-start | bytes 3538952 | tf_op jit(solution)/shard_map/ppermute | solution.py:32
  262.9 28.6 %collective-permute-start.37 = (bf16[192,1152]{1,0:T(8,128)(2,1)S(1)}, bf16[192,1152]{1,0:T(8,128)(2,1)S(1)}, u32[]{:S(2)}, u32[]{:S(2)}) collective-permute-start(bf16[192,1152]{1,0:T(8,128)(2,1)S(1)} %copy-done.39), channel_id=1, source_target_pairs={{12,0},{0,4},{4,8},{8,12},{13,1},{1,5},{5,9},{9,13},{14,2},{2,6},{... | collective-permute-start | bytes 1327112 | tf_op jit(solution)/shard_map/ppermute | solution.py:24
  263.0 28.0 %collective-permute-start.36 = (bf16[192,1152]{1,0:T(8,128)(2,1)S(1)}, bf16[192,1152]{1,0:T(8,128)(2,1)S(1)}, u32[]{:S(2)}, u32[]{:S(2)}) collective-permute-start(bf16[192,1152]{1,0:T(8,128)(2,1)S(1)} %copy-done.39), channel_id=1, source_target_pairs={{8,0},{12,4},{0,8},{4,12},{9,1},{13,5},{1,9},{5,13},{10,2},{14,6},... | collective-permute-start | bytes 1327112 | tf_op jit(solution)/shard_map/ppermute | solution.py:24
  315.2 29.0 %collective-permute-start.50 = (bf16[192,1536]{1,0:T(8,128)(2,1)S(1)}, bf16[192,1536]{1,0:T(8,128)(2,1)S(1)}, u32[]{:S(2)}, u32[]{:S(2)}) collective-permute-start(bf16[192,1536]{1,0:T(8,128)(2,1)S(1)} %copy-done.18), channel_id=1, source_target_pairs={{16,0},{0,16},{17,1},{1,17},{18,2},{2,18},{19,3},{3,19},{20,4},{4,... | collective-permute-start | bytes 1769480 | tf_op jit(solution)/shard_map/ppermute | solution.py:28
  330.2 54.2 %collective-permute-start.56 = (bf16[192,1536]{1,0:T(8,128)(2,1)S(1)}, bf16[192,1536]{1,0:T(8,128)(2,1)S(1)}, u32[]{:S(2)}, u32[]{:S(2)}) collective-permute-start(bf16[192,1536]{1,0:T(8,128)(2,1)S(1)} %copy-done.19), channel_id=1, source_target_pairs={{12,0},{0,4},{4,8},{8,12},{13,1},{1,5},{5,9},{9,13},{14,2},{2,6},{... | collective-permute-start | bytes 1769480 | tf_op jit(solution)/shard_map/ppermute | solution.py:24
  331.0 29.7 %collective-permute-start.54 = (bf16[192,1536]{1,0:T(8,128)(2,1)S(1)}, bf16[192,1536]{1,0:T(8,128)(2,1)S(1)}, u32[]{:S(2)}, u32[]{:S(2)}) collective-permute-start(bf16[192,1536]{1,0:T(8,128)(2,1)S(1)} %copy-done.19), channel_id=1, source_target_pairs={{4,0},{8,4},{12,8},{0,12},{5,1},{9,5},{13,9},{1,13},{6,2},{10,6},{... | collective-permute-start | bytes 1769480 | tf_op jit(solution)/shard_map/ppermute | solution.py:24
  339.1 42.7 %collective-permute-start.42 = (bf16[2,192,1536]{2,1,0:T(8,128)(2,1)S(1)}, bf16[2,192,1536]{2,1,0:T(8,128)(2,1)S(1)}, u32[]{:S(2)}, u32[]{:S(2)}) collective-permute-start(bf16[2,192,1536]{2,1,0:T(8,128)(2,1)S(1)} %slice.775), channel_id=1, source_target_pairs={{0,1},{1,0},{2,3},{3,2},{4,5},{5,4},{6,7},{7,6},{8,9},{9,8},{10,11... | collective-permute-start | bytes 3538952 | tf_op jit(solution)/shard_map/ppermute | solution.py:32
  340.0 41.7 %collective-permute-start.55 = (bf16[192,1536]{1,0:T(8,128)(2,1)S(1)}, bf16[192,1536]{1,0:T(8,128)(2,1)S(1)}, u32[]{:S(2)}, u32[]{:S(2)}) collective-permute-start(bf16[192,1536]{1,0:T(8,128)(2,1)S(1)} %copy-done.19), channel_id=1, source_target_pairs={{8,0},{12,4},{0,8},{4,12},{9,1},{13,5},{1,9},{5,13},{10,2},{14,6},... | collective-permute-start | bytes 1769480 | tf_op jit(solution)/shard_map/ppermute | solution.py:24
  344.2 40.9 %collective-permute-start.57 = (bf16[192,1536]{1,0:T(8,128)(2,1)S(1)}, bf16[192,1536]{1,0:T(8,128)(2,1)S(1)}, u32[]{:S(2)}, u32[]{:S(2)}) collective-permute-start(bf16[192,1536]{1,0:T(8,128)(2,1)S(1)} %copy-done.19), channel_id=1, source_target_pairs={{16,0},{0,16},{17,1},{1,17},{18,2},{2,18},{19,3},{3,19},{20,4},{4,... | collective-permute-start | bytes 1769480 | tf_op jit(solution)/shard_map/ppermute | solution.py:28
  360.7 63.4 %collective-permute-start.63 = (bf16[2,96,1536]{2,1,0:T(8,128)(2,1)S(1)}, bf16[2,96,1536]{2,1,0:T(8,128)(2,1)S(1)}, u32[]{:S(2)}, u32[]{:S(2)}) collective-permute-start(bf16[2,96,1536]{2,1,0:T(8,128)(2,1)S(1)} %get-tuple-element.169), channel_id=1, source_target_pairs={{0,2},{1,3},{2,0},{3,1},{4,6},{5,7},{6,4},{7,5},{8,10},{9,11},{10,... | collective-permute-start | bytes 1769480 | tf_op jit(solution)/shard_map/ppermute | solution.py:32
  381.8 42.2 %collective-permute-start.53 = (bf16[192,1536]{1,0:T(8,128)(2,1)S(1)}, bf16[192,1536]{1,0:T(8,128)(2,1)S(1)}, u32[]{:S(2)}, u32[]{:S(2)}) collective-permute-start(bf16[192,1536]{1,0:T(8,128)(2,1)S(1)} %collective-permute-done.49), channel_id=1, source_target_pairs={{16,0},{0,16},{17,1},{1,17},{18,2},{2,18},{19,3},{3,19},{20,4},{4,... | collective-permute-start | bytes 1769480 | tf_op jit(solution)/shard_map/ppermute | solution.py:28
  381.9 28.8 %collective-permute-start.51 = (bf16[192,1536]{1,0:T(8,128)(2,1)S(1)}, bf16[192,1536]{1,0:T(8,128)(2,1)S(1)}, u32[]{:S(2)}, u32[]{:S(2)}) collective-permute-start(bf16[192,1536]{1,0:T(8,128)(2,1)S(1)} %collective-permute-done.47), channel_id=1, source_target_pairs={{16,0},{0,16},{17,1},{1,17},{18,2},{2,18},{19,3},{3,19},{20,4},{4,... | collective-permute-start | bytes 1769480 | tf_op jit(solution)/shard_map/ppermute | solution.py:28
  384.3 26.4 %collective-permute-start.43 = (bf16[2,96,1536]{2,1,0:T(8,128)(2,1)S(1)}, bf16[2,96,1536]{2,1,0:T(8,128)(2,1)S(1)}, u32[]{:S(2)}, u32[]{:S(2)}) collective-permute-start(bf16[2,96,1536]{2,1,0:T(8,128)(2,1)S(1)} %slice.781), channel_id=1, source_target_pairs={{0,2},{1,3},{2,0},{3,1},{4,6},{5,7},{6,4},{7,5},{8,10},{9,11},{10,... | collective-permute-start | bytes 1769480 | tf_op jit(solution)/shard_map/ppermute | solution.py:32
  385.2 38.1 %collective-permute-start.52 = (bf16[192,1536]{1,0:T(8,128)(2,1)S(1)}, bf16[192,1536]{1,0:T(8,128)(2,1)S(1)}, u32[]{:S(2)}, u32[]{:S(2)}) collective-permute-start(bf16[192,1536]{1,0:T(8,128)(2,1)S(1)} %collective-permute-done.48), channel_id=1, source_target_pairs={{16,0},{0,16},{17,1},{1,17},{18,2},{2,18},{19,3},{3,19},{20,4},{4,... | collective-permute-start | bytes 1769480 | tf_op jit(solution)/shard_map/ppermute | solution.py:28
  410.6 38.0 %collective-permute-start.59 = (bf16[192,1536]{1,0:T(8,128)(2,1)S(1)}, bf16[192,1536]{1,0:T(8,128)(2,1)S(1)}, u32[]{:S(2)}, u32[]{:S(2)}) collective-permute-start(bf16[192,1536]{1,0:T(8,128)(2,1)S(1)} %collective-permute-done.55), channel_id=1, source_target_pairs={{16,0},{0,16},{17,1},{1,17},{18,2},{2,18},{19,3},{3,19},{20,4},{4,... | collective-permute-start | bytes 1769480 | tf_op jit(solution)/shard_map/ppermute | solution.py:28
  410.7 37.8 %collective-permute-start.58 = (bf16[192,1536]{1,0:T(8,128)(2,1)S(1)}, bf16[192,1536]{1,0:T(8,128)(2,1)S(1)}, u32[]{:S(2)}, u32[]{:S(2)}) collective-permute-start(bf16[192,1536]{1,0:T(8,128)(2,1)S(1)} %collective-permute-done.54), channel_id=1, source_target_pairs={{16,0},{0,16},{17,1},{1,17},{18,2},{2,18},{19,3},{3,19},{20,4},{4,... | collective-permute-start | bytes 1769480 | tf_op jit(solution)/shard_map/ppermute | solution.py:28
  423.3 25.9 %collective-permute-start.44 = (bf16[2,96,1536]{2,1,0:T(8,128)(2,1)S(1)}, bf16[2,96,1536]{2,1,0:T(8,128)(2,1)S(1)}, u32[]{:S(2)}, u32[]{:S(2)}) collective-permute-start(bf16[2,96,1536]{2,1,0:T(8,128)(2,1)S(1)} %add_convert_fusion), channel_id=1, source_target_pairs={{0,2},{1,3},{2,0},{3,1},{4,6},{5,7},{6,4},{7,5},{8,10},{9,11},{10,... | collective-permute-start | bytes 1769480 | tf_op jit(solution)/shard_map/ppermute | solution.py:32
  424.0 36.1 %collective-permute-start.60 = (bf16[192,1536]{1,0:T(8,128)(2,1)S(1)}, bf16[192,1536]{1,0:T(8,128)(2,1)S(1)}, u32[]{:S(2)}, u32[]{:S(2)}) collective-permute-start(bf16[192,1536]{1,0:T(8,128)(2,1)S(1)} %collective-permute-done.56), channel_id=1, source_target_pairs={{16,0},{0,16},{17,1},{1,17},{18,2},{2,18},{19,3},{3,19},{20,4},{4,... | collective-permute-start | bytes 1769480 | tf_op jit(solution)/shard_map/ppermute | solution.py:28
  424.2 36.0 %collective-permute-start.64 = (bf16[2,96,1536]{2,1,0:T(8,128)(2,1)S(1)}, bf16[2,96,1536]{2,1,0:T(8,128)(2,1)S(1)}, u32[]{:S(2)}, u32[]{:S(2)}) collective-permute-start(bf16[2,96,1536]{2,1,0:T(8,128)(2,1)S(1)} %get-tuple-element.169), channel_id=1, source_target_pairs={{0,1},{1,0},{2,3},{3,2},{4,5},{5,4},{6,7},{7,6},{8,9},{9,8},{10,11... | collective-permute-start | bytes 1769480 | tf_op jit(solution)/shard_map/ppermute | solution.py:32
  492.6 54.4 %collective-permute-start.109 = (bf16[768,1536]{1,0:T(8,128)(2,1)}, bf16[768,1536]{1,0:T(8,128)(2,1)}, u32[]{:S(2)}, u32[]{:S(2)}) collective-permute-start(bf16[768,1536]{1,0:T(8,128)(2,1)} %convolution_convert_fusion), channel_id=1, source_target_pairs={{16,0},{0,16},{17,1},{1,17},{18,2},{2,18},{19,3},{3,19},{20,4},{4,... | collective-permute-start | bytes 7077896 | tf_op jit(solution)/shard_map/ppermute | solution.py:28
  494.2 28.0 %collective-permute-start.62 = (bf16[2,96,1536]{2,1,0:T(8,128)(2,1)S(1)}, bf16[2,96,1536]{2,1,0:T(8,128)(2,1)S(1)}, u32[]{:S(2)}, u32[]{:S(2)}) collective-permute-start(bf16[2,96,1536]{2,1,0:T(8,128)(2,1)S(1)} %slice.780), channel_id=1, source_target_pairs={{0,2},{1,3},{2,0},{3,1},{4,6},{5,7},{6,4},{7,5},{8,10},{9,11},{10,... | collective-permute-start | bytes 1769480 | tf_op jit(solution)/shard_map/ppermute | solution.py:32
  515.5 81.7 %collective-permute-start.105 = (bf16[768,1536]{1,0:T(8,128)(2,1)}, bf16[768,1536]{1,0:T(8,128)(2,1)}, u32[]{:S(2)}, u32[]{:S(2)}) collective-permute-start(bf16[768,1536]{1,0:T(8,128)(2,1)} %convolution_convert_fusion.1), channel_id=1, source_target_pairs={{16,0},{0,16},{17,1},{1,17},{18,2},{2,18},{19,3},{3,19},{20,4},{4,... | collective-permute-start | bytes 7077896 | tf_op jit(solution)/shard_map/ppermute | solution.py:28
  517.2 43.2 %collective-permute-start.69 = (bf16[2,96,1536]{2,1,0:T(8,128)(2,1)S(1)}, bf16[2,96,1536]{2,1,0:T(8,128)(2,1)S(1)}, u32[]{:S(2)}, u32[]{:S(2)}) collective-permute-start(bf16[2,96,1536]{2,1,0:T(8,128)(2,1)S(1)} %get-tuple-element.68), channel_id=1, source_target_pairs={{0,1},{1,0},{2,3},{3,2},{4,5},{5,4},{6,7},{7,6},{8,9},{9,8},{10,11... | collective-permute-start | bytes 1769480 | tf_op jit(solution)/shard_map/ppermute | solution.py:32
  534.1 26.3 %collective-permute-start.70 = (bf16[2,96,1536]{2,1,0:T(8,128)(2,1)S(1)}, bf16[2,96,1536]{2,1,0:T(8,128)(2,1)S(1)}, u32[]{:S(2)}, u32[]{:S(2)}) collective-permute-start(bf16[2,96,1536]{2,1,0:T(8,128)(2,1)S(1)} %collective-permute-done.68), channel_id=1, source_target_pairs={{0,1},{1,0},{2,3},{3,2},{4,5},{5,4},{6,7},{7,6},{8,9},{9,8},{10,11... | collective-permute-start | bytes 1769480 | tf_op jit(solution)/shard_map/ppermute | solution.py:32
  553.1 54.2 %collective-permute-start.110 = (bf16[192,1536]{1,0:T(8,128)(2,1)S(1)}, bf16[192,1536]{1,0:T(8,128)(2,1)}, u32[]{:S(2)}, u32[]{:S(2)}) collective-permute-start(bf16[192,1536]{1,0:T(8,128)(2,1)S(1)} %get-tuple-element.74), channel_id=1, source_target_pairs={{12,0},{0,4},{4,8},{8,12},{13,1},{1,5},{5,9},{9,13},{14,2},{2,6},{... | collective-permute-start | bytes 1769480 | tf_op jit(solution)/shard_map/ppermute | solution.py:24
  556.1 55.5 %collective-permute-start.112 = (bf16[192,1536]{1,0:T(8,128)(2,1)S(1)}, bf16[192,1536]{1,0:T(8,128)(2,1)}, u32[]{:S(2)}, u32[]{:S(2)}) collective-permute-start(bf16[192,1536]{1,0:T(8,128)(2,1)S(1)} %get-tuple-element.75), channel_id=1, source_target_pairs={{8,0},{12,4},{0,8},{4,12},{9,1},{13,5},{1,9},{5,13},{10,2},{14,6},... | collective-permute-start | bytes 1769480 | tf_op jit(solution)/shard_map/ppermute | solution.py:24
  560.4 75.8 %collective-permute-start.111 = (bf16[192,1536]{1,0:T(8,128)(2,1)S(1)}, bf16[192,1536]{1,0:T(8,128)(2,1)}, u32[]{:S(2)}, u32[]{:S(2)}) collective-permute-start(bf16[192,1536]{1,0:T(8,128)(2,1)S(1)} %get-tuple-element.76), channel_id=1, source_target_pairs={{4,0},{8,4},{12,8},{0,12},{5,1},{9,5},{13,9},{1,13},{6,2},{10,6},{... | collective-permute-start | bytes 1769480 | tf_op jit(solution)/shard_map/ppermute | solution.py:24
  568.0 37.7 %collective-permute-start.71 = (bf16[2,192,1536]{2,1,0:T(8,128)(2,1)S(1)}, bf16[2,192,1536]{2,1,0:T(8,128)(2,1)S(1)}, u32[]{:S(2)}, u32[]{:S(2)}) collective-permute-start(bf16[2,192,1536]{2,1,0:T(8,128)(2,1)S(1)} %slice.772), channel_id=1, source_target_pairs={{0,1},{1,0},{2,3},{3,2},{4,5},{5,4},{6,7},{7,6},{8,9},{9,8},{10,11... | collective-permute-start | bytes 3538952 | tf_op jit(solution)/shard_map/ppermute | solution.py:32
  601.1 44.7 %collective-permute-start.106 = (bf16[192,1536]{1,0:T(8,128)(2,1)S(1)}, bf16[192,1536]{1,0:T(8,128)(2,1)S(1)}, u32[]{:S(2)}, u32[]{:S(2)}) collective-permute-start(bf16[192,1536]{1,0:T(8,128)(2,1)S(1)} %get-tuple-element.77), channel_id=1, source_target_pairs={{12,0},{0,4},{4,8},{8,12},{13,1},{1,5},{5,9},{9,13},{14,2},{2,6},{... | collective-permute-start | bytes 1769480 | tf_op jit(solution)/shard_map/ppermute | solution.py:24
  606.1 33.2 %collective-permute-start.72 = (bf16[2,96,1536]{2,1,0:T(8,128)(2,1)S(1)}, bf16[2,96,1536]{2,1,0:T(8,128)(2,1)S(1)}, u32[]{:S(2)}, u32[]{:S(2)}) collective-permute-start(bf16[2,96,1536]{2,1,0:T(8,128)(2,1)S(1)} %slice.778), channel_id=1, source_target_pairs={{0,2},{1,3},{2,0},{3,1},{4,6},{5,7},{6,4},{7,5},{8,10},{9,11},{10,... | collective-permute-start | bytes 1769480 | tf_op jit(solution)/shard_map/ppermute | solution.py:32
  607.3 49.3 %collective-permute-start.108 = (bf16[192,1536]{1,0:T(8,128)(2,1)S(1)}, bf16[192,1536]{1,0:T(8,128)(2,1)S(1)}, u32[]{:S(2)}, u32[]{:S(2)}) collective-permute-start(bf16[192,1536]{1,0:T(8,128)(2,1)S(1)} %get-tuple-element.78), channel_id=1, source_target_pairs={{8,0},{12,4},{0,8},{4,12},{9,1},{13,5},{1,9},{5,13},{10,2},{14,6},... | collective-permute-start | bytes 1769480 | tf_op jit(solution)/shard_map/ppermute | solution.py:24
  611.6 49.0 %collective-permute-start.107 = (bf16[192,1536]{1,0:T(8,128)(2,1)S(1)}, bf16[192,1536]{1,0:T(8,128)(2,1)S(1)}, u32[]{:S(2)}, u32[]{:S(2)}) collective-permute-start(bf16[192,1536]{1,0:T(8,128)(2,1)S(1)} %get-tuple-element.79), channel_id=1, source_target_pairs={{4,0},{8,4},{12,8},{0,12},{5,1},{9,5},{13,9},{1,13},{6,2},{10,6},{... | collective-permute-start | bytes 1769480 | tf_op jit(solution)/shard_map/ppermute | solution.py:24
  670.1 65.3 %collective-permute-start.97 = (bf16[192,384]{1,0:T(8,128)(2,1)S(1)}, bf16[192,384]{1,0:T(8,128)(2,1)S(1)}, u32[]{:S(2)}, u32[]{:S(2)}) collective-permute-start(bf16[192,384]{1,0:T(8,128)(2,1)S(1)} %get-tuple-element.128), channel_id=1, source_target_pairs={{12,0},{0,4},{4,8},{8,12},{13,1},{1,5},{5,9},{9,13},{14,2},{2,6},{... | collective-permute-start | bytes 442376 | tf_op jit(solution)/shard_map/ppermute | solution.py:24
  670.2 65.2 %collective-permute-start.99 = (bf16[192,384]{1,0:T(8,128)(2,1)S(1)}, bf16[192,384]{1,0:T(8,128)(2,1)S(1)}, u32[]{:S(2)}, u32[]{:S(2)}) collective-permute-start(bf16[192,384]{1,0:T(8,128)(2,1)S(1)} %get-tuple-element.129), channel_id=1, source_target_pairs={{8,0},{12,4},{0,8},{4,12},{9,1},{13,5},{1,9},{5,13},{10,2},{14,6},... | collective-permute-start | bytes 442376 | tf_op jit(solution)/shard_map/ppermute | solution.py:24
  700.8 36.2 %collective-permute-start.98 = (bf16[192,384]{1,0:T(8,128)(2,1)S(1)}, bf16[192,384]{1,0:T(8,128)(2,1)S(1)}, u32[]{:S(2)}, u32[]{:S(2)}) collective-permute-start(bf16[192,384]{1,0:T(8,128)(2,1)S(1)} %get-tuple-element.130), channel_id=1, source_target_pairs={{4,0},{8,4},{12,8},{0,12},{5,1},{9,5},{13,9},{1,13},{6,2},{10,6},{... | collective-permute-start | bytes 442376 | tf_op jit(solution)/shard_map/ppermute | solution.py:24
  702.4 36.3 %collective-permute-start.86 = (f32[128,1536]{1,0:T(8,128)S(1)}, f32[128,1536]{1,0:T(8,128)S(1)}, u32[]{:S(2)}, u32[]{:S(2)}) collective-permute-start(f32[128,1536]{1,0:T(8,128)S(1)} %fusion.19), channel_id=1, source_target_pairs={{0,1},{1,0},{2,3},{3,2},{4,5},{5,4},{6,7},{7,6},{8,9},{9,8},{10,11... | collective-permute-start | bytes 2359304 | tf_op jit(solution)/shard_map/ppermute | solution.py:32
  732.9 35.3 %collective-permute-start.81 = (bf16[384,640]{1,0:T(8,128)(2,1)S(1)}, bf16[384,640]{1,0:T(8,128)(2,1)S(1)}, u32[]{:S(2)}, u32[]{:S(2)}) collective-permute-start(bf16[384,640]{1,0:T(8,128)(2,1)S(1)} %get-tuple-element.92), channel_id=1, source_target_pairs={{12,0},{0,4},{4,8},{8,12},{13,1},{1,5},{5,9},{9,13},{14,2},{2,6},{... | collective-permute-start | bytes 1474568 | tf_op jit(solution)/shard_map/ppermute | solution.py:24
  735.4 49.5 %collective-permute-start.80 = (bf16[384,640]{1,0:T(8,128)(2,1)S(1)}, bf16[384,640]{1,0:T(8,128)(2,1)S(1)}, u32[]{:S(2)}, u32[]{:S(2)}) collective-permute-start(bf16[384,640]{1,0:T(8,128)(2,1)S(1)} %get-tuple-element.93), channel_id=1, source_target_pairs={{8,0},{12,4},{0,8},{4,12},{9,1},{13,5},{1,9},{5,13},{10,2},{14,6},... | collective-permute-start | bytes 1474568 | tf_op jit(solution)/shard_map/ppermute | solution.py:24
  735.5 49.8 %collective-permute-start.79 = (bf16[384,640]{1,0:T(8,128)(2,1)S(1)}, bf16[384,640]{1,0:T(8,128)(2,1)S(1)}, u32[]{:S(2)}, u32[]{:S(2)}) collective-permute-start(bf16[384,640]{1,0:T(8,128)(2,1)S(1)} %get-tuple-element.94), channel_id=1, source_target_pairs={{4,0},{8,4},{12,8},{0,12},{5,1},{9,5},{13,9},{1,13},{6,2},{10,6},{... | collective-permute-start | bytes 1474568 | tf_op jit(solution)/shard_map/ppermute | solution.py:24
  737.1 56.2 %collective-permute-start.102 = (bf16[192,384]{1,0:T(8,128)(2,1)S(1)}, bf16[192,384]{1,0:T(8,128)(2,1)S(1)}, u32[]{:S(2)}, u32[]{:S(2)}) collective-permute-start(bf16[192,384]{1,0:T(8,128)(2,1)S(1)} %get-tuple-element.123), channel_id=1, source_target_pairs={{12,0},{0,4},{4,8},{8,12},{13,1},{1,5},{5,9},{9,13},{14,2},{2,6},{... | collective-permute-start | bytes 442376 | tf_op jit(solution)/shard_map/ppermute | solution.py:24
  738.7 54.6 %collective-permute-start.104 = (bf16[192,384]{1,0:T(8,128)(2,1)S(1)}, bf16[192,384]{1,0:T(8,128)(2,1)S(1)}, u32[]{:S(2)}, u32[]{:S(2)}) collective-permute-start(bf16[192,384]{1,0:T(8,128)(2,1)S(1)} %get-tuple-element.124), channel_id=1, source_target_pairs={{8,0},{12,4},{0,8},{4,12},{9,1},{13,5},{1,9},{5,13},{10,2},{14,6},... | collective-permute-start | bytes 442376 | tf_op jit(solution)/shard_map/ppermute | solution.py:24
  816.5 53.8 %collective-permute-start.88 = (bf16[768,1280]{1,0:T(8,128)(2,1)}, bf16[768,1280]{1,0:T(8,128)(2,1)}, u32[]{:S(2)}, u32[]{:S(2)}) collective-permute-start(bf16[768,1280]{1,0:T(8,128)(2,1)} %convolution_convert_fusion.3), channel_id=1, source_target_pairs={{16,0},{0,16},{17,1},{1,17},{18,2},{2,18},{19,3},{3,19},{20,4},{4,... | collective-permute-start | bytes 5898248 | tf_op jit(solution)/shard_map/ppermute | solution.py:28
  874.8 34.2 %collective-permute-start.89 = (bf16[192,1280]{1,0:T(8,128)(2,1)S(1)}, bf16[192,1280]{1,0:T(8,128)(2,1)S(1)}, u32[]{:S(2)}, u32[]{:S(2)}) collective-permute-start(bf16[192,1280]{1,0:T(8,128)(2,1)S(1)} %get-tuple-element.80), channel_id=1, source_target_pairs={{12,0},{0,4},{4,8},{8,12},{13,1},{1,5},{5,9},{9,13},{14,2},{2,6},{... | collective-permute-start | bytes 1474568 | tf_op jit(solution)/shard_map/ppermute | solution.py:24
  876.4 39.6 %collective-permute-start.91 = (bf16[192,1280]{1,0:T(8,128)(2,1)S(1)}, bf16[192,1280]{1,0:T(8,128)(2,1)S(1)}, u32[]{:S(2)}, u32[]{:S(2)}) collective-permute-start(bf16[192,1280]{1,0:T(8,128)(2,1)S(1)} %get-tuple-element.81), channel_id=1, source_target_pairs={{8,0},{12,4},{0,8},{4,12},{9,1},{13,5},{1,9},{5,13},{10,2},{14,6},... | collective-permute-start | bytes 1474568 | tf_op jit(solution)/shard_map/ppermute | solution.py:24
  879.7 39.3 %collective-permute-start.90 = (bf16[192,1280]{1,0:T(8,128)(2,1)S(1)}, bf16[192,1280]{1,0:T(8,128)(2,1)S(1)}, u32[]{:S(2)}, u32[]{:S(2)}) collective-permute-start(bf16[192,1280]{1,0:T(8,128)(2,1)S(1)} %get-tuple-element.82), channel_id=1, source_target_pairs={{4,0},{8,4},{12,8},{0,12},{5,1},{9,5},{13,9},{1,13},{6,2},{10,6},{... | collective-permute-start | bytes 1474568 | tf_op jit(solution)/shard_map/ppermute | solution.py:24
  (116 other events, 2289.3 us)
where the time goes:
time: 930 us; the launch traced here: 922 us
  waiting for transfers between devices  583 us (63%)
  starting transfers between devices  119 us (13%)
  matrix products  90.7 us (10%)
  local copies, waits for them, and re-layouts  50.8 us (5%)
  Pallas kernels  50.2 us (5%)
  other arithmetic  25.7 us (3%)
    ppermute x51, waiting for transfers between devices, from_context(): lax.ppermute(values, 'context', [((i + step) % size, i) for i in range(si...  327 us
    ppermute x32, waiting for transfers between devices, from_fsdp(): lax.ppermute(values, 'fsdp', [((i + step) % size, i) for i in range(size)])  188 us
    ppermute x51, starting transfers between devices, from_context(): lax.ppermute(values, 'context', [((i + step) % size, i) for i in range(si...  75.7 us
    dot_general x28, matrix products, dot(): lax.dot_general(left, right, (((left_dim,), (right_dim,)), ((), ())), pre...  73.2 us
    ppermute x34, waiting for transfers between devices, swap_tensor(): return lax.ppermute(values, 'tensor', [(i, i ^ mask) for i in range(size)])  61 us
    unnamed x161, local copies, waits for them, and re-layouts  28.5 us
    ppermute x32, starting transfers between devices, from_fsdp(): lax.ppermute(values, 'fsdp', [((i + step) % size, i) for i in range(size)])  26.8 us
    pallas_call x1, Pallas kernels, self_backward(): pl.pallas_call(functools.partial(self_backward_kernel, frames, order), ou...  24.5 us
  transfers between devices with their start and end apart: 119, of which 51 were waited for; matrix products, arithmetic and copies ran while one was open for 14% of the time, Pallas kernels for 5%

commit v1 on v0

--- a/solution.py
+++ b/solution.py
@@ -41,43 +41,45 @@
     return order
 
 
-def gather_group(shard, fsdp_size, context_size, axis=0):
-    arrived = {0: shard}
+def gather_group(shard, sizes, own):
+    fsdp_size, context_size = sizes
+    own_fsdp, own_context = own
+    rows = shard.shape[0]
+    pieces = [(0, 0, shard)]
+    for far in range(1, fsdp_size):
+        pieces.append((far, 0, from_fsdp(shard, far, fsdp_size)))
     for step in shift_order(context_size):
-        arrived[step] = from_context(shard, step, context_size)
-    pieces = [arrived[step] for step in range(context_size)]
-    for far in range(1, fsdp_size):
-        there = {0: from_fsdp(shard, far, fsdp_size)}
-        for step in shift_order(context_size):
-            there[step] = from_fsdp(arrived[step], far, fsdp_size)
-        pieces += [there[step] for step in range(context_size)]
-    return jnp.concatenate(pieces, axis=axis)
-
-
-def reduce_fsdp(near, far_blocks, fsdp_size):
-    total = near
+        arrived = from_context(shard, step, context_size)
+        pieces.append((0, step, arrived))
+        for far in range(1, fsdp_size):
+            pieces.append((far, step, from_fsdp(arrived, far, fsdp_size)))
+    result = jnp.zeros((fsdp_size * context_size,) + shard.shape, shard.dtype)
+    for far, step, piece in pieces:
+        index = lax.rem(own_fsdp + far, fsdp_size) * context_size + lax.rem(
+            own_context + step, context_size
+        )
+        result = lax.dynamic_update_index_in_dim(result, piece, index, 0)
+    return result.reshape((fsdp_size * context_size * rows,) + shard.shape[1:])
+
+
+def reduce_group(parts, sizes, own):
+    fsdp_size, context_size = sizes
+    own_fsdp, own_context = own
+    kind = low if parts.shape[1] * parts.shape[2] > 16384 else wide
+    parts = parts.reshape((fsdp_size, context_size) + parts.shape[1:])
+    total = pick(parts, own_fsdp)
     for step in range(1, fsdp_size):
-        total = total + from_fsdp(far_blocks[step - 1], fsdp_size - step, fsdp_size).astype(wide)
-    return total
-
-
-def reduce_context(total, context_size):
-    rows = total.shape[0] // context_size
-    result = total[:rows]
+        piece = pick(parts, lax.rem(own_fsdp + step, fsdp_size)).astype(kind)
+        total = total + from_fsdp(piece, fsdp_size - step, fsdp_size).astype(wide)
+    result = pick(total, own_context)
     for step in shift_order(context_size):
-        piece = total[step * rows : (step + 1) * rows].astype(low)
+        piece = pick(total, lax.rem(own_context + step, context_size)).astype(kind)
         result = result + from_context(piece, context_size - step, context_size).astype(wide)
     return result
 
 
-def weight_grad(left_rows, right_rows, fsdp_size, context_size):
-    half = left_rows.shape[-1] // fsdp_size
-    far = [
-        dot(left_rows[:, step * half : (step + 1) * half], right_rows, 0, 0).astype(low)
-        for step in range(1, fsdp_size)
-    ]
-    near = dot(left_rows[:, :half], right_rows, 0, 0)
-    return reduce_context(reduce_fsdp(near, far, fsdp_size), context_size)
+def pick(values, index):
+    return lax.dynamic_index_in_dim(values, index, 0, keepdims=False)
 
 
 def gather_rows(values, tensor_size):
@@ -402,10 +404,6 @@
     )(query, key, value, grad)
 
 
-def pick(values, index):
-    return lax.dynamic_index_in_dim(values, index, 0, keepdims=False)
-
-
 def to_heads(chunks, own, size):
     slots = {0: pick(chunks, own)}
     for step in shift_order(size):
@@ -420,16 +418,6 @@
         arrived[step] = from_context(slots[step], step, size)
     stacked = jnp.stack([arrived[step] for step in range(size)])
     return jnp.stack([pick(stacked, lax.rem(j - own + size, size)) for j in range(size)])
-
-
-def relative_columns(own_fsdp, own_context, fsdp_size, context_size, width):
-    block = width // (fsdp_size * context_size)
-    there = lax.broadcasted_iota(jnp.int32, (width, width), 0)
-    here = lax.broadcasted_iota(jnp.int32, (width, width), 1)
-    far = lax.rem(here // (block * context_size) + own_fsdp, fsdp_size)
-    step = lax.rem(lax.rem(here // block, context_size) + own_context, context_size)
-    source = (far * context_size + step) * block + lax.rem(here, block)
-    return (there == source).astype(low)
 
 
 def on_device(sizes, frames, text_states, cotangent, *parameters):
@@ -456,29 +444,38 @@
     halves = nc // clips
     width = columns // halves
     padded = -(-3 * width // 128) * 128
-    gather = functools.partial(gather_group, fsdp_size=nf, context_size=nc)
     place = jnp.stack([own_context, own_tensor]).astype(jnp.int32)
-
-    vectors = gather(jnp.stack(parameters[10:16] + parameters[10:12]), axis=1).astype(wide)
+    group = ((nf, nc), (own_fsdp, own_context))
+    both = ("fsdp", "context")
+
+    vectors = lax.all_gather(jnp.stack(parameters[10:16] + parameters[10:12]), both, axis=0)
+    vectors = vectors.transpose(1, 0, 2).reshape(-1, features).astype(wide)
     pieces = []
     for part in range(halves):
         lanes = slice(part * width, (part + 1) * width)
         pieces += [self_query[:, lanes], self_key[:, lanes], self_value[:, lanes]]
         if padded > 3 * width:
             pieces.append(jnp.zeros((block, padded - 3 * width), low))
-    qkv_all = gather(jnp.concatenate(pieces, axis=1))
-    second_all = gather(jnp.concatenate([self_out, cross_query], axis=1))
-    third_all = gather(jnp.concatenate([cross_key, cross_value, cross_out], axis=1))
-    feed_in_all = gather(feed_in)
-    feed_out_all = gather(feed_out)
+    qkv_all = gather_group(jnp.concatenate(pieces, axis=1), *group)
+    second_all = gather_group(jnp.concatenate([self_out, cross_query], axis=1), *group)
+    third_all = gather_group(jnp.concatenate([cross_key, cross_value, cross_out], axis=1), *group)
+    feed_in_all = lax.all_gather(feed_in, both, axis=0, tiled=True)
+    feed_out_all = lax.all_gather(feed_out, both, axis=0, tiled=True)
     self_out_all, cross_query_all = second_all[:, :columns], second_all[:, columns:]
     cross_key_value = third_all[:, : 2 * columns]
     cross_out_all = third_all[:, 2 * columns :]
 
-    relative = relative_columns(own_fsdp, own_context, nf, nc, features)
-    residual = jnp.einsum("fcd,de->cfe", frames, relative, preferred_element_type=wide)
-    incoming = jnp.einsum("fcd,de->cfe", cotangent, relative, preferred_element_type=wide)
-    text = jnp.einsum("tcd,de->cte", text_states, relative, preferred_element_type=wide).astype(low)
+    residual = frames.transpose(1, 0, 2).astype(wide)
+    incoming = cotangent.transpose(1, 0, 2)
+    text = text_states.transpose(1, 0, 2)
+
+    def weight_grad(left_rows, right_rows):
+        parts = dot(left_rows, right_rows, 0, 0).reshape(nf * nc, block, -1)
+        return reduce_group(parts, *group)
+
+    def feed_grad(left_rows, right_rows):
+        parts = dot(left_rows, right_rows, 0, 0).astype(low)
+        return lax.psum_scatter(parts, both, scatter_dimension=0, tiled=True).astype(wide)
 
     def by_row(values):
         return values.reshape(-1, values.shape[-1])
@@ -513,26 +510,26 @@
     gate = 0.5 + 0.5 * lax.erf(hidden * (0.5**0.5))
     active = (hidden * gate).astype(low)
     layer_out = after_cross + scatter_rows(by_clip(dot(active, feed_out_all, 1, 1)), nt)
-    layer_out = jnp.einsum("cfe,de->fcd", layer_out.astype(low), relative, preferred_element_type=wide).astype(low)
-
-    grad_rows = by_row(gather_rows(incoming.astype(low), nt))
+    layer_out = layer_out.astype(low).transpose(1, 0, 2)
+
+    grad_rows = by_row(gather_rows(incoming, nt))
     grad_active = dot(grad_rows, feed_out_all, 1, 0)
-    feed_out_grad = weight_grad(grad_rows, active, nf, nc)
+    feed_out_grad = feed_grad(grad_rows, active)
     slope = gate + hidden * jnp.exp(-0.5 * hidden * hidden) * ((2.0 * jnp.pi) ** -0.5)
     grad_hidden = (grad_active * slope).astype(low)
-    feed_in_grad = weight_grad(normed_three, grad_hidden, nf, nc)
+    feed_in_grad = feed_grad(normed_three, grad_hidden)
     grad_normed = scatter_rows(by_clip(dot(grad_hidden, feed_in_all, 1, 1)), nt)
     piece, third_gain, third_shift = norm_back(after_cross, vectors[4], grad_normed)
-    grad_after_cross = incoming + piece
+    grad_after_cross = incoming.astype(wide) + piece
 
     grad_rows = by_row(gather_rows(grad_after_cross.astype(low), nt))
     grad_crossed = by_clip(dot(grad_rows, cross_out_all, 1, 0).astype(low))
-    cross_out_grad = weight_grad(grad_rows, by_row(crossed), nf, nc)
+    cross_out_grad = weight_grad(grad_rows, by_row(crossed))
     grad_cross_queries, grad_cross_keys, grad_cross_values = cross_backward(
         cross_queries, cross_keys, cross_values, grad_crossed
     )
     grad_cross_queries = by_row(grad_cross_queries)
-    cross_query_grad = weight_grad(normed_two, grad_cross_queries, nf, nc)
+    cross_query_grad = weight_grad(normed_two, grad_cross_queries)
     grad_normed = scatter_rows(by_clip(dot(grad_cross_queries, cross_query_all, 1, 1)), nt)
     piece, second_gain, second_shift = norm_back(after_self, vectors[2], grad_normed)
     grad_after_self = grad_after_cross + piece
@@ -545,36 +542,28 @@
         )
         mask *= 2
     text_low = text_grads.astype(low)
-    near_columns = by_row(text[..., :block])
-    far_blocks = [
-        dot(by_row(text[..., far * nc * block : far * nc * block + block]), text_low, 0, 0).astype(low)
-        for far in range(1, nf)
-    ]
-    key_value_grad = reduce_fsdp(dot(near_columns, text_low, 0, 0), far_blocks, nf)
+    text_parts = dot(by_row(text), text_low, 0, 0).reshape(nf, nc, block, 2 * columns)
+    key_value_grad = pick(pick(text_parts, own_fsdp), own_context)
+    for step in range(1, nf):
+        part = pick(pick(text_parts, lax.rem(own_fsdp + step, nf)), own_context).astype(low)
+        key_value_grad = key_value_grad + from_fsdp(part, nf - step, nf).astype(wide)
     text_part = dot(text_low, cross_key_value, 1, 1)
     mask = 1
     while mask < nt:
         text_part = text_part + swap_tensor(text_part, mask, nt)
         mask *= 2
-    text_grad = jnp.einsum(
-        "cte,de->tcd", by_clip(text_part), relative.astype(wide), precision=lax.Precision.HIGHEST
-    )
+    text_grad = by_clip(text_part).transpose(1, 0, 2)
 
     grad_rows = by_row(gather_rows(grad_after_self.astype(low), nt))
     grad_attended = by_clip(dot(grad_rows, self_out_all, 1, 0).astype(low))
-    self_out_grad = weight_grad(grad_rows, attended, nf, nc)
+    self_out_grad = weight_grad(grad_rows, attended)
     head_grad = to_heads(to_chunks(grad_attended, width), own_context, nc)
     head_back = self_backward(place, head_rows, head_out, head_top, head_grad, frame_count, order)
     grad_projected = by_row(from_chunks(to_frames(head_back, own_context, nc)))
-    qkv_grad = weight_grad(normed_one, grad_projected, nf, nc)
+    qkv_grad = weight_grad(normed_one, grad_projected)
     grad_normed = scatter_rows(by_clip(dot(grad_projected, qkv_all, 1, 1)), nt)
     piece, first_gain, first_shift = norm_back(residual, vectors[0], grad_normed)
-    frames_grad = jnp.einsum(
-        "cfe,de->fcd",
-        grad_after_self + piece,
-        relative.astype(wide),
-        precision=lax.Precision.HIGHEST,
-    )
+    frames_grad = (grad_after_self + piece).transpose(1, 0, 2)
 
     norm_grads = jnp.stack(
         [first_gain, first_shift, second_gain, second_shift, third_gain, third_shift]
@@ -583,15 +572,8 @@
     while mask < nt:
         norm_grads = norm_grads + swap_tensor(norm_grads, mask, nt)
         mask *= 2
-    half = nc * block
-    total = norm_grads[:, :half]
-    for step in range(1, nf):
-        total = total + from_fsdp(norm_grads[:, step * half : (step + 1) * half], nf - step, nf)
-    norm_result = total[:, :block]
-    for step in shift_order(nc):
-        norm_result = norm_result + from_context(
-            total[:, step * block : (step + 1) * block], nc - step, nc
-        )
+    norm_parts = norm_grads.reshape(6, nf * nc, block).transpose(1, 0, 2)
+    norm_result = reduce_group(norm_parts, *group)
 
     qkv_parts = []
     for kind in range(3):

time: 930 us -> 886 us (0.953)
  waiting for transfers between devices: 583 us -> 388 us
  blocking collectives: 0 us -> 60.6 us
  local copies, waits for them, and re-layouts: 50.8 us -> 110 us
  other arithmetic: 25.7 us -> 53.2 us
  matrix products: 90.7 us -> 76 us
  between operations: 2.89 us -> 16.1 us
    ppermute x32 -> x18, waiting for transfers between devices: 188 us -> 67.1 us  [from_fsdp(): lax.ppermute(values, 'fsdp', [((i + step) % size, i) for i in range(size)])]
    ppermute x51 -> x36, waiting for transfers between devices: 327 us -> 231 us  [from_context(): lax.ppermute(values, 'context', [((i + step) % size, i) for i in range(si...]
    all_gather x0 -> x1, blocking collectives: none -> 60.6 us  [on_device(): lax.all_gather(jnp.stack(parameters[10:16] + parameters[10:12]), both, ax...]
    dynamic_update_slice x0 -> x24, local copies, waits for them, and re-layouts: none -> 24.2 us  [gather_group(): result = lax.dynamic_update_index_in_dim(result, piece, index, 0)]
    dot_general x0 -> x5, local copies, waits for them, and re-layouts: none -> 21.8 us  [dot(): lax.dot_general(left, right, (((left_dim,), (right_dim,)), ((), ())), pre...]
    dot_general x6 -> x0, matrix products: 17.5 us -> none  [the longest x1 5.24 us: on_device(): jnp.einsum('cfe,de->fcd', grad_after_self + piece, relative.astype(wide),...]
    ppermute x2, waiting for transfers between devices: 6.44 us -> 18.1 us  [on_device(): lax.ppermute(text_grads, 'context', [(i, i ^ mask) for i in range(nc)])]
    ppermute x34, waiting for transfers between devices: 61 us -> 70.6 us  [swap_tensor(): return lax.ppermute(values, 'tensor', [(i, i ^ mask) for i in range(size)])]
  transfers between devices with their start and end apart: 119 -> 94, of which waited for: 51 -> 39; matrix products, arithmetic and copies ran while one was open for 14% -> 24% of each run, Pallas kernels for 5% -> 6%
where the time goes in v1:
time: 886 us; the launch traced here: 875 us
  waiting for transfers between devices  388 us (44%)
  starting transfers between devices  122 us (14%)
  local copies, waits for them, and re-layouts  110 us (12%)
  matrix products  76 us (9%)
  blocking collectives  60.6 us (7%)
  other arithmetic  53.2 us (6%)
  Pallas kernels  49.8 us (6%)
  between operations  16.1 us (2%)
    ppermute x36, waiting for transfers between devices, from_context(): lax.ppermute(values, 'context', [((i + step) % size, i) for i in range(si...  231 us
    ppermute x36, starting transfers between devices, from_context(): lax.ppermute(values, 'context', [((i + step) % size, i) for i in range(si...  78.2 us
    dot_general x21, matrix products, dot(): lax.dot_general(left, right, (((left_dim,), (right_dim,)), ((), ())), pre...  76 us
    ppermute x34, waiting for transfers between devices, swap_tensor(): return lax.ppermute(values, 'tensor', [(i, i ^ mask) for i in range(size)])  70.6 us
    ppermute x18, waiting for transfers between devices, from_fsdp(): lax.ppermute(values, 'fsdp', [((i + step) % size, i) for i in range(size)])  67.1 us
    all_gather x1, blocking collectives, on_device(): lax.all_gather(jnp.stack(parameters[10:16] + parameters[10:12]), both, ax...  60.6 us
    unnamed x182, local copies, waits for them, and re-layouts  33 us
    pallas_call x1, Pallas kernels, self_backward(): pl.pallas_call(functools.partial(self_backward_kernel, frames, order), ou...  24.4 us
  transfers between devices with their start and end apart: 94, of which 39 were waited for; matrix products, arithmetic and copies ran while one was open for 24% of the time, Pallas kernels for 6%

profile of v1, /device:TPU:8, one launch (start us, length us, event | category | flops | bytes accessed | tf_op | source)
XLA Modules:
  0.0 875.5 jit_solution(10528930742954384164)
XLA Ops:
  21.7 60.6 %all-gather = bf16[64,192]{1,0:T(8,128)(2,1)S(1)} all-gather(bf16[8,192]{1,0:T(8,128)(2,1)S(1)} %stack.144), channel_id=2, replica_groups=mesh['fsdp'=2,'context'=4,'tensor'=4] {'fsdp','context'}, dimensions={0}, use_global_device_ids=true | all-gather | bytes 27648 | tf_op jit(solution)/shard_map/all_gather | solution.py:451
  101.2 5.3 collective-permute-done.18
  108.8 28.2 %collective-permute-done.6 = bf16[192,1280]{1,0:T(8,128)(2,1)S(1)} collective-permute-done((bf16[192,1280]{1,0:T(8,128)(2,1)}, bf16[192,1280]{1,0:T(8,128)(2,1)S(1)}, u32[]{:S(2)}, u32[]{:S(2)}) %collective-permute-start.6) | collective-permute-done | bytes 491552 | tf_op jit(solution)/shard_map/ppermute | solution.py:24
  141.9 4.4 collective-permute-done.8
  150.3 20.6 %collective-permute-done.9 = bf16[192,1280]{1,0:T(8,128)(2,1)S(1)} collective-permute-done((bf16[192,1280]{1,0:T(8,128)(2,1)S(1)}, bf16[192,1280]{1,0:T(8,128)(2,1)S(1)}, u32[]{:S(2)}, u32[]{:S(2)}) %collective-permute-start.9) | collective-permute-done | bytes 491552 | tf_op jit(solution)/shard_map/ppermute | solution.py:28
  172.0 2.8 copy-done.32
  174.8 3.2 convolution_convert_fusion.2
  178.6 4.5 collective-permute-start.12
  187.8 30.2 %collective-permute-done.12 = bf16[384,640]{1,0:T(8,128)(2,1)S(1)} collective-permute-done((bf16[384,640]{1,0:T(8,128)(2,1)S(1)}, bf16[384,640]{1,0:T(8,128)(2,1)S(1)}, u32[]{:S(2)}, u32[]{:S(2)}) %collective-permute-start.12) | collective-permute-done | bytes 491552 | tf_op jit(solution)/shard_map/ppermute | solution.py:24
  219.0 18.7 %collective-permute-done.11 = bf16[384,640]{1,0:T(8,128)(2,1)S(1)} collective-permute-done((bf16[384,640]{1,0:T(8,128)(2,1)S(1)}, bf16[384,640]{1,0:T(8,128)(2,1)S(1)}, u32[]{:S(2)}, u32[]{:S(2)}) %collective-permute-start.11) | collective-permute-done | bytes 491552 | tf_op jit(solution)/shard_map/ppermute | solution.py:24
  237.7 33.8 %collective-permute-done.10 = bf16[384,640]{1,0:T(8,128)(2,1)S(1)} collective-permute-done((bf16[384,640]{1,0:T(8,128)(2,1)S(1)}, bf16[384,640]{1,0:T(8,128)(2,1)S(1)}, u32[]{:S(2)}, u32[]{:S(2)}) %collective-permute-start.10) | collective-permute-done | bytes 491552 | tf_op jit(solution)/shard_map/ppermute | solution.py:24
  271.8 18.0 %shard_map.330 = (bf16[4,384,192]{2,1,0:T(8,128)(2,1)S(1)}, f32[4,3,384]{2,1,0:T(4,128)S(1)}) custom-call(s32[2]{0:T(128)S(1)} %pad_add_fusion.place_ref, bf16[4,384,640]{2,1,0:T(8,128)(2,1)S(1)} %pad_maximum_fusion.7.rows_ref), custom_call_target="tpu_custom_call" | custom-call | flops 1132462080 | bytes 3932160 | tf_op jit(solution)/shard_map/pallas_call | solution.py:290
  289.9 8.2 collective-permute-start.15
  298.1 4.3 collective-permute-start.14
  303.1 9.2 %collective-permute-done.15 = bf16[384,192]{1,0:T(8,128)(2,1)S(1)} collective-permute-done((bf16[384,192]{1,0:T(8,128)(2,1)S(1)}, bf16[384,192]{1,0:T(8,128)(2,1)S(1)}, u32[]{:S(2)}, u32[]{:S(2)}) %collective-permute-start.15) | collective-permute-done | bytes 147488 | tf_op jit(solution)/shard_map/ppermute | solution.py:24
  312.5 6.6 collective-permute-done.14
  322.0 2.7 fusion.26
  342.3 21.7 %collective-permute-done.30 = bf16[192,1152]{1,0:T(8,128)(2,1)S(1)} collective-permute-done((bf16[192,1152]{1,0:T(8,128)(2,1)}, bf16[192,1152]{1,0:T(8,128)(2,1)S(1)}, u32[]{:S(2)}, u32[]{:S(2)}) %collective-permute-start.30) | collective-permute-done | bytes 442400 | tf_op jit(solution)/shard_map/ppermute | solution.py:28
  371.5 11.0 %collective-permute-done.25 = bf16[2,96,1536]{2,1,0:T(8,128)(2,1)S(1)} collective-permute-done((bf16[2,96,1536]{2,1,0:T(8,128)(2,1)S(1)}, bf16[2,96,1536]{2,1,0:T(8,128)(2,1)S(1)}, u32[]{:S(2)}, u32[]{:S(2)}) %collective-permute-start.25) | collective-permute-done | bytes 589856 | tf_op jit(solution)/shard_map/ppermute | solution.py:32
  389.4 3.3 shard_map.331
  392.7 2.7 fusion.24
  404.3 13.5 %collective-permute-done.36 = bf16[2,96,1536]{2,1,0:T(8,128)(2,1)} collective-permute-done((bf16[2,96,1536]{2,1,0:T(8,128)(2,1)}, bf16[2,96,1536]{2,1,0:T(8,128)(2,1)}, u32[]{:S(2)}, u32[]{:S(2)}) %collective-permute-start.36) | collective-permute-done | bytes 589856 | tf_op jit(solution)/shard_map/ppermute | solution.py:32
  422.4 8.0 collective-permute-done.42
  430.9 11.4 %collective-permute-done.37 = bf16[2,96,1536]{2,1,0:T(8,128)(2,1)S(1)} collective-permute-done((bf16[2,96,1536]{2,1,0:T(8,128)(2,1)S(1)}, bf16[2,96,1536]{2,1,0:T(8,128)(2,1)S(1)}, u32[]{:S(2)}, u32[]{:S(2)}) %collective-permute-start.37) | collective-permute-done | bytes 589856 | tf_op jit(solution)/shard_map/ppermute | solution.py:32
  442.3 2.8 pad_maximum_fusion.3
  446.7 8.2 multiply_convert_fusion
  456.3 5.7 convolution_convert_fusion
  462.0 8.4 fusion.5
  470.4 6.6 fusion.109
  484.1 4.4 copy.65
  488.5 4.3 copy.67
  492.8 6.0 collective-permute-done.46
  503.9 5.9 fusion.108
  513.9 3.8 collective-permute-done.47
  517.7 5.7 convolution_convert_fusion.1
  525.2 3.5 convolution_convert_fusion.4
  528.8 4.1 shard_map.332
  546.3 4.3 copy.69
  556.6 7.2 collective-permute-done.63
  563.8 3.5 collective-permute-start.64
  568.4 3.3 fusion.92
  575.0 2.9 collective-permute-start.76
  579.6 6.6 collective-permute-done.52
  586.2 10.9 %collective-permute-done.64 = f32[128,768]{1,0:T(8,128)S(1)} collective-permute-done((f32[128,768]{1,0:T(8,128)S(1)}, f32[128,768]{1,0:T(8,128)S(1)}, u32[]{:S(2)}, u32[]{:S(2)}) %collective-permute-start.64) | collective-permute-done | bytes 393248 | tf_op jit(solution)/shard_map/ppermute | solution.py:540
  597.2 3.0 convolution_bitcast_fusion
  605.3 12.6 %collective-permute-start.57 = (bf16[384,192]{1,0:T(8,128)(2,1)}, bf16[384,192]{1,0:T(8,128)(2,1)S(1)}, u32[]{:S(2)}, u32[]{:S(2)}) collective-permute-start(bf16[384,192]{1,0:T(8,128)(2,1)} %get-tuple-element.134), channel_id=1, source_target_pairs={{4,0},{8,4},{12,8},{0,12},{5,1},{9,5},{13,9},{1,13},{6,2},{10,6},{... | collective-permute-start | bytes 442376 | tf_op jit(solution)/shard_map/ppermute | solution.py:24
  619.4 3.4 fusion.6
  622.8 6.1 copy.68
  630.0 8.4 collective-permute-done.57
  640.2 8.1 collective-permute-start.81
  648.2 2.8 collective-permute-done.55
  653.7 24.4 %shard_map.333 = bf16[4,384,640]{2,1,0:T(8,128)(2,1)S(1)} custom-call(s32[2]{0:T(128)S(1)} %pad_add_fusion.place_ref, bf16[4,384,640]{2,1,0:T(8,128)(2,1)S(1)} %pad_maximum_fusion.7.rows_ref, bf16[4,384,192]{2,1,0:T(8,128)(2,1)S(1)} %copy-done.1, f32[4,3,384]{2,1,0:T(4,128)S(1)} %get-tuple-element.26.top_ref, ...), custom_call_target="tpu_custom_call" | custom-call | flops 2831155200 | bytes 7864320 | tf_op jit(solution)/shard_map/pallas_call | solution.py:311
  686.1 9.0 %collective-permute-done.82 = bf16[192,384]{1,0:T(8,128)(2,1)S(1)} collective-permute-done((bf16[192,384]{1,0:T(8,128)(2,1)S(1)}, bf16[192,384]{1,0:T(8,128)(2,1)S(1)}, u32[]{:S(2)}, u32[]{:S(2)}) %collective-permute-start.82) | collective-permute-done | bytes 147488 | tf_op jit(solution)/shard_map/ppermute | solution.py:24
  695.2 3.5 collective-permute-start.58
  705.1 2.7 copy.66
  708.9 30.6 %collective-permute-done.59 = bf16[384,640]{1,0:T(8,128)(2,1)} collective-permute-done((bf16[384,640]{1,0:T(8,128)(2,1)}, bf16[384,640]{1,0:T(8,128)(2,1)}, u32[]{:S(2)}, u32[]{:S(2)}) %collective-permute-start.59) | collective-permute-done | bytes 491552 | tf_op jit(solution)/shard_map/ppermute | solution.py:24
  745.8 3.2 fusion.11
  753.8 3.3 fusion.15
  777.3 3.3 collective-permute-done.72
  787.2 2.9 collective-permute-done.85
  791.6 18.5 %collective-permute-done.86 = f32[4,6,192]{2,0,1:T(4,128)S(1)} collective-permute-done((f32[4,6,192]{2,0,1:T(4,128)S(1)}, f32[4,6,192]{2,0,1:T(4,128)S(1)}, u32[]{:S(2)}, u32[]{:S(2)}) %collective-permute-start.86) | collective-permute-done | bytes 18464 | tf_op jit(solution)/shard_map/ppermute | solution.py:28
  813.9 3.1 bitcast_add_fusion
  823.9 27.0 %collective-permute-done.68 = bf16[192,1280]{1,0:T(8,128)(2,1)S(1)} collective-permute-done((bf16[192,1280]{1,0:T(8,128)(2,1)S(1)}, bf16[192,1280]{1,0:T(8,128)(2,1)S(1)}, u32[]{:S(2)}, u32[]{:S(2)}) %collective-permute-start.68) | collective-permute-done | bytes 491552 | tf_op jit(solution)/shard_map/ppermute | solution.py:24
  850.9 8.3 collective-permute-done.70
  (508 shorter events, 234.3 us)
Async XLA Ops:
  7.3 439.5 %all-gather.4.cloned.1.call-start = ((), (), s32[]{:S(2)}) async-start(), calls=%async_computation.2 | async-start | bytes 5308416 | tf_op jit(solution)/shard_map/all_gather | solution.py:462
  8.0 454.0 %all-gather.6.cloned.1.call-start = ((), (), s32[]{:S(2)}) async-start(), calls=%async_computation.3 | async-start | bytes 5308416 | tf_op jit(solution)/shard_map/all_gather | solution.py:463
  11.3 174.9 %collective-permute-start.21 = (bf16[192,768]{1,0:T(8,128)(2,1)}, bf16[192,768]{1,0:T(8,128)(2,1)}, u32[]{:S(2)}, u32[]{:S(2)}) collective-permute-start(bf16[192,768]{1,0:T(8,128)(2,1)} %constant_dynamic-update-slice_fusion), channel_id=1, source_target_pairs={{8,0},{12,4},{0,8},{4,12},{9,1},{13,5},{1,9},{5,13},{10,2},{14,6},... | collective-permute-start | bytes 884744 | tf_op jit(solution)/shard_map/ppermute | solution.py:24
  13.8 78.3 %collective-permute-start.17 = (bf16[192,768]{1,0:T(8,128)(2,1)}, bf16[192,768]{1,0:T(8,128)(2,1)}, u32[]{:S(2)}, u32[]{:S(2)}) collective-permute-start(bf16[192,768]{1,0:T(8,128)(2,1)} %constant_dynamic-update-slice_fusion), channel_id=1, source_target_pairs={{4,0},{8,4},{12,8},{0,12},{5,1},{9,5},{13,9},{1,13},{6,2},{10,6},{... | collective-permute-start | bytes 884744 | tf_op jit(solution)/shard_map/ppermute | solution.py:24
  14.3 74.9 %collective-permute-start.16 = (bf16[192,768]{1,0:T(8,128)(2,1)}, bf16[192,768]{1,0:T(8,128)(2,1)}, u32[]{:S(2)}, u32[]{:S(2)}) collective-permute-start(bf16[192,768]{1,0:T(8,128)(2,1)} %constant_dynamic-update-slice_fusion), channel_id=1, source_target_pairs={{16,0},{0,16},{17,1},{1,17},{18,2},{2,18},{19,3},{3,19},{20,4},{4,... | collective-permute-start | bytes 884744 | tf_op jit(solution)/shard_map/ppermute | solution.py:28
  19.1 76.3 %collective-permute-start.4 = (bf16[192,1280]{1,0:T(8,128)(2,1)}, bf16[192,1280]{1,0:T(8,128)(2,1)}, u32[]{:S(2)}, u32[]{:S(2)}) collective-permute-start(bf16[192,1280]{1,0:T(8,128)(2,1)} %concatenate.70), channel_id=1, source_target_pairs={{4,0},{8,4},{12,8},{0,12},{5,1},{9,5},{13,9},{1,13},{6,2},{10,6},{... | collective-permute-start | bytes 1474568 | tf_op jit(solution)/shard_map/ppermute | solution.py:24
  20.5 75.3 %collective-permute-start.3 = (bf16[192,1280]{1,0:T(8,128)(2,1)}, bf16[192,1280]{1,0:T(8,128)(2,1)}, u32[]{:S(2)}, u32[]{:S(2)}) collective-permute-start(bf16[192,1280]{1,0:T(8,128)(2,1)} %concatenate.70), channel_id=1, source_target_pairs={{16,0},{0,16},{17,1},{1,17},{18,2},{2,18},{19,3},{3,19},{20,4},{4,... | collective-permute-start | bytes 1474568 | tf_op jit(solution)/shard_map/ppermute | solution.py:28
  21.0 843.1 %reduce-scatter.5.cloned.1.call-start = ((), (), s32[]{:S(2)}) async-start(), calls=%async_computation.5 | async-start | bytes 5308416 | tf_op jit(solution)/shard_map/reduce_scatter | solution.py:478
  89.2 52.7 %collective-permute-start.19 = (bf16[192,768]{1,0:T(8,128)(2,1)}, bf16[192,768]{1,0:T(8,128)(2,1)S(1)}, u32[]{:S(2)}, u32[]{:S(2)}) collective-permute-start(bf16[192,768]{1,0:T(8,128)(2,1)} %constant_dynamic-update-slice_fusion), channel_id=1, source_target_pairs={{12,0},{0,4},{4,8},{8,12},{13,1},{1,5},{5,9},{9,13},{14,2},{2,6},{... | collective-permute-start | bytes 884744 | tf_op jit(solution)/shard_map/ppermute | solution.py:24
  92.2 44.8 %collective-permute-start.6 = (bf16[192,1280]{1,0:T(8,128)(2,1)}, bf16[192,1280]{1,0:T(8,128)(2,1)S(1)}, u32[]{:S(2)}, u32[]{:S(2)}) collective-permute-start(bf16[192,1280]{1,0:T(8,128)(2,1)} %concatenate.70), channel_id=1, source_target_pairs={{12,0},{0,4},{4,8},{8,12},{13,1},{1,5},{5,9},{9,13},{14,2},{2,6},{... | collective-permute-start | bytes 1474568 | tf_op jit(solution)/shard_map/ppermute | solution.py:24
  95.8 42.9 %collective-permute-start.5 = (bf16[192,1280]{1,0:T(8,128)(2,1)}, bf16[192,1280]{1,0:T(8,128)(2,1)S(1)}, u32[]{:S(2)}, u32[]{:S(2)}) collective-permute-start(bf16[192,1280]{1,0:T(8,128)(2,1)} %collective-permute-done.4), channel_id=1, source_target_pairs={{16,0},{0,16},{17,1},{1,17},{18,2},{2,18},{19,3},{3,19},{20,4},{4,... | collective-permute-start | bytes 1474568 | tf_op jit(solution)/shard_map/ppermute | solution.py:28
  106.5 39.8 %collective-permute-start.8 = (bf16[192,1280]{1,0:T(8,128)(2,1)}, bf16[192,1280]{1,0:T(8,128)(2,1)S(1)}, u32[]{:S(2)}, u32[]{:S(2)}) collective-permute-start(bf16[192,1280]{1,0:T(8,128)(2,1)} %concatenate.70), channel_id=1, source_target_pairs={{8,0},{12,4},{0,8},{4,12},{9,1},{13,5},{1,9},{5,13},{10,2},{14,6},... | collective-permute-start | bytes 1474568 | tf_op jit(solution)/shard_map/ppermute | solution.py:24
  141.9 29.9 %collective-permute-start.1 = (bf16[2,96,1536]{2,1,0:T(8,128)(2,1)S(1)}, bf16[2,96,1536]{2,1,0:T(8,128)(2,1)S(1)}, u32[]{:S(2)}, u32[]{:S(2)}) collective-permute-start(bf16[2,96,1536]{2,1,0:T(8,128)(2,1)S(1)} %fusion.35), channel_id=1, source_target_pairs={{0,1},{1,0},{2,3},{3,2},{4,5},{5,4},{6,7},{7,6},{8,9},{9,8},{10,11... | collective-permute-start | bytes 1769480 | tf_op jit(solution)/shard_map/ppermute | solution.py:32
  146.3 38.6 %collective-permute-start.20 = (bf16[192,768]{1,0:T(8,128)(2,1)S(1)}, bf16[192,768]{1,0:T(8,128)(2,1)S(1)}, u32[]{:S(2)}, u32[]{:S(2)}) collective-permute-start(bf16[192,768]{1,0:T(8,128)(2,1)S(1)} %collective-permute-done.19), channel_id=1, source_target_pairs={{16,0},{0,16},{17,1},{1,17},{18,2},{2,18},{19,3},{3,19},{20,4},{4,... | collective-permute-start | bytes 884744 | tf_op jit(solution)/shard_map/ppermute | solution.py:28
  147.9 23.0 %collective-permute-start.9 = (bf16[192,1280]{1,0:T(8,128)(2,1)S(1)}, bf16[192,1280]{1,0:T(8,128)(2,1)S(1)}, u32[]{:S(2)}, u32[]{:S(2)}) collective-permute-start(bf16[192,1280]{1,0:T(8,128)(2,1)S(1)} %collective-permute-done.8), channel_id=1, source_target_pairs={{16,0},{0,16},{17,1},{1,17},{18,2},{2,18},{19,3},{3,19},{20,4},{4,... | collective-permute-start | bytes 1474568 | tf_op jit(solution)/shard_map/ppermute | solution.py:28
  148.7 23.1 %collective-permute-start.2 = (bf16[2,96,1536]{2,1,0:T(8,128)(2,1)S(1)}, bf16[2,96,1536]{2,1,0:T(8,128)(2,1)S(1)}, u32[]{:S(2)}, u32[]{:S(2)}) collective-permute-start(bf16[2,96,1536]{2,1,0:T(8,128)(2,1)S(1)} %collective-permute-done), channel_id=1, source_target_pairs={{0,1},{1,0},{2,3},{3,2},{4,5},{5,4},{6,7},{7,6},{8,9},{9,8},{10,11... | collective-permute-start | bytes 1769480 | tf_op jit(solution)/shard_map/ppermute | solution.py:32
  178.6 39.4 %collective-permute-start.12 = (bf16[384,640]{1,0:T(8,128)(2,1)S(1)}, bf16[384,640]{1,0:T(8,128)(2,1)S(1)}, u32[]{:S(2)}, u32[]{:S(2)}) collective-permute-start(bf16[384,640]{1,0:T(8,128)(2,1)S(1)} %get-tuple-element.108), channel_id=1, source_target_pairs={{4,0},{8,4},{12,8},{0,12},{5,1},{9,5},{13,9},{1,13},{6,2},{10,6},{... | collective-permute-start | bytes 1474568 | tf_op jit(solution)/shard_map/ppermute | solution.py:24
  183.1 54.7 %collective-permute-start.11 = (bf16[384,640]{1,0:T(8,128)(2,1)S(1)}, bf16[384,640]{1,0:T(8,128)(2,1)S(1)}, u32[]{:S(2)}, u32[]{:S(2)}) collective-permute-start(bf16[384,640]{1,0:T(8,128)(2,1)S(1)} %get-tuple-element.109), channel_id=1, source_target_pairs={{8,0},{12,4},{0,8},{4,12},{9,1},{13,5},{1,9},{5,13},{10,2},{14,6},... | collective-permute-start | bytes 1474568 | tf_op jit(solution)/shard_map/ppermute | solution.py:24
  183.1 88.5 %collective-permute-start.10 = (bf16[384,640]{1,0:T(8,128)(2,1)S(1)}, bf16[384,640]{1,0:T(8,128)(2,1)S(1)}, u32[]{:S(2)}, u32[]{:S(2)}) collective-permute-start(bf16[384,640]{1,0:T(8,128)(2,1)S(1)} %get-tuple-element.110), channel_id=1, source_target_pairs={{12,0},{0,4},{4,8},{8,12},{13,1},{1,5},{5,9},{9,13},{14,2},{2,6},{... | collective-permute-start | bytes 1474568 | tf_op jit(solution)/shard_map/ppermute | solution.py:24
  184.9 147.3 %collective-permute-start.33 = (bf16[192,1152]{1,0:T(8,128)(2,1)S(1)}, bf16[192,1152]{1,0:T(8,128)(2,1)}, u32[]{:S(2)}, u32[]{:S(2)}) collective-permute-start(bf16[192,1152]{1,0:T(8,128)(2,1)S(1)} %copy-done.54), channel_id=1, source_target_pairs={{8,0},{12,4},{0,8},{4,12},{9,1},{13,5},{1,9},{5,13},{10,2},{14,6},... | collective-permute-start | bytes 1327112 | tf_op jit(solution)/shard_map/ppermute | solution.py:24
  186.1 146.7 %collective-permute-start.31 = (bf16[192,1152]{1,0:T(8,128)(2,1)S(1)}, bf16[192,1152]{1,0:T(8,128)(2,1)}, u32[]{:S(2)}, u32[]{:S(2)}) collective-permute-start(bf16[192,1152]{1,0:T(8,128)(2,1)S(1)} %copy-done.54), channel_id=1, source_target_pairs={{12,0},{0,4},{4,8},{8,12},{13,1},{1,5},{5,9},{9,13},{14,2},{2,6},{... | collective-permute-start | bytes 1327112 | tf_op jit(solution)/shard_map/ppermute | solution.py:24
  218.0 84.4 %collective-permute-start.22 = (bf16[192,768]{1,0:T(8,128)(2,1)}, bf16[192,768]{1,0:T(8,128)(2,1)S(1)}, u32[]{:S(2)}, u32[]{:S(2)}) collective-permute-start(bf16[192,768]{1,0:T(8,128)(2,1)} %collective-permute-done.21), channel_id=1, source_target_pairs={{16,0},{0,16},{17,1},{1,17},{18,2},{2,18},{19,3},{3,19},{20,4},{4,... | collective-permute-start | bytes 884744 | tf_op jit(solution)/shard_map/ppermute | solution.py:28
  289.9 22.5 %collective-permute-start.15 = (bf16[384,192]{1,0:T(8,128)(2,1)S(1)}, bf16[384,192]{1,0:T(8,128)(2,1)S(1)}, u32[]{:S(2)}, u32[]{:S(2)}) collective-permute-start(bf16[384,192]{1,0:T(8,128)(2,1)S(1)} %get-tuple-element.142), channel_id=1, source_target_pairs={{12,0},{0,4},{4,8},{8,12},{13,1},{1,5},{5,9},{9,13},{14,2},{2,6},{... | collective-permute-start | bytes 442376 | tf_op jit(solution)/shard_map/ppermute | solution.py:24
  298.1 21.1 %collective-permute-start.14 = (bf16[384,192]{1,0:T(8,128)(2,1)S(1)}, bf16[384,192]{1,0:T(8,128)(2,1)S(1)}, u32[]{:S(2)}, u32[]{:S(2)}) collective-permute-start(bf16[384,192]{1,0:T(8,128)(2,1)S(1)} %get-tuple-element.143), channel_id=1, source_target_pairs={{8,0},{12,4},{0,8},{4,12},{9,1},{13,5},{1,9},{5,13},{10,2},{14,6},... | collective-permute-start | bytes 442376 | tf_op jit(solution)/shard_map/ppermute | solution.py:24
  302.3 18.2 %collective-permute-start.13 = (bf16[384,192]{1,0:T(8,128)(2,1)S(1)}, bf16[384,192]{1,0:T(8,128)(2,1)S(1)}, u32[]{:S(2)}, u32[]{:S(2)}) collective-permute-start(bf16[384,192]{1,0:T(8,128)(2,1)S(1)} %get-tuple-element.144), channel_id=1, source_target_pairs={{4,0},{8,4},{12,8},{0,12},{5,1},{9,5},{13,9},{1,13},{6,2},{10,6},{... | collective-permute-start | bytes 442376 | tf_op jit(solution)/shard_map/ppermute | solution.py:24
  312.3 22.0 %collective-permute-start.29 = (bf16[192,1152]{1,0:T(8,128)(2,1)S(1)}, bf16[192,1152]{1,0:T(8,128)(2,1)}, u32[]{:S(2)}, u32[]{:S(2)}) collective-permute-start(bf16[192,1152]{1,0:T(8,128)(2,1)S(1)} %copy-done.54), channel_id=1, source_target_pairs={{4,0},{8,4},{12,8},{0,12},{5,1},{9,5},{13,9},{1,13},{6,2},{10,6},{... | collective-permute-start | bytes 1327112 | tf_op jit(solution)/shard_map/ppermute | solution.py:24
  332.2 50.3 %collective-permute-start.34 = (bf16[192,1152]{1,0:T(8,128)(2,1)}, bf16[192,1152]{1,0:T(8,128)(2,1)S(1)}, u32[]{:S(2)}, u32[]{:S(2)}) collective-permute-start(bf16[192,1152]{1,0:T(8,128)(2,1)} %collective-permute-done.33), channel_id=1, source_target_pairs={{16,0},{0,16},{17,1},{1,17},{18,2},{2,18},{19,3},{3,19},{20,4},{4,... | collective-permute-start | bytes 1327112 | tf_op jit(solution)/shard_map/ppermute | solution.py:28
  332.9 36.0 %collective-permute-start.32 = (bf16[192,1152]{1,0:T(8,128)(2,1)}, bf16[192,1152]{1,0:T(8,128)(2,1)S(1)}, u32[]{:S(2)}, u32[]{:S(2)}) collective-permute-start(bf16[192,1152]{1,0:T(8,128)(2,1)} %collective-permute-done.31), channel_id=1, source_target_pairs={{16,0},{0,16},{17,1},{1,17},{18,2},{2,18},{19,3},{3,19},{20,4},{4,... | collective-permute-start | bytes 1327112 | tf_op jit(solution)/shard_map/ppermute | solution.py:28
  334.3 29.7 %collective-permute-start.30 = (bf16[192,1152]{1,0:T(8,128)(2,1)}, bf16[192,1152]{1,0:T(8,128)(2,1)S(1)}, u32[]{:S(2)}, u32[]{:S(2)}) collective-permute-start(bf16[192,1152]{1,0:T(8,128)(2,1)} %collective-permute-done.29), channel_id=1, source_target_pairs={{16,0},{0,16},{17,1},{1,17},{18,2},{2,18},{19,3},{3,19},{20,4},{4,... | collective-permute-start | bytes 1327112 | tf_op jit(solution)/shard_map/ppermute | solution.py:28
  340.9 25.8 %collective-permute-start.24 = (bf16[2,96,1536]{2,1,0:T(8,128)(2,1)S(1)}, bf16[2,96,1536]{2,1,0:T(8,128)(2,1)S(1)}, u32[]{:S(2)}, u32[]{:S(2)}) collective-permute-start(bf16[2,96,1536]{2,1,0:T(8,128)(2,1)S(1)} %slice.480), channel_id=1, source_target_pairs={{0,2},{1,3},{2,0},{3,1},{4,6},{5,7},{6,4},{7,5},{8,10},{9,11},{10,... | collective-permute-start | bytes 1769480 | tf_op jit(solution)/shard_map/ppermute | solution.py:32
  401.2 16.5 %collective-permute-start.36 = (bf16[2,96,1536]{2,1,0:T(8,128)(2,1)}, bf16[2,96,1536]{2,1,0:T(8,128)(2,1)}, u32[]{:S(2)}, u32[]{:S(2)}) collective-permute-start(bf16[2,96,1536]{2,1,0:T(8,128)(2,1)} %slice.479), channel_id=1, source_target_pairs={{0,2},{1,3},{2,0},{3,1},{4,6},{5,7},{6,4},{7,5},{8,10},{9,11},{10,... | collective-permute-start | bytes 1769480 | tf_op jit(solution)/shard_map/ppermute | solution.py:32
  403.4 27.0 %collective-permute-start.42 = (bf16[2,96,1536]{2,1,0:T(8,128)(2,1)}, bf16[2,96,1536]{2,1,0:T(8,128)(2,1)}, u32[]{:S(2)}, u32[]{:S(2)}) collective-permute-start(bf16[2,96,1536]{2,1,0:T(8,128)(2,1)} %bitcast.373), channel_id=1, source_target_pairs={{0,2},{1,3},{2,0},{3,1},{4,6},{5,7},{6,4},{7,5},{8,10},{9,11},{10,... | collective-permute-start | bytes 1769480 | tf_op jit(solution)/shard_map/ppermute | solution.py:32
  421.1 21.2 %collective-permute-start.37 = (bf16[2,96,1536]{2,1,0:T(8,128)(2,1)S(1)}, bf16[2,96,1536]{2,1,0:T(8,128)(2,1)S(1)}, u32[]{:S(2)}, u32[]{:S(2)}) collective-permute-start(bf16[2,96,1536]{2,1,0:T(8,128)(2,1)S(1)} %add_convert_fusion), channel_id=1, source_target_pairs={{0,2},{1,3},{2,0},{3,1},{4,6},{5,7},{6,4},{7,5},{8,10},{9,11},{10,... | collective-permute-start | bytes 1769480 | tf_op jit(solution)/shard_map/ppermute | solution.py:32
  422.4 19.9 %collective-permute-start.43 = (bf16[2,96,1536]{2,1,0:T(8,128)(2,1)}, bf16[2,96,1536]{2,1,0:T(8,128)(2,1)S(1)}, u32[]{:S(2)}, u32[]{:S(2)}) collective-permute-start(bf16[2,96,1536]{2,1,0:T(8,128)(2,1)} %bitcast.373), channel_id=1, source_target_pairs={{0,1},{1,0},{2,3},{3,2},{4,5},{5,4},{6,7},{7,6},{8,9},{9,8},{10,11... | collective-permute-start | bytes 1769480 | tf_op jit(solution)/shard_map/ppermute | solution.py:32
  462.0 404.3 %reduce-scatter.3.cloned.1.call-start = ((), (), s32[]{:S(2)}) async-start(), calls=%async_computation.4 | async-start | bytes 5308416 | tf_op jit(solution)/shard_map/reduce_scatter | solution.py:478
  482.9 15.9 %collective-permute-start.46 = (bf16[2,96,1536]{2,1,0:T(8,128)(2,1)}, bf16[2,96,1536]{2,1,0:T(8,128)(2,1)}, u32[]{:S(2)}, u32[]{:S(2)}) collective-permute-start(bf16[2,96,1536]{2,1,0:T(8,128)(2,1)} %slice.477), channel_id=1, source_target_pairs={{0,2},{1,3},{2,0},{3,1},{4,6},{5,7},{6,4},{7,5},{8,10},{9,11},{10,... | collective-permute-start | bytes 1769480 | tf_op jit(solution)/shard_map/ppermute | solution.py:32
  513.3 22.8 %collective-permute-start.40 = (bf16[2,192,1536]{2,1,0:T(8,128)(2,1)}, bf16[2,192,1536]{2,1,0:T(8,128)(2,1)}, u32[]{:S(2)}, u32[]{:S(2)}) collective-permute-start(bf16[2,192,1536]{2,1,0:T(8,128)(2,1)} %slice.472), channel_id=1, source_target_pairs={{0,1},{1,0},{2,3},{3,2},{4,5},{5,4},{6,7},{7,6},{8,9},{9,8},{10,11... | collective-permute-start | bytes 3538952 | tf_op jit(solution)/shard_map/ppermute | solution.py:32
  539.7 28.6 %collective-permute-start.41 = (bf16[2,96,1536]{2,1,0:T(8,128)(2,1)}, bf16[2,96,1536]{2,1,0:T(8,128)(2,1)}, u32[]{:S(2)}, u32[]{:S(2)}) collective-permute-start(bf16[2,96,1536]{2,1,0:T(8,128)(2,1)} %slice.478), channel_id=1, source_target_pairs={{0,2},{1,3},{2,0},{3,1},{4,6},{5,7},{6,4},{7,5},{8,10},{9,11},{10,... | collective-permute-start | bytes 1769480 | tf_op jit(solution)/shard_map/ppermute | solution.py:32
  542.3 21.5 %collective-permute-start.63 = (f32[128,768]{1,0:T(8,128)S(1)}, f32[128,768]{1,0:T(8,128)S(1)}, u32[]{:S(2)}, u32[]{:S(2)}) collective-permute-start(f32[128,768]{1,0:T(8,128)S(1)} %bitcast.418), channel_id=1, source_target_pairs={{0,4},{4,0},{8,12},{12,8},{1,5},{5,1},{9,13},{13,9},{2,6},{6,2},{1... | collective-permute-start | bytes 1179656 | tf_op jit(solution)/shard_map/ppermute | solution.py:540
  545.4 27.5 %collective-permute-start.75 = (bf16[4,192,384]{2,1,0:T(8,128)(2,1)}, bf16[4,192,384]{2,1,0:T(8,128)(2,1)}, u32[]{:S(2)}, u32[]{:S(2)}) collective-permute-start(bf16[4,192,384]{2,1,0:T(8,128)(2,1)} %fusion.55), channel_id=1, source_target_pairs={{16,0},{0,16},{17,1},{1,17},{18,2},{2,18},{19,3},{3,19},{20,4},{4,... | collective-permute-start | bytes 1769480 | tf_op jit(solution)/shard_map/ppermute | solution.py:28
  555.4 23.2 %collective-permute-start.80 = (bf16[4,192,384]{2,1,0:T(8,128)(2,1)S(1)}, bf16[4,192,384]{2,1,0:T(8,128)(2,1)S(1)}, u32[]{:S(2)}, u32[]{:S(2)}) collective-permute-start(bf16[4,192,384]{2,1,0:T(8,128)(2,1)S(1)} %fusion.56), channel_id=1, source_target_pairs={{16,0},{0,16},{17,1},{1,17},{18,2},{2,18},{19,3},{3,19},{20,4},{4,... | collective-permute-start | bytes 1769480 | tf_op jit(solution)/shard_map/ppermute | solution.py:28
  563.8 33.3 %collective-permute-start.64 = (f32[128,768]{1,0:T(8,128)S(1)}, f32[128,768]{1,0:T(8,128)S(1)}, u32[]{:S(2)}, u32[]{:S(2)}) collective-permute-start(f32[128,768]{1,0:T(8,128)S(1)} %bitcast_add_fusion.11), channel_id=1, source_target_pairs={{0,8},{4,12},{8,0},{12,4},{1,9},{5,13},{9,1},{13,5},{2,10},{6,14},... | collective-permute-start | bytes 1179656 | tf_op jit(solution)/shard_map/ppermute | solution.py:540
  575.0 103.2 %collective-permute-start.76 = (bf16[192,384]{1,0:T(8,128)(2,1)}, bf16[192,384]{1,0:T(8,128)(2,1)S(1)}, u32[]{:S(2)}, u32[]{:S(2)}) collective-permute-start(bf16[192,384]{1,0:T(8,128)(2,1)} %get-tuple-element.116), channel_id=1, source_target_pairs={{12,0},{0,4},{4,8},{8,12},{13,1},{1,5},{5,9},{9,13},{14,2},{2,6},{... | collective-permute-start | bytes 442376 | tf_op jit(solution)/shard_map/ppermute | solution.py:24
  577.9 102.9 %collective-permute-start.78 = (bf16[192,384]{1,0:T(8,128)(2,1)}, bf16[192,384]{1,0:T(8,128)(2,1)}, u32[]{:S(2)}, u32[]{:S(2)}) collective-permute-start(bf16[192,384]{1,0:T(8,128)(2,1)} %get-tuple-element.117), channel_id=1, source_target_pairs={{8,0},{12,4},{0,8},{4,12},{9,1},{13,5},{1,9},{5,13},{10,2},{14,6},... | collective-permute-start | bytes 442376 | tf_op jit(solution)/shard_map/ppermute | solution.py:24
  579.6 20.6 %collective-permute-start.53 = (bf16[2,96,1536]{2,1,0:T(8,128)(2,1)S(1)}, bf16[2,96,1536]{2,1,0:T(8,128)(2,1)S(1)}, u32[]{:S(2)}, u32[]{:S(2)}) collective-permute-start(bf16[2,96,1536]{2,1,0:T(8,128)(2,1)S(1)} %get-tuple-element.85), channel_id=1, source_target_pairs={{0,1},{1,0},{2,3},{3,2},{4,5},{5,4},{6,7},{7,6},{8,9},{9,8},{10,11... | collective-permute-start | bytes 1769480 | tf_op jit(solution)/shard_map/ppermute | solution.py:32
  605.3 33.1 %collective-permute-start.57 = (bf16[384,192]{1,0:T(8,128)(2,1)}, bf16[384,192]{1,0:T(8,128)(2,1)S(1)}, u32[]{:S(2)}, u32[]{:S(2)}) collective-permute-start(bf16[384,192]{1,0:T(8,128)(2,1)} %get-tuple-element.134), channel_id=1, source_target_pairs={{4,0},{8,4},{12,8},{0,12},{5,1},{9,5},{13,9},{1,13},{6,2},{10,6},{... | collective-permute-start | bytes 442376 | tf_op jit(solution)/shard_map/ppermute | solution.py:24
  617.9 22.3 %collective-permute-start.56 = (bf16[384,192]{1,0:T(8,128)(2,1)}, bf16[384,192]{1,0:T(8,128)(2,1)}, u32[]{:S(2)}, u32[]{:S(2)}) collective-permute-start(bf16[384,192]{1,0:T(8,128)(2,1)} %get-tuple-element.135), channel_id=1, source_target_pairs={{8,0},{12,4},{0,8},{4,12},{9,1},{13,5},{1,9},{5,13},{10,2},{14,6},... | collective-permute-start | bytes 442376 | tf_op jit(solution)/shard_map/ppermute | solution.py:24
  617.9 33.2 %collective-permute-start.55 = (bf16[384,192]{1,0:T(8,128)(2,1)}, bf16[384,192]{1,0:T(8,128)(2,1)}, u32[]{:S(2)}, u32[]{:S(2)}) collective-permute-start(bf16[384,192]{1,0:T(8,128)(2,1)} %get-tuple-element.136), channel_id=1, source_target_pairs={{12,0},{0,4},{4,8},{8,12},{13,1},{1,5},{5,9},{9,13},{14,2},{2,6},{... | collective-permute-start | bytes 442376 | tf_op jit(solution)/shard_map/ppermute | solution.py:24
  638.4 43.6 %collective-permute-start.77 = (bf16[192,384]{1,0:T(8,128)(2,1)}, bf16[192,384]{1,0:T(8,128)(2,1)S(1)}, u32[]{:S(2)}, u32[]{:S(2)}) collective-permute-start(bf16[192,384]{1,0:T(8,128)(2,1)} %get-tuple-element.118), channel_id=1, source_target_pairs={{4,0},{8,4},{12,8},{0,12},{5,1},{9,5},{13,9},{1,13},{6,2},{10,6},{... | collective-permute-start | bytes 442376 | tf_op jit(solution)/shard_map/ppermute | solution.py:24
  640.2 43.1 %collective-permute-start.81 = (bf16[192,384]{1,0:T(8,128)(2,1)}, bf16[192,384]{1,0:T(8,128)(2,1)S(1)}, u32[]{:S(2)}, u32[]{:S(2)}) collective-permute-start(bf16[192,384]{1,0:T(8,128)(2,1)} %get-tuple-element.113), channel_id=1, source_target_pairs={{12,0},{0,4},{4,8},{8,12},{13,1},{1,5},{5,9},{9,13},{14,2},{2,6},{... | collective-permute-start | bytes 442376 | tf_op jit(solution)/shard_map/ppermute | solution.py:24
  651.1 32.8 %collective-permute-start.83 = (bf16[192,384]{1,0:T(8,128)(2,1)}, bf16[192,384]{1,0:T(8,128)(2,1)S(1)}, u32[]{:S(2)}, u32[]{:S(2)}) collective-permute-start(bf16[192,384]{1,0:T(8,128)(2,1)} %get-tuple-element.114), channel_id=1, source_target_pairs={{8,0},{12,4},{0,8},{4,12},{9,1},{13,5},{1,9},{5,13},{10,2},{14,6},... | collective-permute-start | bytes 442376 | tf_op jit(solution)/shard_map/ppermute | solution.py:24
  678.2 17.0 %collective-permute-start.82 = (bf16[192,384]{1,0:T(8,128)(2,1)S(1)}, bf16[192,384]{1,0:T(8,128)(2,1)S(1)}, u32[]{:S(2)}, u32[]{:S(2)}) collective-permute-start(bf16[192,384]{1,0:T(8,128)(2,1)S(1)} %copy-done.60), channel_id=1, source_target_pairs={{4,0},{8,4},{12,8},{0,12},{5,1},{9,5},{13,9},{1,13},{6,2},{10,6},{... | collective-permute-start | bytes 442376 | tf_op jit(solution)/shard_map/ppermute | solution.py:24
  680.8 22.7 %collective-permute-start.65 = (f32[128,1536]{1,0:T(8,128)S(1)}, f32[128,1536]{1,0:T(8,128)S(1)}, u32[]{:S(2)}, u32[]{:S(2)}) collective-permute-start(f32[128,1536]{1,0:T(8,128)S(1)} %copy-done.34), channel_id=1, source_target_pairs={{0,1},{1,0},{2,3},{3,2},{4,5},{5,4},{6,7},{7,6},{8,9},{9,8},{10,11... | collective-permute-start | bytes 2359304 | tf_op jit(solution)/shard_map/ppermute | solution.py:32
  682.0 20.4 %collective-permute-start.79 = (bf16[192,768]{1,0:T(8,128)(2,1)S(1)}, bf16[192,768]{1,0:T(8,128)(2,1)S(1)}, u32[]{:S(2)}, u32[]{:S(2)}) collective-permute-start(bf16[192,768]{1,0:T(8,128)(2,1)S(1)} %fusion.67), channel_id=1, source_target_pairs={{16,0},{0,16},{17,1},{1,17},{18,2},{2,18},{19,3},{3,19},{20,4},{4,... | collective-permute-start | bytes 884744 | tf_op jit(solution)/shard_map/ppermute | solution.py:28
  683.3 25.6 %collective-permute-start.60 = (bf16[384,640]{1,0:T(8,128)(2,1)}, bf16[384,640]{1,0:T(8,128)(2,1)}, u32[]{:S(2)}, u32[]{:S(2)}) collective-permute-start(bf16[384,640]{1,0:T(8,128)(2,1)} %get-tuple-element.104), channel_id=1, source_target_pairs={{12,0},{0,4},{4,8},{8,12},{13,1},{1,5},{5,9},{9,13},{14,2},{2,6},{... | collective-permute-start | bytes 1474568 | tf_op jit(solution)/shard_map/ppermute | solution.py:24
  683.8 55.6 %collective-permute-start.59 = (bf16[384,640]{1,0:T(8,128)(2,1)}, bf16[384,640]{1,0:T(8,128)(2,1)}, u32[]{:S(2)}, u32[]{:S(2)}) collective-permute-start(bf16[384,640]{1,0:T(8,128)(2,1)} %get-tuple-element.105), channel_id=1, source_target_pairs={{8,0},{12,4},{0,8},{4,12},{9,1},{13,5},{1,9},{5,13},{10,2},{14,6},... | collective-permute-start | bytes 1474568 | tf_op jit(solution)/shard_map/ppermute | solution.py:24
  695.2 46.5 %collective-permute-start.58 = (bf16[384,640]{1,0:T(8,128)(2,1)}, bf16[384,640]{1,0:T(8,128)(2,1)}, u32[]{:S(2)}, u32[]{:S(2)}) collective-permute-start(bf16[384,640]{1,0:T(8,128)(2,1)} %get-tuple-element.106), channel_id=1, source_target_pairs={{4,0},{8,4},{12,8},{0,12},{5,1},{9,5},{13,9},{1,13},{6,2},{10,6},{... | collective-permute-start | bytes 1474568 | tf_op jit(solution)/shard_map/ppermute | solution.py:24
  704.4 60.2 %collective-permute-start.66 = (f32[128,1536]{1,0:T(8,128)}, f32[128,1536]{1,0:T(8,128)}, u32[]{:S(2)}, u32[]{:S(2)}) collective-permute-start(f32[128,1536]{1,0:T(8,128)} %add.524), channel_id=1, source_target_pairs={{0,2},{1,3},{2,0},{3,1},{4,6},{5,7},{6,4},{7,5},{8,10},{9,11},{10,... | collective-permute-start | bytes 2359304 | tf_op jit(solution)/shard_map/ppermute | solution.py:32
  752.3 16.3 %collective-permute-start.71 = (bf16[4,192,384]{2,1,0:T(8,128)(2,1)S(1)}, bf16[4,192,384]{2,1,0:T(8,128)(2,1)S(1)}, u32[]{:S(2)}, u32[]{:S(2)}) collective-permute-start(bf16[4,192,384]{2,1,0:T(8,128)(2,1)S(1)} %fusion.54), channel_id=1, source_target_pairs={{16,0},{0,16},{17,1},{1,17},{18,2},{2,18},{19,3},{3,19},{20,4},{4,... | collective-permute-start | bytes 1769480 | tf_op jit(solution)/shard_map/ppermute | solution.py:28
  758.8 55.2 %collective-permute-start.67 = (bf16[4,192,1280]{2,1,0:T(8,128)(2,1)}, bf16[4,192,1280]{2,1,0:T(8,128)(2,1)}, u32[]{:S(2)}, u32[]{:S(2)}) collective-permute-start(bf16[4,192,1280]{2,1,0:T(8,128)(2,1)} %fusion.10), channel_id=1, source_target_pairs={{16,0},{0,16},{17,1},{1,17},{18,2},{2,18},{19,3},{3,19},{20,4},{4,... | collective-permute-start | bytes 5898248 | tf_op jit(solution)/shard_map/ppermute | solution.py:28
  790.3 19.8 %collective-permute-start.86 = (f32[4,6,192]{2,0,1:T(4,128)S(1)}, f32[4,6,192]{2,0,1:T(4,128)S(1)}, u32[]{:S(2)}, u32[]{:S(2)}) collective-permute-start(f32[4,6,192]{2,0,1:T(4,128)S(1)} %dynamic-slice_bitcast_fusion.6), channel_id=1, source_target_pairs={{16,0},{0,16},{17,1},{1,17},{18,2},{2,18},{19,3},{3,19},{20,4},{4,... | collective-permute-start | bytes 55304 | tf_op jit(solution)/shard_map/ppermute | solution.py:28
  817.2 33.7 %collective-permute-start.68 = (bf16[192,1280]{1,0:T(8,128)(2,1)S(1)}, bf16[192,1280]{1,0:T(8,128)(2,1)S(1)}, u32[]{:S(2)}, u32[]{:S(2)}) collective-permute-start(bf16[192,1280]{1,0:T(8,128)(2,1)S(1)} %get-tuple-element.92), channel_id=1, source_target_pairs={{12,0},{0,4},{4,8},{8,12},{13,1},{1,5},{5,9},{9,13},{14,2},{2,6},{... | collective-permute-start | bytes 1474568 | tf_op jit(solution)/shard_map/ppermute | solution.py:24
  818.2 41.0 %collective-permute-start.70 = (bf16[192,1280]{1,0:T(8,128)(2,1)S(1)}, bf16[192,1280]{1,0:T(8,128)(2,1)S(1)}, u32[]{:S(2)}, u32[]{:S(2)}) collective-permute-start(bf16[192,1280]{1,0:T(8,128)(2,1)S(1)} %get-tuple-element.93), channel_id=1, source_target_pairs={{8,0},{12,4},{0,8},{4,12},{9,1},{13,5},{1,9},{5,13},{10,2},{14,6},... | collective-permute-start | bytes 1474568 | tf_op jit(solution)/shard_map/ppermute | solution.py:24
  819.7 41.4 %collective-permute-start.69 = (bf16[192,1280]{1,0:T(8,128)(2,1)S(1)}, bf16[192,1280]{1,0:T(8,128)(2,1)S(1)}, u32[]{:S(2)}, u32[]{:S(2)}) collective-permute-start(bf16[192,1280]{1,0:T(8,128)(2,1)S(1)} %get-tuple-element.94), channel_id=1, source_target_pairs={{4,0},{8,4},{12,8},{0,12},{5,1},{9,5},{13,9},{1,13},{6,2},{10,6},{... | collective-permute-start | bytes 1474568 | tf_op jit(solution)/shard_map/ppermute | solution.py:24
  (116 other events, 1257.6 us)
Sparse Core Ops, SparseCore 0:
  10.2 119.3 all-gather.3
  131.7 143.7 all-gather.5
  462.1 105.2 reduce-scatter.4
  570.9 142.0 reduce-scatter.2

commit v2 on v1

--- a/solution.py
+++ b/solution.py
@@ -5,6 +5,7 @@
 from jax import lax
 from jax.experimental import pallas as pl
 from jax.experimental.pallas import tpu as pltpu
+from jax.experimental.layout import Layout, with_layout_constraint
 from jax.sharding import PartitionSpec as P
 
 HEAD = 64
@@ -78,6 +79,14 @@
     return result
 
 
+def pick_columns(values, index, count):
+    span = values.shape[1] // count
+    result = values[:, :span]
+    for place in range(1, count):
+        result = jnp.where(index == place, values[:, place * span : (place + 1) * span], result)
+    return result
+
+
 def pick(values, index):
     return lax.dynamic_index_in_dim(values, index, 0, keepdims=False)
 
@@ -100,14 +109,18 @@
     return order
 
 
-def scatter_rows(parts, tensor_size):
-    mask = 1
+def scatter_rows(parts, tensor_size, first=1):
+    mask = first
     while mask < tensor_size:
-        half = parts.shape[1] // 2
-        arrived = swap_tensor(parts[:, half:].astype(low), mask, tensor_size)
-        parts = parts[:, :half] + arrived.astype(wide)
+        parts = scatter_step(parts, mask, tensor_size)
         mask *= 2
     return parts
+
+
+def scatter_step(parts, mask, tensor_size):
+    half = parts.shape[1] // 2
+    arrived = swap_tensor(parts[:, half:].astype(low), mask, tensor_size)
+    return parts[:, :half] + arrived.astype(wide)
 
 
 def norm_stats(values):
@@ -443,39 +456,113 @@
     columns = self_query.shape[1]
     halves = nc // clips
     width = columns // halves
-    padded = -(-3 * width // 128) * 128
+    padded = 3 * width
     place = jnp.stack([own_context, own_tensor]).astype(jnp.int32)
     group = ((nf, nc), (own_fsdp, own_context))
     both = ("fsdp", "context")
 
-    vectors = lax.all_gather(jnp.stack(parameters[10:16] + parameters[10:12]), both, axis=0)
-    vectors = vectors.transpose(1, 0, 2).reshape(-1, features).astype(wide)
+    def gather_calls(shard):
+        return lax.all_gather(shard, both, axis=0, tiled=True)
+
+    vectors = gather_group(jnp.stack(parameters[10:16] + parameters[10:12]), *group)
+    vectors = vectors.reshape(nf * nc, -1, block).transpose(1, 0, 2).reshape(-1, features)
+    vectors = vectors.astype(wide)
     pieces = []
     for part in range(halves):
         lanes = slice(part * width, (part + 1) * width)
         pieces += [self_query[:, lanes], self_key[:, lanes], self_value[:, lanes]]
-        if padded > 3 * width:
-            pieces.append(jnp.zeros((block, padded - 3 * width), low))
     qkv_all = gather_group(jnp.concatenate(pieces, axis=1), *group)
-    second_all = gather_group(jnp.concatenate([self_out, cross_query], axis=1), *group)
-    third_all = gather_group(jnp.concatenate([cross_key, cross_value, cross_out], axis=1), *group)
-    feed_in_all = lax.all_gather(feed_in, both, axis=0, tiled=True)
-    feed_out_all = lax.all_gather(feed_out, both, axis=0, tiled=True)
-    self_out_all, cross_query_all = second_all[:, :columns], second_all[:, columns:]
-    cross_key_value = third_all[:, : 2 * columns]
-    cross_out_all = third_all[:, 2 * columns :]
+    second_all = gather_calls(jnp.concatenate([cross_query, cross_out], axis=1))
+    third_all = gather_calls(jnp.concatenate([self_out, cross_key, cross_value], axis=1))
+    feed_in_near = lax.all_gather(feed_in, "context", axis=0, tiled=True)
+    feed_out_all = gather_calls(feed_out)
+    self_out_all = third_all[:, :columns]
+    cross_key_value = third_all[:, columns:]
+
+    def gather_columns(blocks, first, last):
+        mask = first
+        while mask >= last:
+            blocks = blocks + [swap_tensor(part, mask, nt) for part in blocks]
+            mask //= 2
+        return blocks
+
+    def side_by_side(blocks):
+        return [
+            jnp.concatenate([part[:, side * columns : (side + 1) * columns] for part in blocks], axis=1)
+            for side in range(2)
+        ]
+
+    def scatter_columns(parts, mask=1):
+        while mask < nt:
+            half = parts.shape[-1] // 2
+            arrived = swap_tensor(parts[..., half:].astype(low), mask, nt)
+            parts = parts[..., :half] + arrived.astype(wide)
+            mask *= 2
+        return parts
+
+    def row_major(values):
+        return with_layout_constraint(values, Layout(major_to_minor=(0, 1)))
+
+    def outer_start(*products):
+        half = products[0][1].shape[1] // 2
+        far = [row_major(dot(left, right[:, half:], 0, 0)).astype(low) for left, right in products]
+        near = [row_major(dot(left, right[:, :half], 0, 0)) for left, right in products]
+        return near + [swap_tensor(jnp.concatenate(far, axis=1), 1, nt)]
+
+    def outer_step(near, arrived):
+        span = near[0].shape[1]
+        return [
+            part + arrived[:, k * span : (k + 1) * span].astype(wide) for k, part in enumerate(near)
+        ]
+
+    def outer_rest(near, arrived):
+        near = outer_step(near, arrived)
+        mask = 2
+        while mask < nt:
+            half = near[0].shape[1] // 2
+            far = jnp.concatenate([part[:, half:].astype(low) for part in near], axis=1)
+            far = swap_tensor(far, mask, nt)
+            near = [part[:, :half] for part in near]
+            mask *= 2
+            if mask < nt:
+                near = outer_step(near, far)
+        return near + [far]
+
 
     residual = frames.transpose(1, 0, 2).astype(wide)
     incoming = cotangent.transpose(1, 0, 2)
     text = text_states.transpose(1, 0, 2)
 
-    def weight_grad(left_rows, right_rows):
-        parts = dot(left_rows, right_rows, 0, 0).reshape(nf * nc, block, -1)
-        return reduce_group(parts, *group)
-
-    def feed_grad(left_rows, right_rows):
-        parts = dot(left_rows, right_rows, 0, 0).astype(low)
-        return lax.psum_scatter(parts, both, scatter_dimension=0, tiled=True).astype(wide)
+    def after(*values):
+        return lax.optimization_barrier(values)
+
+    def grad_start(*products):
+        def block_of(index):
+            parts = [
+                with_layout_constraint(
+                    dot(pick_columns(left, index, nf), right, 0, 0), Layout(major_to_minor=(0, 1))
+                )
+                for left, right in products
+            ]
+            return parts[0] if len(parts) == 1 else jnp.concatenate(parts, axis=1)
+
+        far = [
+            from_fsdp(block_of(lax.rem(own_fsdp + step, nf)).astype(low), nf - step, nf)
+            for step in range(1, nf)
+        ]
+        return [block_of(own_fsdp)] + far
+
+    def block_sum(blocks):
+        total = blocks[0]
+        for piece in blocks[1:]:
+            total = total + piece.astype(wide)
+        return total
+
+    def grad_scatter(total):
+        return lax.psum_scatter(total, "context", scatter_dimension=0, tiled=True)
+
+    def grad_finish(blocks):
+        return grad_scatter(block_sum(blocks).astype(low))
 
     def by_row(values):
         return values.reshape(-1, values.shape[-1])
@@ -492,20 +579,38 @@
         return jnp.concatenate([chunks[:, j] for j in range(halves)], axis=-1)
 
     normed_one = by_row(gather_rows(layer_norm(residual, vectors[0], vectors[1]), nt))
+    normed_one, second_all = after(normed_one, second_all)
+    second_blocks = gather_columns([second_all], nt // 2, 2)
     projected = by_clip(dot(normed_one, qkv_all, 1, 0).astype(low))
     head_rows = to_heads(to_chunks(projected, padded), own_context, nc)
+    head_rows, *second_blocks = after(head_rows, *second_blocks)
     head_out, head_top = self_forward(place, head_rows, width, frame_count, order)
+    head_out, cross_key_value, *second_blocks = after(head_out, cross_key_value, *second_blocks)
+    cross_query_all, cross_out_all = side_by_side(gather_columns(second_blocks, 1, 1))
     attended = by_row(from_chunks(to_frames(head_out, own_context, nc)))
+    text_projected = dot(by_row(text), cross_key_value, 1, 0).astype(low)
+    cross_keys, cross_values = [
+        by_clip(part) for part in side_by_side(gather_columns([text_projected], nt // 2, 1))
+    ]
+    attended, cross_keys, cross_values, feed_in_near = after(
+        attended, cross_keys, cross_values, feed_in_near
+    )
+    feed_in_pieces = [feed_in_near] + [from_fsdp(feed_in_near, far, nf) for far in range(1, nf)]
     after_self = residual + scatter_rows(by_clip(dot(attended, self_out_all, 1, 1)), nt)
 
-    normed_two = by_row(gather_rows(layer_norm(after_self, vectors[2], vectors[3]), nt))
+    normed_two = by_row(layer_norm(after_self, vectors[2], vectors[3]))
     cross_queries = by_clip(dot(normed_two, cross_query_all, 1, 0).astype(low))
-    text_projected = by_clip(dot(by_row(text), cross_key_value, 1, 0).astype(low))
-    cross_keys, cross_values = text_projected[..., :columns], text_projected[..., columns:]
     crossed = cross_forward(cross_queries, cross_keys, cross_values)
-    after_cross = after_self + scatter_rows(by_clip(dot(by_row(crossed), cross_out_all, 1, 1)), nt)
+    after_cross = after_self + by_clip(dot(by_row(crossed), cross_out_all, 1, 1))
 
     normed_three = by_row(gather_rows(layer_norm(after_cross, vectors[4], vectors[5]), nt))
+    normed_three, *feed_in_pieces = after(normed_three, *feed_in_pieces)
+    feed_in_all = jnp.zeros((nf,) + feed_in_near.shape, low)
+    for far, piece in enumerate(feed_in_pieces):
+        feed_in_all = lax.dynamic_update_index_in_dim(
+            feed_in_all, piece, lax.rem(own_fsdp + far, nf), 0
+        )
+    feed_in_all = feed_in_all.reshape(features, -1)
     hidden = dot(normed_three, feed_in_all, 1, 0)
     gate = 0.5 + 0.5 * lax.erf(hidden * (0.5**0.5))
     active = (hidden * gate).astype(low)
@@ -514,54 +619,107 @@
 
     grad_rows = by_row(gather_rows(incoming, nt))
     grad_active = dot(grad_rows, feed_out_all, 1, 0)
-    feed_out_grad = feed_grad(grad_rows, active)
+    feed_out_blocks = grad_start((grad_rows, active))
     slope = gate + hidden * jnp.exp(-0.5 * hidden * hidden) * ((2.0 * jnp.pi) ** -0.5)
     grad_hidden = (grad_active * slope).astype(low)
-    feed_in_grad = feed_grad(normed_three, grad_hidden)
     grad_normed = scatter_rows(by_clip(dot(grad_hidden, feed_in_all, 1, 1)), nt)
     piece, third_gain, third_shift = norm_back(after_cross, vectors[4], grad_normed)
     grad_after_cross = incoming.astype(wide) + piece
 
-    grad_rows = by_row(gather_rows(grad_after_cross.astype(low), nt))
-    grad_crossed = by_clip(dot(grad_rows, cross_out_all, 1, 0).astype(low))
-    cross_out_grad = weight_grad(grad_rows, by_row(crossed))
+    cross_rows = by_row(grad_after_cross.astype(low))
+    grad_crossed = by_clip(dot(cross_rows, cross_out_all, 1, 0).astype(low))
     grad_cross_queries, grad_cross_keys, grad_cross_values = cross_backward(
         cross_queries, cross_keys, cross_values, grad_crossed
     )
     grad_cross_queries = by_row(grad_cross_queries)
-    cross_query_grad = weight_grad(normed_two, grad_cross_queries)
-    grad_normed = scatter_rows(by_clip(dot(grad_cross_queries, cross_query_all, 1, 1)), nt)
+    grad_normed = by_clip(dot(grad_cross_queries, cross_query_all, 1, 1))
     piece, second_gain, second_shift = norm_back(after_self, vectors[2], grad_normed)
     grad_after_self = grad_after_cross + piece
-
-    text_grads = by_row(jnp.concatenate([grad_cross_keys, grad_cross_values], axis=-1))
+    grad_after_self, normed_three, grad_hidden = after(grad_after_self, normed_three, grad_hidden)
+    feed_in_blocks = grad_start((normed_three, grad_hidden))
+    cross_parts = outer_start((cross_rows, by_row(crossed)), (normed_two, grad_cross_queries))
+
+    def text_sum(values, mask):
+        arrived = lax.ppermute(values.astype(low), "context", [(i, i ^ mask) for i in range(nc)])
+        return values + arrived.astype(wide)
+
+    text_grads = scatter_columns(jnp.stack([by_row(grad_cross_keys), by_row(grad_cross_values)]))
+    text_grads = jnp.concatenate([text_grads[0], text_grads[1]], axis=1)
     mask = 1
-    while mask < nc:
-        text_grads = text_grads + lax.ppermute(
-            text_grads, "context", [(i, i ^ mask) for i in range(nc)]
-        )
+    while 2 * mask < nc:
+        text_grads = text_sum(text_grads, mask)
         mask *= 2
+    grad_rows = by_row(gather_rows(grad_after_self.astype(low), nt))
+    grad_rows, text_grads, *feed_out_blocks = after(grad_rows, text_grads, *feed_out_blocks)
+    feed_out_grad = grad_finish(feed_out_blocks)
+    text_grads = text_sum(text_grads, mask)
+
+    grad_attended = by_clip(dot(grad_rows, self_out_all, 1, 0).astype(low))
+    grad_attended, *cross_parts = after(grad_attended, *cross_parts)
+    cross_parts = outer_rest(cross_parts[:2], cross_parts[2])
+    self_out_blocks = grad_start((grad_rows, attended))
+    head_grad = to_heads(to_chunks(grad_attended, width), own_context, nc)
+    head_grad, text_grads, feed_out_grad, *feed_in_blocks = after(
+        head_grad, text_grads, feed_out_grad, *feed_in_blocks
+    )
+    feed_in_grad = grad_finish(feed_in_blocks)
+    feed_out_grad = feed_out_grad.astype(wide)
+    head_back = self_backward(place, head_rows, head_out, head_top, head_grad, frame_count, order)
+    head_back, *cross_parts = after(head_back, *cross_parts)
+    cross_parts = outer_step(cross_parts[:2], cross_parts[2])
+
+    def cross_block(index):
+        span = nc * block
+        picked = []
+        for part in cross_parts:
+            chosen = part[:span]
+            for where in range(1, nf):
+                chosen = jnp.where(index == where, part[where * span : (where + 1) * span], chosen)
+            picked.append(chosen)
+        return jnp.concatenate(picked, axis=1)
+
+    cross_blocks = [cross_block(own_fsdp)] + [
+        from_fsdp(cross_block(lax.rem(own_fsdp + step, nf)).astype(low), nf - step, nf)
+        for step in range(1, nf)
+    ]
     text_low = text_grads.astype(low)
-    text_parts = dot(by_row(text), text_low, 0, 0).reshape(nf, nc, block, 2 * columns)
-    key_value_grad = pick(pick(text_parts, own_fsdp), own_context)
-    for step in range(1, nf):
-        part = pick(pick(text_parts, lax.rem(own_fsdp + step, nf)), own_context).astype(low)
-        key_value_grad = key_value_grad + from_fsdp(part, nf - step, nf).astype(wide)
+    def text_block(step):
+        place = lax.rem(own_fsdp + step, nf) * nc + own_context
+        return dot(pick_columns(by_row(text), place, nf * nc), text_low, 0, 0)
+
+    text_blocks = [text_block(0)] + [
+        from_fsdp(text_block(step).astype(low), nf - step, nf) for step in range(1, nf)
+    ]
     text_part = dot(text_low, cross_key_value, 1, 1)
     mask = 1
     while mask < nt:
-        text_part = text_part + swap_tensor(text_part, mask, nt)
+        text_part = text_part + swap_tensor(text_part.astype(low), mask, nt).astype(wide)
         mask *= 2
+
+    grad_projected = by_row(from_chunks(to_frames(head_back, own_context, nc)))
+    count = len(cross_blocks)
+    grad_projected, feed_in_grad, text_part, *moved = after(
+        grad_projected, feed_in_grad, text_part, *cross_blocks, *self_out_blocks, *text_blocks
+    )
+    middle_total = [block_sum(moved[:count]).astype(low), block_sum(moved[count : 2 * count]).astype(low)]
+    middle_grad = grad_scatter(jnp.concatenate(middle_total, axis=1))
+    text_blocks = moved[2 * count :]
+    key_value_grad = block_sum(text_blocks)
     text_grad = by_clip(text_part).transpose(1, 0, 2)
-
-    grad_rows = by_row(gather_rows(grad_after_self.astype(low), nt))
-    grad_attended = by_clip(dot(grad_rows, self_out_all, 1, 0).astype(low))
-    self_out_grad = weight_grad(grad_rows, attended)
-    head_grad = to_heads(to_chunks(grad_attended, width), own_context, nc)
-    head_back = self_backward(place, head_rows, head_out, head_top, head_grad, frame_count, order)
-    grad_projected = by_row(from_chunks(to_frames(head_back, own_context, nc)))
-    qkv_grad = weight_grad(normed_one, grad_projected)
-    grad_normed = scatter_rows(by_clip(dot(grad_projected, qkv_all, 1, 1)), nt)
+    feed_in_grad = feed_in_grad.astype(wide)
+    cut = grad_projected.shape[1] // 256 * 128 + 128
+    early = grad_start((normed_one, grad_projected[:, :cut]))
+    late = grad_start((normed_one, grad_projected[:, cut:]))
+    grad_normed = scatter_step(by_clip(dot(grad_projected, qkv_all, 1, 1)), 1, nt)
+    grad_normed, middle_grad, *early = after(grad_normed, middle_grad, *early)
+    early = grad_finish(early)
+    grad_normed = scatter_rows(grad_normed, nt, 2)
+    grad_normed, *late = after(grad_normed, *late)
+    qkv_grad = jnp.concatenate([early.astype(wide), grad_finish(late).astype(wide)], axis=1)
+    middle_grad = middle_grad.astype(wide)
+    cross_out_grad = middle_grad[:, :columns]
+    cross_query_grad = middle_grad[:, columns : 2 * columns]
+    self_out_grad = middle_grad[:, 2 * columns :]
     piece, first_gain, first_shift = norm_back(residual, vectors[0], grad_normed)
     frames_grad = (grad_after_self + piece).transpose(1, 0, 2)
 

time: 886 us -> 759 us (0.86)
  blocking collectives: 60.6 us -> 0 us
  starting transfers between devices: 122 us -> 77.5 us
  local copies, waits for them, and re-layouts: 110 us -> 67.7 us
  waiting for transfers between devices: 388 us -> 353 us
  other arithmetic: 53.2 us -> 75.6 us
  matrix products: 76 us -> 93.4 us
  Pallas kernels: 49.8 us -> 63.3 us
    all_gather x1 -> x0, blocking collectives: 60.6 us -> none  [on_device(): lax.all_gather(jnp.stack(parameters[10:16] + parameters[10:12]), both, ax...]
    ppermute x36 -> x21, waiting for transfers between devices: 231 us -> 185 us  [from_context(): lax.ppermute(values, 'context', [((i + step) % size, i) for i in range(si...]
    ppermute x36 -> x21, starting transfers between devices: 78.2 us -> 36.7 us  [from_context(): lax.ppermute(values, 'context', [((i + step) % size, i) for i in range(si...]
    dot_general x5 -> x0, local copies, waits for them, and re-layouts: 21.8 us -> none  [dot(): lax.dot_general(left, right, (((left_dim,), (right_dim,)), ((), ())), pre...]
    reduce_scatter x2 -> x5, waiting for transfers between devices: 0.01 us -> 18.2 us  [grad_scatter(): return lax.psum_scatter(total, 'context', scatter_dimension=0, tiled=True)]
    convert_element_type x5 -> x15, other arithmetic: 5.76 us -> 23.4 us  [the longest x4 13.3 us: grad_finish(): return grad_scatter(block_sum(blocks).astype(low))]
    dot_general x21 -> x30, matrix products: 76 us -> 93.4 us  [dot(): lax.dot_general(left, right, (((left_dim,), (right_dim,)), ((), ())), pre...]
    dynamic_update_slice x24 -> x16, local copies, waits for them, and re-layouts: 24.2 us -> 8.7 us  [gather_group(): result = lax.dynamic_update_index_in_dim(result, piece, index, 0)]
  transfers between devices with their start and end apart: 94 -> 83, of which waited for: 39 -> 37; matrix products, arithmetic and copies ran while one was open for 24% -> 26% of each run, Pallas kernels for 6% -> 8%
where the time goes in v2:
time: 759 us; the launch traced here: 747 us
  waiting for transfers between devices  353 us (47%)
  matrix products  93.4 us (12%)
  starting transfers between devices  77.5 us (10%)
  other arithmetic  75.6 us (10%)
  local copies, waits for them, and re-layouts  67.7 us (9%)
  Pallas kernels  63.3 us (8%)
  between operations  15.9 us (2%)
    ppermute x21, waiting for transfers between devices, from_context(): lax.ppermute(values, 'context', [((i + step) % size, i) for i in range(si...  185 us
    dot_general x30, matrix products, dot(): lax.dot_general(left, right, (((left_dim,), (right_dim,)), ((), ())), pre...  93.4 us
    ppermute x34, waiting for transfers between devices, swap_tensor(): return lax.ppermute(values, 'tensor', [(i, i ^ mask) for i in range(size)])  74 us
    ppermute x17, waiting for transfers between devices, from_fsdp(): lax.ppermute(values, 'fsdp', [((i + step) % size, i) for i in range(size)])  52.7 us
    ppermute x21, starting transfers between devices, from_context(): lax.ppermute(values, 'context', [((i + step) % size, i) for i in range(si...  36.7 us
    pallas_call x1, Pallas kernels, self_backward(): pl.pallas_call(functools.partial(self_backward_kernel, frames, order), ou...  24.4 us
    ppermute x34, starting transfers between devices, swap_tensor(): return lax.ppermute(values, 'tensor', [(i, i ^ mask) for i in range(size)])  20.4 us
    unnamed x183, local copies, waits for them, and re-layouts  18.9 us
  transfers between devices with their start and end apart: 83, of which 37 were waited for; matrix products, arithmetic and copies ran while one was open for 26% of the time, Pallas kernels for 8%

profile of v2, /device:TPU:8, one launch (start us, length us, event | category | flops | bytes accessed | tf_op | source)
XLA Modules:
  0.0 746.6 jit_solution(3622056014839012926)
XLA Ops:
  18.7 4.4 collective-permute-start.5
  31.5 3.7 collective-permute-done.2
  35.8 2.4 collective-permute-start.15
  39.7 2.8 collective-permute-done.6
  45.4 17.3 %collective-permute-done.11 = bf16[192,1152]{1,0:T(8,128)(2,1)S(1)} collective-permute-done((bf16[192,1152]{1,0:T(8,128)(2,1)S(1)}, bf16[192,1152]{1,0:T(8,128)(2,1)S(1)}, u32[]{:S(2)}, u32[]{:S(2)}) %collective-permute-start.11) | collective-permute-done | bytes 442400 | tf_op jit(solution)/shard_map/ppermute | solution.py:25
  64.7 23.9 %collective-permute-done.15 = bf16[192,1152]{1,0:T(8,128)(2,1)} collective-permute-done((bf16[192,1152]{1,0:T(8,128)(2,1)S(1)}, bf16[192,1152]{1,0:T(8,128)(2,1)}, u32[]{:S(2)}, u32[]{:S(2)}) %collective-permute-start.15) | collective-permute-done | bytes 442400 | tf_op jit(solution)/shard_map/ppermute | solution.py:25
  97.3 3.4 collective-permute-done.16
  102.6 5.2 convolution_convert_fusion.4
  113.1 2.9 collective-permute-start.17
  117.9 11.2 %collective-permute-done.19 = bf16[384,576]{1,0:T(8,128)(2,1)S(1)} collective-permute-done((bf16[384,576]{1,0:T(8,128)(2,1)}, bf16[384,576]{1,0:T(8,128)(2,1)S(1)}, u32[]{:S(2)}, u32[]{:S(2)}) %collective-permute-start.19) | collective-permute-done | bytes 442400 | tf_op jit(solution)/shard_map/ppermute | solution.py:25
  129.1 20.3 %collective-permute-done.18 = bf16[384,576]{1,0:T(8,128)(2,1)S(1)} collective-permute-done((bf16[384,576]{1,0:T(8,128)(2,1)S(1)}, bf16[384,576]{1,0:T(8,128)(2,1)S(1)}, u32[]{:S(2)}, u32[]{:S(2)}) %collective-permute-start.18) | collective-permute-done | bytes 442400 | tf_op jit(solution)/shard_map/ppermute | solution.py:25
  149.4 31.9 %collective-permute-done.17 = bf16[384,576]{1,0:T(8,128)(2,1)} collective-permute-done((bf16[384,576]{1,0:T(8,128)(2,1)S(1)}, bf16[384,576]{1,0:T(8,128)(2,1)}, u32[]{:S(2)}, u32[]{:S(2)}) %collective-permute-start.17) | collective-permute-done | bytes 442400 | tf_op jit(solution)/shard_map/ppermute | solution.py:25
  183.1 5.4 all-gather.7.cloned.1.call-done
  190.4 18.0 %shard_map.330 = (bf16[4,384,192]{2,1,0:T(8,128)(2,1)S(1)}, f32[4,3,384]{2,1,0:T(4,128)S(1)}) custom-call(s32[2]{0:T(128)S(1)} %pad_add_fusion.place_ref, bf16[4,384,576]{2,1,0:T(8,128)(2,1)S(1)} %pad_maximum_fusion.10.rows_ref), custom_call_target="tpu_custom_call" | custom-call | flops 1132462080 | bytes 3538944 | tf_op jit(solution)/shard_map/pallas_call | solution.py:303
  211.7 4.4 collective-permute-start.22
  216.1 10.4 %collective-permute-done.23 = bf16[384,192]{1,0:T(8,128)(2,1)S(1)} collective-permute-done((bf16[384,192]{1,0:T(8,128)(2,1)S(1)}, bf16[384,192]{1,0:T(8,128)(2,1)S(1)}, u32[]{:S(2)}, u32[]{:S(2)}) %collective-permute-start.23) | collective-permute-done | bytes 147488 | tf_op jit(solution)/shard_map/ppermute | solution.py:25
  226.5 23.4 %collective-permute-done.22 = bf16[384,192]{1,0:T(8,128)(2,1)S(1)} collective-permute-done((bf16[384,192]{1,0:T(8,128)(2,1)S(1)}, bf16[384,192]{1,0:T(8,128)(2,1)S(1)}, u32[]{:S(2)}, u32[]{:S(2)}) %collective-permute-start.22) | collective-permute-done | bytes 147488 | tf_op jit(solution)/shard_map/ppermute | solution.py:25
  249.9 3.2 collective-permute-done.21
  257.5 2.7 fusion.52
  274.3 18.7 %collective-permute-done.28 = bf16[2,96,1536]{2,1,0:T(8,128)(2,1)S(1)} collective-permute-done((bf16[2,96,1536]{2,1,0:T(8,128)(2,1)S(1)}, bf16[2,96,1536]{2,1,0:T(8,128)(2,1)S(1)}, u32[]{:S(2)}, u32[]{:S(2)}) %collective-permute-start.28) | collective-permute-done | bytes 589856 | tf_op jit(solution)/shard_map/ppermute | solution.py:33
  295.2 3.4 convolution_convert_fusion.6
  298.5 10.0 %shard_map.331 = bf16[2,96,1536]{2,1,0:T(8,128)(2,1)S(1)} custom-call(bf16[2,96,1536]{2,1,0:T(8,128)(2,1)S(1)} %bitcast.267, bf16[2,64,1536]{2,1,0:T(8,128)(2,1)S(1)} %bitcast.257, bf16[2,64,1536]{2,1,0:T(8,128)(2,1)S(1)} %bitcast.259), custom_call_target="tpu_custom_call" | custom-call | flops 75497472 | bytes 1179648 | tf_op jit(solution)/shard_map/pallas_call | solution.py:383
  308.6 3.1 fusion.159
  314.8 13.2 %collective-permute-done.31 = bf16[2,96,1536]{2,1,0:T(8,128)(2,1)} collective-permute-done((bf16[2,96,1536]{2,1,0:T(8,128)(2,1)S(1)}, bf16[2,96,1536]{2,1,0:T(8,128)(2,1)}, u32[]{:S(2)}, u32[]{:S(2)}) %collective-permute-start.31) | collective-permute-done | bytes 589856 | tf_op jit(solution)/shard_map/ppermute | solution.py:33
  328.0 3.2 pad_maximum_fusion.5
  332.8 24.6 %collective-permute-done.34 = bf16[768,1536]{1,0:T(8,128)(2,1)} collective-permute-done((bf16[768,1536]{1,0:T(8,128)(2,1)}, bf16[768,1536]{1,0:T(8,128)(2,1)}, u32[]{:S(2)}, u32[]{:S(2)}) %collective-permute-start.34) | collective-permute-done | bytes 2359328 | tf_op jit(solution)/shard_map/ppermute | solution.py:29
  363.8 6.0 multiply_convert_fusion
  371.7 8.2 %fusion.5 = bf16[768,1536]{1,0:T(8,128)(2,1)S(1)} fusion(f32[768,1536]{1,0:T(8,128)} %get-tuple-element.278, bf16[768,1536]{1,0:T(8,128)(2,1)} %bitcast.301, bf16[1536,1536]{1,0:T(8,128)(2,1)} %all-gather.11.cloned.1.call-done), kind=kOutput, calls=%fused_computation.6 | convolution fusion | flops 3635675136 | bytes 14155776 | tf_op jit(solution)/shard_map/dot_general | solution.py:19
  379.9 3.8 fusion.162
  387.1 3.8 fusion.161
  394.4 6.0 convolution_convert_fusion.3
  408.0 11.0 %collective-permute-done.41 = bf16[2,96,1536]{2,1,0:T(8,128)(2,1)S(1)} collective-permute-done((bf16[2,96,1536]{2,1,0:T(8,128)(2,1)S(1)}, bf16[2,96,1536]{2,1,0:T(8,128)(2,1)S(1)}, u32[]{:S(2)}, u32[]{:S(2)}) %collective-permute-start.41) | collective-permute-done | bytes 589856 | tf_op jit(solution)/shard_map/ppermute | solution.py:33
  422.3 3.4 convolution_convert_fusion.5
  425.7 10.9 %shard_map.332 = (bf16[2,96,1536]{2,1,0:T(8,128)(2,1)S(1)}, f32[2,64,1536]{2,1,0:T(8,128)S(1)}, f32[2,64,1536]{2,1,0:T(8,128)S(1)}) custom-call(bf16[2,96,1536]{2,1,0:T(8,128)(2,1)S(1)} %bitcast.268, bf16[2,64,1536]{2,1,0:T(8,128)(2,1)S(1)} %bitcast.258, bf16[2,64,1536]{2,1,0:T(8,128)(2,1)S(1)} %bitcast.260, bf16[2,96,1536]{2,1,0:T(8,128)(2,1)S(1)} %bitcast.271), custom_call_target="tpu_custom_call" | custom-call | flops 188743680 | bytes 2359296 | tf_op jit(solution)/shard_map/pallas_call | solution.py:398
  436.6 2.4 multiply_reduce_fusion.1
  445.5 2.5 pad_maximum_fusion.2
  448.0 10.8 %collective-permute-done.46 = bf16[2,128,384]{2,1,0:T(8,128)(2,1)S(1)} collective-permute-done((bf16[2,128,384]{2,1,0:T(8,128)(2,1)S(1)}, bf16[2,128,384]{2,1,0:T(8,128)(2,1)S(1)}, u32[]{:S(2)}, u32[]{:S(2)}) %collective-permute-start.46) | collective-permute-done | bytes 196640 | tf_op jit(solution)/shard_map/ppermute | solution.py:33
  469.0 5.9 convolution_convert_fusion
  477.1 3.1 fusion.77
  480.9 4.2 fusion.35
  490.9 2.6 convolution_convert_fusion.9
  493.5 13.9 %collective-permute-done.53 = bf16[128,768]{1,0:T(8,128)(2,1)S(1)} collective-permute-done((bf16[128,768]{1,0:T(8,128)(2,1)S(1)}, bf16[128,768]{1,0:T(8,128)(2,1)S(1)}, u32[]{:S(2)}, u32[]{:S(2)}) %collective-permute-start.53) | collective-permute-done | bytes 196640 | tf_op jit(solution)/shard_map/ppermute | solution.py:643
  508.0 3.0 collective-permute-start.52
  511.7 2.8 collective-permute-start.50
  514.5 8.3 %convert_add_fusion = (f32[1536,768]{1,0:T(8,128)}, f32[1536,768]{1,0:T(8,128)}) fusion(f32[1536,768]{1,0:T(8,128)} %fusion.77, bf16[1536,1536]{1,0:T(8,128)(2,1)} %collective-permute-done.49, f32[1536,768]{1,0:T(8,128)S(1)} %fusion.79), kind=kLoop, calls=%fused_computation.15 | loop fusion | flops 4718592 | bytes 23592960 | tf_op jit(solution)/shard_map/add | solution.py:515
  533.0 4.8 collective-permute-done.50
  538.0 2.9 reduce-scatter.6.cloned.1.call-done
  540.9 3.6 fusion.160
  544.4 5.2 add_convert_fusion
  550.0 2.6 fusion.88
  557.0 24.4 %shard_map.333 = bf16[4,384,576]{2,1,0:T(8,128)(2,1)S(1)} custom-call(s32[2]{0:T(128)S(1)} %pad_add_fusion.place_ref, bf16[4,384,576]{2,1,0:T(8,128)(2,1)S(1)} %copy-done.1, bf16[4,384,192]{2,1,0:T(8,128)(2,1)S(1)} %get-tuple-element.82.out_ref, f32[4,3,384]{2,1,0:T(4,128)S(1)} %copy-done.3, bf16[4,384,192]{2,1,0:T(8,128)(2,1)S(1)} %pad_maximum_fusion.24.grad_ref), custom_call_target="tpu_custom_call" | custom-call | flops 2831155200 | bytes 7077888 | tf_op jit(solution)/shard_map/pallas_call | solution.py:324
  581.5 11.2 %collective-permute-done.60 = bf16[128,1536]{1,0:T(8,128)(2,1)S(1)} collective-permute-done((bf16[128,1536]{1,0:T(8,128)(2,1)S(1)}, bf16[128,1536]{1,0:T(8,128)(2,1)S(1)}, u32[]{:S(2)}, u32[]{:S(2)}) %collective-permute-start.60) | collective-permute-done | bytes 393248 | tf_op jit(solution)/shard_map/ppermute | solution.py:33
  600.4 26.8 %collective-permute-done.58 = bf16[384,576]{1,0:T(8,128)(2,1)S(1)} collective-permute-done((bf16[384,576]{1,0:T(8,128)(2,1)S(1)}, bf16[384,576]{1,0:T(8,128)(2,1)S(1)}, u32[]{:S(2)}, u32[]{:S(2)}) %collective-permute-start.58) | collective-permute-done | bytes 442400 | tf_op jit(solution)/shard_map/ppermute | solution.py:25
  627.2 8.4 %collective-permute-done.57 = bf16[384,576]{1,0:T(8,128)(2,1)S(1)} collective-permute-done((bf16[384,576]{1,0:T(8,128)(2,1)S(1)}, bf16[384,576]{1,0:T(8,128)(2,1)S(1)}, u32[]{:S(2)}, u32[]{:S(2)}) %collective-permute-start.57) | collective-permute-done | bytes 442400 | tf_op jit(solution)/shard_map/ppermute | solution.py:25
  635.6 2.5 collective-permute-done.56
  649.5 5.7 fusion.163
  663.3 2.4 fusion.63
  666.1 15.3 %collective-permute-done.65 = bf16[768,640]{1,0:T(8,128)(2,1)} collective-permute-done((bf16[768,640]{1,0:T(8,128)(2,1)S(1)}, bf16[768,640]{1,0:T(8,128)(2,1)}, u32[]{:S(2)}, u32[]{:S(2)}) %collective-permute-start.65) | collective-permute-done | bytes 983072 | tf_op jit(solution)/shard_map/ppermute | solution.py:29
  684.4 2.9 add_convert_fusion.3
  692.9 4.4 collective-permute-done.66
  699.4 2.9 add_convert_fusion.4
  703.8 2.6 collective-permute-done.69
  710.5 2.4 collective-permute-start.73
  720.8 14.6 %reduce-scatter.14.cloned.1.call-done = bf16[192,512]{1,0:T(8,128)(2,1)} async-done(((bf16[768,512]{1,0:T(8,128)(2,1)}), bf16[192,512]{1,0:T(8,128)(2,1)}) %reduce-scatter.14.cloned.1.call-update) | async-done | bytes 196624 | tf_op jit(solution)/shard_map/reduce_scatter | solution.py:562
  (508 shorter events, 199.2 us)
Async XLA Ops:
  7.2 88.5 %all-gather.5.cloned.1.call-start = ((), (), s32[]{:S(2)}) async-start(), calls=%async_computation.5 | async-start | bytes 2654208 | tf_op jit(solution)/shard_map/all_gather | solution.py:465
  9.1 179.4 %all-gather.7.cloned.1.call-start = ((), (), s32[]{:S(2)}) async-start(), calls=%async_computation.6 | async-start | bytes 3981312 | tf_op jit(solution)/shard_map/all_gather | solution.py:465
  11.1 246.3 %all-gather.9.cloned.1.call-start = ((), (), s32[]{:S(2)}) async-start(), calls=%async_computation.7 | async-start | bytes 2949120 | tf_op jit(solution)/shard_map/all_gather | solution.py:477
  15.1 12.9 %collective-permute-start = (bf16[8,192]{1,0:T(8,128)(2,1)S(1)}, bf16[8,192]{1,0:T(8,128)(2,1)S(1)}, u32[]{:S(2)}, u32[]{:S(2)}) collective-permute-start(bf16[8,192]{1,0:T(8,128)(2,1)S(1)} %stack.147), channel_id=1, source_target_pairs={{16,0},{0,16},{17,1},{1,17},{18,2},{2,18},{19,3},{3,19},{20,4},{4,... | collective-permute-start | bytes 9224 | tf_op jit(solution)/shard_map/ppermute | solution.py:29
  16.7 11.3 %collective-permute-start.1 = (bf16[8,192]{1,0:T(8,128)(2,1)S(1)}, bf16[8,192]{1,0:T(8,128)(2,1)S(1)}, u32[]{:S(2)}, u32[]{:S(2)}) collective-permute-start(bf16[8,192]{1,0:T(8,128)(2,1)S(1)} %stack.147), channel_id=1, source_target_pairs={{4,0},{8,4},{12,8},{0,12},{5,1},{9,5},{13,9},{1,13},{6,2},{10,6},{... | collective-permute-start | bytes 9224 | tf_op jit(solution)/shard_map/ppermute | solution.py:25
  17.2 12.4 %collective-permute-start.3 = (bf16[8,192]{1,0:T(8,128)(2,1)S(1)}, bf16[8,192]{1,0:T(8,128)(2,1)S(1)}, u32[]{:S(2)}, u32[]{:S(2)}) collective-permute-start(bf16[8,192]{1,0:T(8,128)(2,1)S(1)} %stack.147), channel_id=1, source_target_pairs={{12,0},{0,4},{4,8},{8,12},{13,1},{1,5},{5,9},{9,13},{14,2},{2,6},{... | collective-permute-start | bytes 9224 | tf_op jit(solution)/shard_map/ppermute | solution.py:25
  18.7 17.1 %collective-permute-start.5 = (bf16[8,192]{1,0:T(8,128)(2,1)S(1)}, bf16[8,192]{1,0:T(8,128)(2,1)S(1)}, u32[]{:S(2)}, u32[]{:S(2)}) collective-permute-start(bf16[8,192]{1,0:T(8,128)(2,1)S(1)} %stack.147), channel_id=1, source_target_pairs={{8,0},{12,4},{0,8},{4,12},{9,1},{13,5},{1,9},{5,13},{10,2},{14,6},... | collective-permute-start | bytes 9224 | tf_op jit(solution)/shard_map/ppermute | solution.py:25
  23.6 21.7 %collective-permute-start.10 = (bf16[192,1152]{1,0:T(8,128)(2,1)S(1)}, bf16[192,1152]{1,0:T(8,128)(2,1)S(1)}, u32[]{:S(2)}, u32[]{:S(2)}) collective-permute-start(bf16[192,1152]{1,0:T(8,128)(2,1)S(1)} %concatenate.82), channel_id=1, source_target_pairs={{16,0},{0,16},{17,1},{1,17},{18,2},{2,18},{19,3},{3,19},{20,4},{4,... | collective-permute-start | bytes 1327112 | tf_op jit(solution)/shard_map/ppermute | solution.py:29
  24.2 347.4 %all-gather.11.cloned.1.call-start = ((), (), s32[]{:S(2)}) async-start(), calls=%async_computation.8 | async-start | bytes 5308416 | tf_op jit(solution)/shard_map/all_gather | solution.py:465
  28.0 34.7 %collective-permute-start.11 = (bf16[192,1152]{1,0:T(8,128)(2,1)S(1)}, bf16[192,1152]{1,0:T(8,128)(2,1)S(1)}, u32[]{:S(2)}, u32[]{:S(2)}) collective-permute-start(bf16[192,1152]{1,0:T(8,128)(2,1)S(1)} %concatenate.82), channel_id=1, source_target_pairs={{4,0},{8,4},{12,8},{0,12},{5,1},{9,5},{13,9},{1,13},{6,2},{10,6},{... | collective-permute-start | bytes 1327112 | tf_op jit(solution)/shard_map/ppermute | solution.py:25
  29.6 34.7 %collective-permute-start.13 = (bf16[192,1152]{1,0:T(8,128)(2,1)S(1)}, bf16[192,1152]{1,0:T(8,128)(2,1)S(1)}, u32[]{:S(2)}, u32[]{:S(2)}) collective-permute-start(bf16[192,1152]{1,0:T(8,128)(2,1)S(1)} %concatenate.82), channel_id=1, source_target_pairs={{12,0},{0,4},{4,8},{8,12},{13,1},{1,5},{5,9},{9,13},{14,2},{2,6},{... | collective-permute-start | bytes 1327112 | tf_op jit(solution)/shard_map/ppermute | solution.py:25
  35.8 52.7 %collective-permute-start.15 = (bf16[192,1152]{1,0:T(8,128)(2,1)S(1)}, bf16[192,1152]{1,0:T(8,128)(2,1)}, u32[]{:S(2)}, u32[]{:S(2)}) collective-permute-start(bf16[192,1152]{1,0:T(8,128)(2,1)S(1)} %concatenate.82), channel_id=1, source_target_pairs={{8,0},{12,4},{0,8},{4,12},{9,1},{13,5},{1,9},{5,13},{10,2},{14,6},... | collective-permute-start | bytes 1327112 | tf_op jit(solution)/shard_map/ppermute | solution.py:25
  43.8 47.4 %collective-permute-start.7 = (bf16[2,96,1536]{2,1,0:T(8,128)(2,1)S(1)}, bf16[2,96,1536]{2,1,0:T(8,128)(2,1)S(1)}, u32[]{:S(2)}, u32[]{:S(2)}) collective-permute-start(bf16[2,96,1536]{2,1,0:T(8,128)(2,1)S(1)} %fusion.23), channel_id=1, source_target_pairs={{0,2},{1,3},{2,0},{3,1},{4,6},{5,7},{6,4},{7,5},{8,10},{9,11},{10,... | collective-permute-start | bytes 1769480 | tf_op jit(solution)/shard_map/ppermute | solution.py:33
  45.3 50.2 %collective-permute-start.8 = (bf16[2,96,1536]{2,1,0:T(8,128)(2,1)S(1)}, bf16[2,96,1536]{2,1,0:T(8,128)(2,1)S(1)}, u32[]{:S(2)}, u32[]{:S(2)}) collective-permute-start(bf16[2,96,1536]{2,1,0:T(8,128)(2,1)S(1)} %fusion.23), channel_id=1, source_target_pairs={{0,1},{1,0},{2,3},{3,2},{4,5},{5,4},{6,7},{7,6},{8,9},{9,8},{10,11... | collective-permute-start | bytes 1769480 | tf_op jit(solution)/shard_map/ppermute | solution.py:33
  62.7 28.6 %collective-permute-start.12 = (bf16[192,1152]{1,0:T(8,128)(2,1)S(1)}, bf16[192,1152]{1,0:T(8,128)(2,1)S(1)}, u32[]{:S(2)}, u32[]{:S(2)}) collective-permute-start(bf16[192,1152]{1,0:T(8,128)(2,1)S(1)} %collective-permute-done.11), channel_id=1, source_target_pairs={{16,0},{0,16},{17,1},{1,17},{18,2},{2,18},{19,3},{3,19},{20,4},{4,... | collective-permute-start | bytes 1327112 | tf_op jit(solution)/shard_map/ppermute | solution.py:29
  64.3 28.6 %collective-permute-start.14 = (bf16[192,1152]{1,0:T(8,128)(2,1)S(1)}, bf16[192,1152]{1,0:T(8,128)(2,1)S(1)}, u32[]{:S(2)}, u32[]{:S(2)}) collective-permute-start(bf16[192,1152]{1,0:T(8,128)(2,1)S(1)} %collective-permute-done.13), channel_id=1, source_target_pairs={{16,0},{0,16},{17,1},{1,17},{18,2},{2,18},{19,3},{3,19},{20,4},{4,... | collective-permute-start | bytes 1327112 | tf_op jit(solution)/shard_map/ppermute | solution.py:29
  88.6 12.2 %collective-permute-start.16 = (bf16[192,1152]{1,0:T(8,128)(2,1)}, bf16[192,1152]{1,0:T(8,128)(2,1)}, u32[]{:S(2)}, u32[]{:S(2)}) collective-permute-start(bf16[192,1152]{1,0:T(8,128)(2,1)} %collective-permute-done.15), channel_id=1, source_target_pairs={{16,0},{0,16},{17,1},{1,17},{18,2},{2,18},{19,3},{3,19},{20,4},{4,... | collective-permute-start | bytes 1327112 | tf_op jit(solution)/shard_map/ppermute | solution.py:29
  95.8 94.6 %collective-permute-start.20 = (bf16[1536,768]{1,0:T(8,128)(2,1)}, bf16[1536,768]{1,0:T(8,128)(2,1)}, u32[]{:S(2)}, u32[]{:S(2)}) collective-permute-start(bf16[1536,768]{1,0:T(8,128)(2,1)} %all-gather.5.cloned.1.call-done), channel_id=1, source_target_pairs={{0,2},{1,3},{2,0},{3,1},{4,6},{5,7},{6,4},{7,5},{8,10},{9,11},{10,... | collective-permute-start | bytes 7077896 | tf_op jit(solution)/shard_map/ppermute | solution.py:33
  109.6 19.5 %collective-permute-start.19 = (bf16[384,576]{1,0:T(8,128)(2,1)}, bf16[384,576]{1,0:T(8,128)(2,1)S(1)}, u32[]{:S(2)}, u32[]{:S(2)}) collective-permute-start(bf16[384,576]{1,0:T(8,128)(2,1)} %get-tuple-element.215), channel_id=1, source_target_pairs={{4,0},{8,4},{12,8},{0,12},{5,1},{9,5},{13,9},{1,13},{6,2},{10,6},{... | collective-permute-start | bytes 1327112 | tf_op jit(solution)/shard_map/ppermute | solution.py:25
  111.3 38.1 %collective-permute-start.18 = (bf16[384,576]{1,0:T(8,128)(2,1)S(1)}, bf16[384,576]{1,0:T(8,128)(2,1)S(1)}, u32[]{:S(2)}, u32[]{:S(2)}) collective-permute-start(bf16[384,576]{1,0:T(8,128)(2,1)S(1)} %get-tuple-element.216), channel_id=1, source_target_pairs={{8,0},{12,4},{0,8},{4,12},{9,1},{13,5},{1,9},{5,13},{10,2},{14,6},... | collective-permute-start | bytes 1327112 | tf_op jit(solution)/shard_map/ppermute | solution.py:25
  113.1 68.2 %collective-permute-start.17 = (bf16[384,576]{1,0:T(8,128)(2,1)S(1)}, bf16[384,576]{1,0:T(8,128)(2,1)}, u32[]{:S(2)}, u32[]{:S(2)}) collective-permute-start(bf16[384,576]{1,0:T(8,128)(2,1)S(1)} %get-tuple-element.217), channel_id=1, source_target_pairs={{12,0},{0,4},{4,8},{8,12},{13,1},{1,5},{5,9},{9,13},{14,2},{2,6},{... | collective-permute-start | bytes 1327112 | tf_op jit(solution)/shard_map/ppermute | solution.py:25
  209.2 44.7 %collective-permute-start.24 = (bf16[128,768]{0,1:T(8,128)(2,1)S(1)}, bf16[128,768]{0,1:T(8,128)(2,1)S(1)}, u32[]{:S(2)}, u32[]{:S(2)}) collective-permute-start(bf16[128,768]{0,1:T(8,128)(2,1)S(1)} %fusion.46), channel_id=1, source_target_pairs={{0,2},{1,3},{2,0},{3,1},{4,6},{5,7},{6,4},{7,5},{8,10},{9,11},{10,... | collective-permute-start | bytes 589832 | tf_op jit(solution)/shard_map/ppermute | solution.py:33
  210.8 43.2 %collective-permute-start.25 = (bf16[128,768]{0,1:T(8,128)(2,1)S(1)}, bf16[128,768]{0,1:T(8,128)(2,1)S(1)}, u32[]{:S(2)}, u32[]{:S(2)}) collective-permute-start(bf16[128,768]{0,1:T(8,128)(2,1)S(1)} %fusion.46), channel_id=1, source_target_pairs={{0,1},{1,0},{2,3},{3,2},{4,5},{5,4},{6,7},{7,6},{8,9},{9,8},{10,11... | collective-permute-start | bytes 589832 | tf_op jit(solution)/shard_map/ppermute | solution.py:33
  210.9 15.6 %collective-permute-start.23 = (bf16[384,192]{1,0:T(8,128)(2,1)S(1)}, bf16[384,192]{1,0:T(8,128)(2,1)S(1)}, u32[]{:S(2)}, u32[]{:S(2)}) collective-permute-start(bf16[384,192]{1,0:T(8,128)(2,1)S(1)} %get-tuple-element.233), channel_id=1, source_target_pairs={{12,0},{0,4},{4,8},{8,12},{13,1},{1,5},{5,9},{9,13},{14,2},{2,6},{... | collective-permute-start | bytes 442376 | tf_op jit(solution)/shard_map/ppermute | solution.py:25
  211.7 38.2 %collective-permute-start.22 = (bf16[384,192]{1,0:T(8,128)(2,1)S(1)}, bf16[384,192]{1,0:T(8,128)(2,1)S(1)}, u32[]{:S(2)}, u32[]{:S(2)}) collective-permute-start(bf16[384,192]{1,0:T(8,128)(2,1)S(1)} %get-tuple-element.234), channel_id=1, source_target_pairs={{8,0},{12,4},{0,8},{4,12},{9,1},{13,5},{1,9},{5,13},{10,2},{14,6},... | collective-permute-start | bytes 442376 | tf_op jit(solution)/shard_map/ppermute | solution.py:25
  216.1 37.1 %collective-permute-start.21 = (bf16[384,192]{1,0:T(8,128)(2,1)S(1)}, bf16[384,192]{1,0:T(8,128)(2,1)S(1)}, u32[]{:S(2)}, u32[]{:S(2)}) collective-permute-start(bf16[384,192]{1,0:T(8,128)(2,1)S(1)} %get-tuple-element.235), channel_id=1, source_target_pairs={{4,0},{8,4},{12,8},{0,12},{5,1},{9,5},{13,9},{1,13},{6,2},{10,6},{... | collective-permute-start | bytes 442376 | tf_op jit(solution)/shard_map/ppermute | solution.py:25
  264.5 49.8 %collective-permute-start.37 = (bf16[2,96,1536]{2,1,0:T(8,128)(2,1)}, bf16[2,96,1536]{2,1,0:T(8,128)(2,1)}, u32[]{:S(2)}, u32[]{:S(2)}) collective-permute-start(bf16[2,96,1536]{2,1,0:T(8,128)(2,1)} %bitcast.253), channel_id=1, source_target_pairs={{0,2},{1,3},{2,0},{3,1},{4,6},{5,7},{6,4},{7,5},{8,10},{9,11},{10,... | collective-permute-start | bytes 1769480 | tf_op jit(solution)/shard_map/ppermute | solution.py:33
  265.8 275.1 %reduce-scatter.6.cloned.1.call-start = ((), (), s32[]{:S(2)}) async-start(), calls=%async_computation.9 | async-start | bytes 2949120 | tf_op jit(solution)/shard_map/reduce_scatter | solution.py:562
  266.2 27.7 %collective-permute-start.30 = (bf16[1536,768]{1,0:T(8,128)(2,1)}, bf16[1536,768]{1,0:T(8,128)(2,1)S(1)}, u32[]{:S(2)}, u32[]{:S(2)}) collective-permute-start(bf16[1536,768]{1,0:T(8,128)(2,1)} %collective-permute-done.20), channel_id=1, source_target_pairs={{0,1},{1,0},{2,3},{3,2},{4,5},{5,4},{6,7},{7,6},{8,9},{9,8},{10,11... | collective-permute-start | bytes 7077896 | tf_op jit(solution)/shard_map/ppermute | solution.py:33
  269.1 23.9 %collective-permute-start.28 = (bf16[2,96,1536]{2,1,0:T(8,128)(2,1)S(1)}, bf16[2,96,1536]{2,1,0:T(8,128)(2,1)S(1)}, u32[]{:S(2)}, u32[]{:S(2)}) collective-permute-start(bf16[2,96,1536]{2,1,0:T(8,128)(2,1)S(1)} %slice.825), channel_id=1, source_target_pairs={{0,2},{1,3},{2,0},{3,1},{4,6},{5,7},{6,4},{7,5},{8,10},{9,11},{10,... | collective-permute-start | bytes 1769480 | tf_op jit(solution)/shard_map/ppermute | solution.py:33
  272.4 21.8 %collective-permute-start.29 = (bf16[1536,768]{1,0:T(8,128)(2,1)S(1)}, bf16[1536,768]{1,0:T(8,128)(2,1)S(1)}, u32[]{:S(2)}, u32[]{:S(2)}) collective-permute-start(bf16[1536,768]{1,0:T(8,128)(2,1)S(1)} %copy-done.36), channel_id=1, source_target_pairs={{0,1},{1,0},{2,3},{3,2},{4,5},{5,4},{6,7},{7,6},{8,9},{9,8},{10,11... | collective-permute-start | bytes 7077896 | tf_op jit(solution)/shard_map/ppermute | solution.py:33
  272.7 84.7 %collective-permute-start.34 = (bf16[768,1536]{1,0:T(8,128)(2,1)}, bf16[768,1536]{1,0:T(8,128)(2,1)}, u32[]{:S(2)}, u32[]{:S(2)}) collective-permute-start(bf16[768,1536]{1,0:T(8,128)(2,1)} %all-gather.9.cloned.1.call-done), channel_id=1, source_target_pairs={{16,0},{0,16},{17,1},{1,17},{18,2},{2,18},{19,3},{3,19},{20,4},{4,... | collective-permute-start | bytes 7077896 | tf_op jit(solution)/shard_map/ppermute | solution.py:29
  313.0 15.0 %collective-permute-start.31 = (bf16[2,96,1536]{2,1,0:T(8,128)(2,1)S(1)}, bf16[2,96,1536]{2,1,0:T(8,128)(2,1)}, u32[]{:S(2)}, u32[]{:S(2)}) collective-permute-start(bf16[2,96,1536]{2,1,0:T(8,128)(2,1)S(1)} %add_convert_fusion.6), channel_id=1, source_target_pairs={{0,2},{1,3},{2,0},{3,1},{4,6},{5,7},{6,4},{7,5},{8,10},{9,11},{10,... | collective-permute-start | bytes 1769480 | tf_op jit(solution)/shard_map/ppermute | solution.py:33
  314.3 13.7 %collective-permute-start.38 = (bf16[2,96,1536]{2,1,0:T(8,128)(2,1)}, bf16[2,96,1536]{2,1,0:T(8,128)(2,1)}, u32[]{:S(2)}, u32[]{:S(2)}) collective-permute-start(bf16[2,96,1536]{2,1,0:T(8,128)(2,1)} %bitcast.253), channel_id=1, source_target_pairs={{0,1},{1,0},{2,3},{3,2},{4,5},{5,4},{6,7},{7,6},{8,9},{9,8},{10,11... | collective-permute-start | bytes 1769480 | tf_op jit(solution)/shard_map/ppermute | solution.py:33
  314.3 13.7 %collective-permute-start.39 = (bf16[2,96,1536]{2,1,0:T(8,128)(2,1)}, bf16[2,96,1536]{2,1,0:T(8,128)(2,1)}, u32[]{:S(2)}, u32[]{:S(2)}) collective-permute-start(bf16[2,96,1536]{2,1,0:T(8,128)(2,1)} %collective-permute-done.37), channel_id=1, source_target_pairs={{0,1},{1,0},{2,3},{3,2},{4,5},{5,4},{6,7},{7,6},{8,9},{9,8},{10,11... | collective-permute-start | bytes 1769480 | tf_op jit(solution)/shard_map/ppermute | solution.py:33
  314.8 16.4 %collective-permute-start.32 = (bf16[2,96,1536]{2,1,0:T(8,128)(2,1)S(1)}, bf16[2,96,1536]{2,1,0:T(8,128)(2,1)}, u32[]{:S(2)}, u32[]{:S(2)}) collective-permute-start(bf16[2,96,1536]{2,1,0:T(8,128)(2,1)S(1)} %add_convert_fusion.6), channel_id=1, source_target_pairs={{0,1},{1,0},{2,3},{3,2},{4,5},{5,4},{6,7},{7,6},{8,9},{9,8},{10,11... | collective-permute-start | bytes 1769480 | tf_op jit(solution)/shard_map/ppermute | solution.py:33
  384.9 16.1 %collective-permute-start.40 = (bf16[2,192,1536]{2,1,0:T(8,128)(2,1)}, bf16[2,192,1536]{2,1,0:T(8,128)(2,1)}, u32[]{:S(2)}, u32[]{:S(2)}) collective-permute-start(bf16[2,192,1536]{2,1,0:T(8,128)(2,1)} %slice.819), channel_id=1, source_target_pairs={{0,1},{1,0},{2,3},{3,2},{4,5},{5,4},{6,7},{7,6},{8,9},{9,8},{10,11... | collective-permute-start | bytes 3538952 | tf_op jit(solution)/shard_map/ppermute | solution.py:33
  400.3 66.0 %collective-permute-start.48 = (bf16[768,1536]{1,0:T(8,128)(2,1)}, bf16[768,1536]{1,0:T(8,128)(2,1)S(1)}, u32[]{:S(2)}, u32[]{:S(2)}) collective-permute-start(bf16[768,1536]{1,0:T(8,128)(2,1)} %convolution_convert_fusion.3), channel_id=1, source_target_pairs={{16,0},{0,16},{17,1},{1,17},{18,2},{2,18},{19,3},{3,19},{20,4},{4,... | collective-permute-start | bytes 7077896 | tf_op jit(solution)/shard_map/ppermute | solution.py:29
  402.7 16.3 %collective-permute-start.41 = (bf16[2,96,1536]{2,1,0:T(8,128)(2,1)S(1)}, bf16[2,96,1536]{2,1,0:T(8,128)(2,1)S(1)}, u32[]{:S(2)}, u32[]{:S(2)}) collective-permute-start(bf16[2,96,1536]{2,1,0:T(8,128)(2,1)S(1)} %slice.823), channel_id=1, source_target_pairs={{0,2},{1,3},{2,0},{3,1},{4,6},{5,7},{6,4},{7,5},{8,10},{9,11},{10,... | collective-permute-start | bytes 1769480 | tf_op jit(solution)/shard_map/ppermute | solution.py:33
  407.3 31.7 %collective-permute-start.36 = (bf16[2,96,1536]{2,1,0:T(8,128)(2,1)}, bf16[2,96,1536]{2,1,0:T(8,128)(2,1)S(1)}, u32[]{:S(2)}, u32[]{:S(2)}) collective-permute-start(bf16[2,96,1536]{2,1,0:T(8,128)(2,1)} %slice.824), channel_id=1, source_target_pairs={{0,2},{1,3},{2,0},{3,1},{4,6},{5,7},{6,4},{7,5},{8,10},{9,11},{10,... | collective-permute-start | bytes 1769480 | tf_op jit(solution)/shard_map/ppermute | solution.py:33
  440.6 19.9 %collective-permute-start.42 = (bf16[2,96,1536]{2,1,0:T(8,128)(2,1)S(1)}, bf16[2,96,1536]{2,1,0:T(8,128)(2,1)S(1)}, u32[]{:S(2)}, u32[]{:S(2)}) collective-permute-start(bf16[2,96,1536]{2,1,0:T(8,128)(2,1)S(1)} %convert_element_type.241), channel_id=1, source_target_pairs={{0,2},{1,3},{2,0},{3,1},{4,6},{5,7},{6,4},{7,5},{8,10},{9,11},{10,... | collective-permute-start | bytes 1769480 | tf_op jit(solution)/shard_map/ppermute | solution.py:33
  442.1 22.6 %collective-permute-start.43 = (bf16[2,96,1536]{2,1,0:T(8,128)(2,1)S(1)}, bf16[2,96,1536]{2,1,0:T(8,128)(2,1)S(1)}, u32[]{:S(2)}, u32[]{:S(2)}) collective-permute-start(bf16[2,96,1536]{2,1,0:T(8,128)(2,1)S(1)} %convert_element_type.241), channel_id=1, source_target_pairs={{0,1},{1,0},{2,3},{3,2},{4,5},{5,4},{6,7},{7,6},{8,9},{9,8},{10,11... | collective-permute-start | bytes 1769480 | tf_op jit(solution)/shard_map/ppermute | solution.py:33
  444.8 14.0 %collective-permute-start.46 = (bf16[2,128,384]{2,1,0:T(8,128)(2,1)S(1)}, bf16[2,128,384]{2,1,0:T(8,128)(2,1)S(1)}, u32[]{:S(2)}, u32[]{:S(2)}) collective-permute-start(bf16[2,128,384]{2,1,0:T(8,128)(2,1)S(1)} %slice.826), channel_id=1, source_target_pairs={{0,2},{1,3},{2,0},{3,1},{4,6},{5,7},{6,4},{7,5},{8,10},{9,11},{10,... | collective-permute-start | bytes 589832 | tf_op jit(solution)/shard_map/ppermute | solution.py:33
  448.0 59.6 %collective-permute-start.49 = (bf16[1536,1536]{1,0:T(8,128)(2,1)}, bf16[1536,1536]{1,0:T(8,128)(2,1)}, u32[]{:S(2)}, u32[]{:S(2)}) collective-permute-start(bf16[1536,1536]{1,0:T(8,128)(2,1)} %pad_maximum_fusion.2), channel_id=1, source_target_pairs={{0,1},{1,0},{2,3},{3,2},{4,5},{5,4},{6,7},{7,6},{8,9},{9,8},{10,11... | collective-permute-start | bytes 14155784 | tf_op jit(solution)/shard_map/ppermute | solution.py:33
  468.5 172.5 %reduce-scatter.8.cloned.1.call-start = ((), (), s32[]{:S(2)}) async-start(), calls=%async_computation.10 | async-start | bytes 2949120 | tf_op jit(solution)/shard_map/reduce_scatter | solution.py:562
  474.9 63.0 %collective-permute-start.54 = (bf16[768,1536]{1,0:T(8,128)(2,1)}, bf16[768,1536]{1,0:T(8,128)(2,1)}, u32[]{:S(2)}, u32[]{:S(2)}) collective-permute-start(bf16[768,1536]{1,0:T(8,128)(2,1)} %convolution_convert_fusion), channel_id=1, source_target_pairs={{16,0},{0,16},{17,1},{1,17},{18,2},{2,18},{19,3},{3,19},{20,4},{4,... | collective-permute-start | bytes 7077896 | tf_op jit(solution)/shard_map/ppermute | solution.py:29
  485.1 22.3 %collective-permute-start.53 = (bf16[128,768]{1,0:T(8,128)(2,1)S(1)}, bf16[128,768]{1,0:T(8,128)(2,1)S(1)}, u32[]{:S(2)}, u32[]{:S(2)}) collective-permute-start(bf16[128,768]{1,0:T(8,128)(2,1)S(1)} %convert_element_type.250), channel_id=1, source_target_pairs={{0,8},{4,12},{8,0},{12,4},{1,9},{5,13},{9,1},{13,5},{2,10},{6,14},... | collective-permute-start | bytes 589832 | tf_op jit(solution)/shard_map/ppermute | solution.py:643
  488.3 152.7 %collective-permute-start.62 = (bf16[768,384]{1,0:T(8,128)(2,1)}, bf16[768,384]{1,0:T(8,128)(2,1)}, u32[]{:S(2)}, u32[]{:S(2)}) collective-permute-start(bf16[768,384]{1,0:T(8,128)(2,1)} %convolution_convert_fusion.10), channel_id=1, source_target_pairs={{16,0},{0,16},{17,1},{1,17},{18,2},{2,18},{19,3},{3,19},{20,4},{4,... | collective-permute-start | bytes 1769480 | tf_op jit(solution)/shard_map/ppermute | solution.py:29
  508.0 23.6 %collective-permute-start.52 = (bf16[384,192]{1,0:T(8,128)(2,1)S(1)}, bf16[384,192]{1,0:T(8,128)(2,1)S(1)}, u32[]{:S(2)}, u32[]{:S(2)}) collective-permute-start(bf16[384,192]{1,0:T(8,128)(2,1)S(1)} %get-tuple-element.223), channel_id=1, source_target_pairs={{4,0},{8,4},{12,8},{0,12},{5,1},{9,5},{13,9},{1,13},{6,2},{10,6},{... | collective-permute-start | bytes 442376 | tf_op jit(solution)/shard_map/ppermute | solution.py:25
  511.0 22.0 %collective-permute-start.51 = (bf16[384,192]{1,0:T(8,128)(2,1)S(1)}, bf16[384,192]{1,0:T(8,128)(2,1)S(1)}, u32[]{:S(2)}, u32[]{:S(2)}) collective-permute-start(bf16[384,192]{1,0:T(8,128)(2,1)S(1)} %get-tuple-element.224), channel_id=1, source_target_pairs={{8,0},{12,4},{0,8},{4,12},{9,1},{13,5},{1,9},{5,13},{10,2},{14,6},... | collective-permute-start | bytes 442376 | tf_op jit(solution)/shard_map/ppermute | solution.py:25
  511.7 26.1 %collective-permute-start.50 = (bf16[384,192]{1,0:T(8,128)(2,1)S(1)}, bf16[384,192]{1,0:T(8,128)(2,1)S(1)}, u32[]{:S(2)}, u32[]{:S(2)}) collective-permute-start(bf16[384,192]{1,0:T(8,128)(2,1)S(1)} %get-tuple-element.225), channel_id=1, source_target_pairs={{12,0},{0,4},{4,8},{8,12},{13,1},{1,5},{5,9},{9,13},{14,2},{2,6},{... | collective-permute-start | bytes 442376 | tf_op jit(solution)/shard_map/ppermute | solution.py:25
  531.6 62.4 %collective-permute-start.55 = (bf16[1536,768]{1,0:T(8,128)(2,1)}, bf16[1536,768]{1,0:T(8,128)(2,1)}, u32[]{:S(2)}, u32[]{:S(2)}) collective-permute-start(bf16[1536,768]{1,0:T(8,128)(2,1)} %pad_maximum_fusion.7), channel_id=1, source_target_pairs={{0,2},{1,3},{2,0},{3,1},{4,6},{5,7},{6,4},{7,5},{8,10},{9,11},{10,... | collective-permute-start | bytes 7077896 | tf_op jit(solution)/shard_map/ppermute | solution.py:33
  549.7 132.3 %reduce-scatter.10.cloned.1.call-start = ((), (), s32[]{:S(2)}) async-start(), calls=%async_computation.11 | async-start | bytes 2211840 | tf_op jit(solution)/shard_map/reduce_scatter | solution.py:562
  553.9 38.7 %collective-permute-start.60 = (bf16[128,1536]{1,0:T(8,128)(2,1)S(1)}, bf16[128,1536]{1,0:T(8,128)(2,1)S(1)}, u32[]{:S(2)}, u32[]{:S(2)}) collective-permute-start(bf16[128,1536]{1,0:T(8,128)(2,1)S(1)} %fusion.72), channel_id=1, source_target_pairs={{0,2},{1,3},{2,0},{3,1},{4,6},{5,7},{6,4},{7,5},{8,10},{9,11},{10,... | collective-permute-start | bytes 1179656 | tf_op jit(solution)/shard_map/ppermute | solution.py:33
  594.1 33.1 %collective-permute-start.58 = (bf16[384,576]{1,0:T(8,128)(2,1)S(1)}, bf16[384,576]{1,0:T(8,128)(2,1)S(1)}, u32[]{:S(2)}, u32[]{:S(2)}) collective-permute-start(bf16[384,576]{1,0:T(8,128)(2,1)S(1)} %get-tuple-element.211), channel_id=1, source_target_pairs={{12,0},{0,4},{4,8},{8,12},{13,1},{1,5},{5,9},{9,13},{14,2},{2,6},{... | collective-permute-start | bytes 1327112 | tf_op jit(solution)/shard_map/ppermute | solution.py:25
  594.5 41.1 %collective-permute-start.57 = (bf16[384,576]{1,0:T(8,128)(2,1)S(1)}, bf16[384,576]{1,0:T(8,128)(2,1)S(1)}, u32[]{:S(2)}, u32[]{:S(2)}) collective-permute-start(bf16[384,576]{1,0:T(8,128)(2,1)S(1)} %get-tuple-element.212), channel_id=1, source_target_pairs={{8,0},{12,4},{0,8},{4,12},{9,1},{13,5},{1,9},{5,13},{10,2},{14,6},... | collective-permute-start | bytes 1327112 | tf_op jit(solution)/shard_map/ppermute | solution.py:25
  596.1 42.0 %collective-permute-start.56 = (bf16[384,576]{1,0:T(8,128)(2,1)S(1)}, bf16[384,576]{1,0:T(8,128)(2,1)S(1)}, u32[]{:S(2)}, u32[]{:S(2)}) collective-permute-start(bf16[384,576]{1,0:T(8,128)(2,1)S(1)} %get-tuple-element.213), channel_id=1, source_target_pairs={{4,0},{8,4},{12,8},{0,12},{5,1},{9,5},{13,9},{1,13},{6,2},{10,6},{... | collective-permute-start | bytes 1327112 | tf_op jit(solution)/shard_map/ppermute | solution.py:25
  599.9 41.1 %collective-permute-start.61 = (bf16[768,768]{1,0:T(8,128)(2,1)S(1)}, bf16[768,768]{1,0:T(8,128)(2,1)}, u32[]{:S(2)}, u32[]{:S(2)}) collective-permute-start(bf16[768,768]{1,0:T(8,128)(2,1)S(1)} %pad_maximum_fusion.15), channel_id=1, source_target_pairs={{16,0},{0,16},{17,1},{1,17},{18,2},{2,18},{19,3},{3,19},{20,4},{4,... | collective-permute-start | bytes 3538952 | tf_op jit(solution)/shard_map/ppermute | solution.py:29
  627.2 13.8 %collective-permute-start.63 = (bf16[192,768]{1,0:T(8,128)(2,1)S(1)}, bf16[192,768]{1,0:T(8,128)(2,1)S(1)}, u32[]{:S(2)}, u32[]{:S(2)}) collective-permute-start(bf16[192,768]{1,0:T(8,128)(2,1)S(1)} %convolution_convert_fusion.11), channel_id=1, source_target_pairs={{16,0},{0,16},{17,1},{1,17},{18,2},{2,18},{19,3},{3,19},{20,4},{4,... | collective-permute-start | bytes 884744 | tf_op jit(solution)/shard_map/ppermute | solution.py:29
  645.5 73.2 %reduce-scatter.12.cloned.1.call-start = ((), (), s32[]{:S(2)}) async-start(), calls=%async_computation.12 | async-start | bytes 1228800 | tf_op jit(solution)/shard_map/reduce_scatter | solution.py:562
  656.6 24.8 %collective-permute-start.65 = (bf16[768,640]{1,0:T(8,128)(2,1)S(1)}, bf16[768,640]{1,0:T(8,128)(2,1)}, u32[]{:S(2)}, u32[]{:S(2)}) collective-permute-start(bf16[768,640]{1,0:T(8,128)(2,1)S(1)} %convolution_convert_fusion.7), channel_id=1, source_target_pairs={{16,0},{0,16},{17,1},{1,17},{18,2},{2,18},{19,3},{3,19},{20,4},{4,... | collective-permute-start | bytes 2949128 | tf_op jit(solution)/shard_map/ppermute | solution.py:29
  658.5 40.1 %collective-permute-start.67 = (bf16[768,512]{1,0:T(8,128)(2,1)}, bf16[768,512]{1,0:T(8,128)(2,1)}, u32[]{:S(2)}, u32[]{:S(2)}) collective-permute-start(bf16[768,512]{1,0:T(8,128)(2,1)} %convolution_convert_fusion.8), channel_id=1, source_target_pairs={{16,0},{0,16},{17,1},{1,17},{18,2},{2,18},{19,3},{3,19},{20,4},{4,... | collective-permute-start | bytes 2359304 | tf_op jit(solution)/shard_map/ppermute | solution.py:29
  682.9 14.5 %collective-permute-start.66 = (bf16[2,96,1536]{2,1,0:T(8,128)(2,1)}, bf16[2,96,1536]{2,1,0:T(8,128)(2,1)}, u32[]{:S(2)}, u32[]{:S(2)}) collective-permute-start(bf16[2,96,1536]{2,1,0:T(8,128)(2,1)} %slice.822), channel_id=1, source_target_pairs={{0,2},{1,3},{2,0},{3,1},{4,6},{5,7},{6,4},{7,5},{8,10},{9,11},{10,... | collective-permute-start | bytes 1769480 | tf_op jit(solution)/shard_map/ppermute | solution.py:33
  687.3 48.1 %reduce-scatter.14.cloned.1.call-start = ((), (), s32[]{:S(2)}) async-start(), calls=%async_computation.13 | async-start | bytes 983040 | tf_op jit(solution)/shard_map/reduce_scatter | solution.py:562
  (107 other events, 1021.5 us)
Sparse Core Ops, SparseCore 0:
  10.7 77.7 all-gather.4
  91.1 97.3 all-gather.6
  190.1 63.9 all-gather.8
  265.9 105.6 all-gather.10
  468.7 72.1 reduce-scatter.5
  549.8 46.2 reduce-scatter.7
  645.6 36.3 reduce-scatter.9
  687.4 23.3 reduce-scatter.11
  713.1 22.3 reduce-scatter.13

commit v3 on v2

--- a/solution.py
+++ b/solution.py
@@ -84,6 +84,14 @@
     result = values[:, :span]
     for place in range(1, count):
         result = jnp.where(index == place, values[:, place * span : (place + 1) * span], result)
+    return result
+
+
+def pick_rows(values, index, count):
+    span = values.shape[0] // count
+    result = values[:span]
+    for place in range(1, count):
+        result = jnp.where(index == place, values[place * span : (place + 1) * span], result)
     return result
 
 
@@ -422,14 +430,18 @@
     for step in shift_order(size):
         chunk = pick(chunks, lax.rem(own + step, size))
         slots[step] = from_context(chunk, size - step, size)
-    return jnp.stack([slots[step] for step in range(size)])
+    return [slots[step] for step in range(size)]
 
 
 def to_frames(slots, own, size):
     arrived = {0: slots[0]}
     for step in shift_order(size):
         arrived[step] = from_context(slots[step], step, size)
-    stacked = jnp.stack([arrived[step] for step in range(size)])
+    return [arrived[step] for step in range(size)]
+
+
+def by_sender(arrived, own, size):
+    stacked = jnp.stack(arrived)
     return jnp.stack([pick(stacked, lax.rem(j - own + size, size)) for j in range(size)])
 
 
@@ -461,6 +473,21 @@
     group = ((nf, nc), (own_fsdp, own_context))
     both = ("fsdp", "context")
 
+    def row_major(values):
+        return with_layout_constraint(values, Layout(major_to_minor=(0, 1)))
+
+    def gather_near(shard):
+        return lax.all_gather(shard, "context", axis=0, tiled=True)
+
+    def gather_far(near):
+        return [from_fsdp(near, far, nf) for far in range(1, nf)]
+
+    def gather_place(pieces):
+        result = jnp.zeros((nf,) + pieces[0].shape, pieces[0].dtype)
+        for far, piece in enumerate(pieces):
+            result = lax.dynamic_update_index_in_dim(result, piece, lax.rem(own_fsdp + far, nf), 0)
+        return result.reshape((nf * pieces[0].shape[0],) + pieces[0].shape[1:])
+
     def gather_calls(shard):
         return lax.all_gather(shard, both, axis=0, tiled=True)
 
@@ -473,11 +500,9 @@
         pieces += [self_query[:, lanes], self_key[:, lanes], self_value[:, lanes]]
     qkv_all = gather_group(jnp.concatenate(pieces, axis=1), *group)
     second_all = gather_calls(jnp.concatenate([cross_query, cross_out], axis=1))
-    third_all = gather_calls(jnp.concatenate([self_out, cross_key, cross_value], axis=1))
-    feed_in_near = lax.all_gather(feed_in, "context", axis=0, tiled=True)
+    third_near = gather_near(jnp.concatenate([self_out, cross_key, cross_value], axis=1))
+    feed_in_all = gather_calls(feed_in)
     feed_out_all = gather_calls(feed_out)
-    self_out_all = third_all[:, :columns]
-    cross_key_value = third_all[:, columns:]
 
     def gather_columns(blocks, first, last):
         mask = first
@@ -500,33 +525,25 @@
             mask *= 2
         return parts
 
-    def row_major(values):
-        return with_layout_constraint(values, Layout(major_to_minor=(0, 1)))
-
-    def outer_start(*products):
-        half = products[0][1].shape[1] // 2
-        far = [row_major(dot(left, right[:, half:], 0, 0)).astype(low) for left, right in products]
-        near = [row_major(dot(left, right[:, :half], 0, 0)) for left, right in products]
-        return near + [swap_tensor(jnp.concatenate(far, axis=1), 1, nt)]
-
-    def outer_step(near, arrived):
-        span = near[0].shape[1]
-        return [
-            part + arrived[:, k * span : (k + 1) * span].astype(wide) for k, part in enumerate(near)
-        ]
-
-    def outer_rest(near, arrived):
-        near = outer_step(near, arrived)
-        mask = 2
-        while mask < nt:
-            half = near[0].shape[1] // 2
-            far = jnp.concatenate([part[:, half:].astype(low) for part in near], axis=1)
-            far = swap_tensor(far, mask, nt)
-            near = [part[:, :half] for part in near]
-            mask *= 2
-            if mask < nt:
-                near = outer_step(near, far)
-        return near + [far]
+    def outer_value(products, arrived, start, stop, index=None):
+        parts = []
+        for k, (left, right) in enumerate(products):
+            if index is not None:
+                left = pick_columns(left, index, nf)
+            value = dot(left, right[:, start:stop], 0, 0)
+            for piece in arrived:
+                span = piece.shape[1] // len(products)
+                piece = piece[:, k * span + start : k * span + stop]
+                if index is not None:
+                    piece = pick_rows(piece, index, nf)
+                value = value + piece.astype(wide)
+            parts.append(row_major(value))
+        return jnp.concatenate(parts, axis=1)
+
+    def outer_swap(products, arrived, mask):
+        half = products[0][1].shape[1] // (2 * mask)
+        far = outer_value(products, arrived, half, 2 * half).astype(low)
+        return arrived + [swap_tensor(far, mask, nt)]
 
 
     residual = frames.transpose(1, 0, 2).astype(wide)
@@ -536,21 +553,23 @@
     def after(*values):
         return lax.optimization_barrier(values)
 
-    def grad_start(*products):
+    def grad_products(*products):
         def block_of(index):
             parts = [
-                with_layout_constraint(
-                    dot(pick_columns(left, index, nf), right, 0, 0), Layout(major_to_minor=(0, 1))
-                )
-                for left, right in products
+                row_major(dot(pick_columns(left, index, nf), right, 0, 0)) for left, right in products
             ]
             return parts[0] if len(parts) == 1 else jnp.concatenate(parts, axis=1)
 
-        far = [
-            from_fsdp(block_of(lax.rem(own_fsdp + step, nf)).astype(low), nf - step, nf)
-            for step in range(1, nf)
+        far = [block_of(lax.rem(own_fsdp + step, nf)).astype(low) for step in range(1, nf)]
+        return [block_of(own_fsdp)] + far
+
+    def exchange(blocks):
+        return blocks[:1] + [
+            from_fsdp(piece, nf - 1 - step, nf) for step, piece in enumerate(blocks[1:])
         ]
-        return [block_of(own_fsdp)] + far
+
+    def grad_start(*products):
+        return exchange(grad_products(*products))
 
     def block_sum(blocks):
         total = blocks[0]
@@ -583,19 +602,24 @@
     second_blocks = gather_columns([second_all], nt // 2, 2)
     projected = by_clip(dot(normed_one, qkv_all, 1, 0).astype(low))
     head_rows = to_heads(to_chunks(projected, padded), own_context, nc)
+    head_rows[1], third_near = after(head_rows[1], third_near)
+    third_far = gather_far(third_near)
+    head_rows = jnp.stack(head_rows)
     head_rows, *second_blocks = after(head_rows, *second_blocks)
     head_out, head_top = self_forward(place, head_rows, width, frame_count, order)
-    head_out, cross_key_value, *second_blocks = after(head_out, cross_key_value, *second_blocks)
+    head_out, *moved = after(head_out, *second_blocks, *third_far)
+    second_blocks, third_far = moved[: len(second_blocks)], moved[len(second_blocks) :]
+    third_all = gather_place([third_near] + third_far)
+    self_out_all = third_all[:, :columns]
+    cross_key_value = third_all[:, columns:]
     cross_query_all, cross_out_all = side_by_side(gather_columns(second_blocks, 1, 1))
-    attended = by_row(from_chunks(to_frames(head_out, own_context, nc)))
+    attended = to_frames(head_out, own_context, nc)
+    attended = by_row(from_chunks(by_sender(attended, own_context, nc)))
     text_projected = dot(by_row(text), cross_key_value, 1, 0).astype(low)
     cross_keys, cross_values = [
         by_clip(part) for part in side_by_side(gather_columns([text_projected], nt // 2, 1))
     ]
-    attended, cross_keys, cross_values, feed_in_near = after(
-        attended, cross_keys, cross_values, feed_in_near
-    )
-    feed_in_pieces = [feed_in_near] + [from_fsdp(feed_in_near, far, nf) for far in range(1, nf)]
+    attended, cross_keys, cross_values = after(attended, cross_keys, cross_values)
     after_self = residual + scatter_rows(by_clip(dot(attended, self_out_all, 1, 1)), nt)
 
     normed_two = by_row(layer_norm(after_self, vectors[2], vectors[3]))
@@ -604,25 +628,19 @@
     after_cross = after_self + by_clip(dot(by_row(crossed), cross_out_all, 1, 1))
 
     normed_three = by_row(gather_rows(layer_norm(after_cross, vectors[4], vectors[5]), nt))
-    normed_three, *feed_in_pieces = after(normed_three, *feed_in_pieces)
-    feed_in_all = jnp.zeros((nf,) + feed_in_near.shape, low)
-    for far, piece in enumerate(feed_in_pieces):
-        feed_in_all = lax.dynamic_update_index_in_dim(
-            feed_in_all, piece, lax.rem(own_fsdp + far, nf), 0
-        )
-    feed_in_all = feed_in_all.reshape(features, -1)
     hidden = dot(normed_three, feed_in_all, 1, 0)
     gate = 0.5 + 0.5 * lax.erf(hidden * (0.5**0.5))
     active = (hidden * gate).astype(low)
-    layer_out = after_cross + scatter_rows(by_clip(dot(active, feed_out_all, 1, 1)), nt)
-    layer_out = layer_out.astype(low).transpose(1, 0, 2)
-
     grad_rows = by_row(gather_rows(incoming, nt))
+    feed_out_blocks = grad_products((grad_rows, active))
+    grad_rows, *feed_out_blocks = after(grad_rows, *feed_out_blocks)
+    feed_out_blocks = exchange(feed_out_blocks)
     grad_active = dot(grad_rows, feed_out_all, 1, 0)
-    feed_out_blocks = grad_start((grad_rows, active))
     slope = gate + hidden * jnp.exp(-0.5 * hidden * hidden) * ((2.0 * jnp.pi) ** -0.5)
     grad_hidden = (grad_active * slope).astype(low)
     grad_normed = scatter_rows(by_clip(dot(grad_hidden, feed_in_all, 1, 1)), nt)
+    feed_in_blocks = grad_products((normed_three, grad_hidden))
+    grad_normed, *feed_in_blocks = after(grad_normed, *feed_in_blocks)
     piece, third_gain, third_shift = norm_back(after_cross, vectors[4], grad_normed)
     grad_after_cross = incoming.astype(wide) + piece
 
@@ -631,13 +649,14 @@
     grad_cross_queries, grad_cross_keys, grad_cross_values = cross_backward(
         cross_queries, cross_keys, cross_values, grad_crossed
     )
+    grad_cross_queries, *feed_in_blocks = after(grad_cross_queries, *feed_in_blocks)
+    feed_in_blocks = exchange(feed_in_blocks)
     grad_cross_queries = by_row(grad_cross_queries)
     grad_normed = by_clip(dot(grad_cross_queries, cross_query_all, 1, 1))
     piece, second_gain, second_shift = norm_back(after_self, vectors[2], grad_normed)
     grad_after_self = grad_after_cross + piece
-    grad_after_self, normed_three, grad_hidden = after(grad_after_self, normed_three, grad_hidden)
-    feed_in_blocks = grad_start((normed_three, grad_hidden))
-    cross_parts = outer_start((cross_rows, by_row(crossed)), (normed_two, grad_cross_queries))
+    cross_products = ((cross_rows, by_row(crossed)), (normed_two, grad_cross_queries))
+    cross_parts = outer_swap(cross_products, [], 1)
 
     def text_sum(values, mask):
         arrived = lax.ppermute(values.astype(low), "context", [(i, i ^ mask) for i in range(nc)])
@@ -645,44 +664,61 @@
 
     text_grads = scatter_columns(jnp.stack([by_row(grad_cross_keys), by_row(grad_cross_values)]))
     text_grads = jnp.concatenate([text_grads[0], text_grads[1]], axis=1)
-    mask = 1
-    while 2 * mask < nc:
-        text_grads = text_sum(text_grads, mask)
+    grad_rows = by_row(gather_rows(grad_after_self.astype(low), nt))
+    grad_rows, *feed_out_blocks = after(grad_rows, *feed_out_blocks)
+    feed_out_grad = grad_finish(feed_out_blocks)
+    grad_attended = by_clip(dot(grad_rows, self_out_all, 1, 0).astype(low))
+    head_grad = to_heads(to_chunks(grad_attended, width), own_context, nc)
+    first_back = head_grad[nc - 1]
+    first_back, grad_rows, text_grads, *cross_parts = after(
+        first_back, grad_rows, text_grads, *cross_parts
+    )
+    head_grad[nc - 1] = first_back
+    head_grad = jnp.stack(head_grad)
+    mask = 2
+    while mask < nt:
+        cross_parts = outer_swap(cross_products, cross_parts, mask)
         mask *= 2
-    grad_rows = by_row(gather_rows(grad_after_self.astype(low), nt))
-    grad_rows, text_grads, *feed_out_blocks = after(grad_rows, text_grads, *feed_out_blocks)
-    feed_out_grad = grad_finish(feed_out_blocks)
-    text_grads = text_sum(text_grads, mask)
-
-    grad_attended = by_clip(dot(grad_rows, self_out_all, 1, 0).astype(low))
-    grad_attended, *cross_parts = after(grad_attended, *cross_parts)
-    cross_parts = outer_rest(cross_parts[:2], cross_parts[2])
     self_out_blocks = grad_start((grad_rows, attended))
-    head_grad = to_heads(to_chunks(grad_attended, width), own_context, nc)
-    head_grad, text_grads, feed_out_grad, *feed_in_blocks = after(
-        head_grad, text_grads, feed_out_grad, *feed_in_blocks
-    )
+    head_grad, feed_out_grad, *feed_in_blocks = after(head_grad, feed_out_grad, *feed_in_blocks)
+    feed_out_grad = feed_out_grad.astype(wide)
     feed_in_grad = grad_finish(feed_in_blocks)
-    feed_out_grad = feed_out_grad.astype(wide)
     head_back = self_backward(place, head_rows, head_out, head_top, head_grad, frame_count, order)
-    head_back, *cross_parts = after(head_back, *cross_parts)
-    cross_parts = outer_step(cross_parts[:2], cross_parts[2])
+    head_back, text_grads = after(head_back, text_grads)
+    head_back = to_frames(head_back, own_context, nc)
+    text_mask = 1
+    while 2 * text_mask < nc:
+        text_grads = text_sum(text_grads, text_mask)
+        text_mask *= 2
+    head_back[1], *cross_parts = after(head_back[1], *cross_parts)
 
     def cross_block(index):
-        span = nc * block
-        picked = []
-        for part in cross_parts:
-            chosen = part[:span]
-            for where in range(1, nf):
-                chosen = jnp.where(index == where, part[where * span : (where + 1) * span], chosen)
-            picked.append(chosen)
-        return jnp.concatenate(picked, axis=1)
+        return outer_value(cross_products, cross_parts, 0, columns, index)
 
     cross_blocks = [cross_block(own_fsdp)] + [
         from_fsdp(cross_block(lax.rem(own_fsdp + step, nf)).astype(low), nf - step, nf)
         for step in range(1, nf)
     ]
+    middle_total = [block_sum(cross_blocks).astype(low), block_sum(self_out_blocks).astype(low)]
+    middle_total = jnp.concatenate(middle_total, axis=1)
+    far = nc // 2
+    head_back[far], middle_total, text_grads = after(head_back[far], middle_total, text_grads)
+    text_grads = text_sum(text_grads, text_mask)
+    middle_grad = grad_scatter(middle_total)
+
+    grad_projected = by_row(from_chunks(by_sender(head_back, own_context, nc)))
+    grad_projected, feed_in_grad = after(grad_projected, feed_in_grad)
+    feed_in_grad = feed_in_grad.astype(wide)
+    own, *qkv_blocks = grad_products((normed_one, grad_projected))
+    grad_projected, *qkv_blocks = after(grad_projected, *qkv_blocks)
+    qkv_blocks = exchange([own] + qkv_blocks)
+    grad_normed = scatter_step(by_clip(dot(grad_projected, qkv_all, 1, 1)), 1, nt)
+    grad_normed, middle_grad, text_grads, *qkv_blocks = after(
+        grad_normed, middle_grad, text_grads, *qkv_blocks
+    )
+    qkv_grad = grad_finish(qkv_blocks).astype(wide)
     text_low = text_grads.astype(low)
+
     def text_block(step):
         place = lax.rem(own_fsdp + step, nf) * nc + own_context
         return dot(pick_columns(by_row(text), place, nf * nc), text_low, 0, 0)
@@ -696,26 +732,13 @@
         text_part = text_part + swap_tensor(text_part.astype(low), mask, nt).astype(wide)
         mask *= 2
 
-    grad_projected = by_row(from_chunks(to_frames(head_back, own_context, nc)))
-    count = len(cross_blocks)
-    grad_projected, feed_in_grad, text_part, *moved = after(
-        grad_projected, feed_in_grad, text_part, *cross_blocks, *self_out_blocks, *text_blocks
-    )
-    middle_total = [block_sum(moved[:count]).astype(low), block_sum(moved[count : 2 * count]).astype(low)]
-    middle_grad = grad_scatter(jnp.concatenate(middle_total, axis=1))
-    text_blocks = moved[2 * count :]
+    grad_normed = scatter_rows(grad_normed, nt, 2)
+    grad_normed, active = after(grad_normed, active)
+
+    layer_out = after_cross + scatter_rows(by_clip(dot(active, feed_out_all, 1, 1)), nt)
+    layer_out = layer_out.astype(low).transpose(1, 0, 2)
     key_value_grad = block_sum(text_blocks)
     text_grad = by_clip(text_part).transpose(1, 0, 2)
-    feed_in_grad = feed_in_grad.astype(wide)
-    cut = grad_projected.shape[1] // 256 * 128 + 128
-    early = grad_start((normed_one, grad_projected[:, :cut]))
-    late = grad_start((normed_one, grad_projected[:, cut:]))
-    grad_normed = scatter_step(by_clip(dot(grad_projected, qkv_all, 1, 1)), 1, nt)
-    grad_normed, middle_grad, *early = after(grad_normed, middle_grad, *early)
-    early = grad_finish(early)
-    grad_normed = scatter_rows(grad_normed, nt, 2)
-    grad_normed, *late = after(grad_normed, *late)
-    qkv_grad = jnp.concatenate([early.astype(wide), grad_finish(late).astype(wide)], axis=1)
     middle_grad = middle_grad.astype(wide)
     cross_out_grad = middle_grad[:, :columns]
     cross_query_grad = middle_grad[:, columns : 2 * columns]

time: 759 us -> 743 us (0.979)
  local copies, waits for them, and re-layouts: 67.7 us -> 52.7 us
  other arithmetic: 75.6 us -> 62.1 us
  matrix products: 93.4 us -> 103 us
    all_gather x1, waiting for transfers between devices: 0.02 us -> 32.7 us  [gather_near(): return lax.all_gather(shard, 'context', axis=0, tiled=True)]
    reduce_scatter x5 -> x4, waiting for transfers between devices: 18.2 us -> 4.91 us  [grad_scatter(): return lax.psum_scatter(total, 'context', scatter_dimension=0, tiled=True)]
    add x4 -> x0, other arithmetic: 12.8 us -> none  [the longest x2 10.4 us: outer_step(): part + arrived[:, k * span:(k + 1) * span].astype(wide)]
    ppermute x2, waiting for transfers between devices: 16 us -> 26.3 us  [text_sum(): lax.ppermute(values.astype(low), 'context', [(i, i ^ mask) for i in range...]
    ppermute x17 -> x16, waiting for transfers between devices: 52.7 us -> 43 us  [from_fsdp(): lax.ppermute(values, 'fsdp', [((i + step) % size, i) for i in range(size)])]
    dot_general x30 -> x32, matrix products: 93.4 us -> 103 us  [dot(): lax.dot_general(left, right, (((left_dim,), (right_dim,)), ((), ())), pre...]
    slice x5 -> x0, local copies, waits for them, and re-layouts: 8.94 us -> none  [the longest x2 3.92 us: outer_rest(): far = jnp.concatenate([part[:, half:].astype(low) for part in near], axis=1)]
    unnamed x183 -> x213, local copies, waits for them, and re-layouts: 18.9 us -> 22.8 us
  transfers between devices with their start and end apart: 83 -> 81, of which waited for: 37 -> 35; matrix products, arithmetic and copies ran while one was open for 26% -> 24% of each run, Pallas kernels for 8% -> 9%
where the time goes in v3:
time: 743 us; the launch traced here: 734 us
  waiting for transfers between devices  358 us (48%)
  matrix products  103 us (14%)
  starting transfers between devices  78.4 us (11%)
  Pallas kernels  63.4 us (9%)
  other arithmetic  62.1 us (8%)
  local copies, waits for them, and re-layouts  52.7 us (7%)
  between operations  16.7 us (2%)
    ppermute x21, waiting for transfers between devices, from_context(): lax.ppermute(values, 'context', [((i + step) % size, i) for i in range(si...  178 us
    dot_general x32, matrix products, dot(): lax.dot_general(left, right, (((left_dim,), (right_dim,)), ((), ())), pre...  103 us
    ppermute x34, waiting for transfers between devices, swap_tensor(): return lax.ppermute(values, 'tensor', [(i, i ^ mask) for i in range(size)])  72.8 us
    ppermute x16, waiting for transfers between devices, from_fsdp(): lax.ppermute(values, 'fsdp', [((i + step) % size, i) for i in range(size)])  43 us
    all_gather x1, waiting for transfers between devices, gather_near(): return lax.all_gather(shard, 'context', axis=0, tiled=True)  32.7 us
    ppermute x21, starting transfers between devices, from_context(): lax.ppermute(values, 'context', [((i + step) % size, i) for i in range(si...  32.2 us
    ppermute x2, waiting for transfers between devices, text_sum(): lax.ppermute(values.astype(low), 'context', [(i, i ^ mask) for i in range...  26.3 us
    pallas_call x1, Pallas kernels, self_backward(): pl.pallas_call(functools.partial(self_backward_kernel, frames, order), ou...  24.7 us
  transfers between devices with their start and end apart: 81, of which 35 were waited for; matrix products, arithmetic and copies ran while one was open for 24% of the time, Pallas kernels for 9%

profile of v3, /device:TPU:8, one launch (start us, length us, event | category | flops | bytes accessed | tf_op | source)
XLA Modules:
  0.0 734.2 jit_solution(8457966442322034882)
XLA Ops:
  15.0 4.4 collective-permute-start.5
  27.7 6.3 collective-permute-done.2
  34.8 2.8 collective-permute-done.4
  38.1 3.1 collective-permute-done.6
  43.6 18.0 %collective-permute-done.11 = bf16[192,1152]{1,0:T(8,128)(2,1)S(1)} collective-permute-done((bf16[192,1152]{1,0:T(8,128)(2,1)S(1)}, bf16[192,1152]{1,0:T(8,128)(2,1)S(1)}, u32[]{:S(2)}, u32[]{:S(2)}) %collective-permute-start.11) | collective-permute-done | bytes 442400 | tf_op jit(solution)/shard_map/ppermute | solution.py:25
  63.6 23.5 %collective-permute-done.15 = bf16[192,1152]{1,0:T(8,128)(2,1)S(1)} collective-permute-done((bf16[192,1152]{1,0:T(8,128)(2,1)S(1)}, bf16[192,1152]{1,0:T(8,128)(2,1)S(1)}, u32[]{:S(2)}, u32[]{:S(2)}) %collective-permute-start.15) | collective-permute-done | bytes 442400 | tf_op jit(solution)/shard_map/ppermute | solution.py:25
  93.5 5.5 collective-permute-done.16
  101.5 5.2 convolution_convert_fusion.4
  108.7 32.7 %all-gather.7.cloned.1.call-done = bf16[768,1152]{1,0:T(8,128)(2,1)} async-done(((bf16[192,1152]{1,0:T(8,128)(2,1)}), bf16[768,1152]{1,0:T(8,128)(2,1)}) %all-gather.7.cloned.1.call-update) | async-done | bytes 1769488 | tf_op jit(solution)/shard_map/all_gather | solution.py:480
  147.0 23.2 %collective-permute-done.19 = bf16[384,576]{1,0:T(8,128)(2,1)} collective-permute-done((bf16[384,576]{1,0:T(8,128)(2,1)}, bf16[384,576]{1,0:T(8,128)(2,1)}, u32[]{:S(2)}, u32[]{:S(2)}) %collective-permute-start.19) | collective-permute-done | bytes 442400 | tf_op jit(solution)/shard_map/ppermute | solution.py:25
  170.2 25.5 %collective-permute-done.18 = bf16[384,576]{1,0:T(8,128)(2,1)} collective-permute-done((bf16[384,576]{1,0:T(8,128)(2,1)}, bf16[384,576]{1,0:T(8,128)(2,1)}, u32[]{:S(2)}, u32[]{:S(2)}) %collective-permute-start.18) | collective-permute-done | bytes 442400 | tf_op jit(solution)/shard_map/ppermute | solution.py:25
  199.8 18.0 %shard_map.330 = (bf16[4,384,192]{2,1,0:T(8,128)(2,1)S(1)}, f32[4,3,384]{2,1,0:T(4,128)S(1)}) custom-call(s32[2]{0:T(128)S(1)} %pad_add_fusion.place_ref, bf16[4,384,576]{2,1,0:T(8,128)(2,1)S(1)} %pad_maximum_fusion.9.rows_ref), custom_call_target="tpu_custom_call" | custom-call | flops 1132462080 | bytes 3538944 | tf_op jit(solution)/shard_map/pallas_call | solution.py:311
  221.7 3.4 collective-permute-start.23
  227.1 8.4 %collective-permute-done.24 = bf16[384,192]{1,0:T(8,128)(2,1)S(1)} collective-permute-done((bf16[384,192]{1,0:T(8,128)(2,1)S(1)}, bf16[384,192]{1,0:T(8,128)(2,1)S(1)}, u32[]{:S(2)}, u32[]{:S(2)}) %collective-permute-start.24) | collective-permute-done | bytes 147488 | tf_op jit(solution)/shard_map/ppermute | solution.py:25
  235.5 20.3 %collective-permute-done.23 = bf16[384,192]{1,0:T(8,128)(2,1)S(1)} collective-permute-done((bf16[384,192]{1,0:T(8,128)(2,1)S(1)}, bf16[384,192]{1,0:T(8,128)(2,1)S(1)}, u32[]{:S(2)}, u32[]{:S(2)}) %collective-permute-start.23) | collective-permute-done | bytes 147488 | tf_op jit(solution)/shard_map/ppermute | solution.py:25
  255.8 2.5 collective-permute-done.22
  261.1 2.7 fusion.79
  275.4 20.2 %collective-permute-done.29 = bf16[2,96,1536]{2,1,0:T(8,128)(2,1)S(1)} collective-permute-done((bf16[2,96,1536]{2,1,0:T(8,128)(2,1)S(1)}, bf16[2,96,1536]{2,1,0:T(8,128)(2,1)S(1)}, u32[]{:S(2)}, u32[]{:S(2)}) %collective-permute-start.29) | collective-permute-done | bytes 589856 | tf_op jit(solution)/shard_map/ppermute | solution.py:33
  297.9 3.6 convolution_convert_fusion.7
  301.4 10.0 %shard_map.331 = bf16[2,96,1536]{2,1,0:T(8,128)(2,1)S(1)} custom-call(bf16[2,96,1536]{2,1,0:T(8,128)(2,1)S(1)} %bitcast.264, bf16[2,64,1536]{2,1,0:T(8,128)(2,1)S(1)} %bitcast.256, bf16[2,64,1536]{2,1,0:T(8,128)(2,1)S(1)} %bitcast.258), custom_call_target="tpu_custom_call" | custom-call | flops 75497472 | bytes 1179648 | tf_op jit(solution)/shard_map/pallas_call | solution.py:391
  311.5 3.1 fusion.200
  318.1 13.0 %collective-permute-done.35 = bf16[2,96,1536]{2,1,0:T(8,128)(2,1)} collective-permute-done((bf16[2,96,1536]{2,1,0:T(8,128)(2,1)}, bf16[2,96,1536]{2,1,0:T(8,128)(2,1)}, u32[]{:S(2)}, u32[]{:S(2)}) %collective-permute-start.35) | collective-permute-done | bytes 589856 | tf_op jit(solution)/shard_map/ppermute | solution.py:33
  331.1 3.3 pad_maximum_fusion.4
  334.4 3.1 pad_maximum_fusion.5
  337.6 8.1 %multiply_convert_fusion = (bf16[768,1536]{1,0:T(8,128)(2,1)S(1)}, f32[768,1536]{1,0:T(8,128)}) fusion(bf16[768,1536]{1,0:T(8,128)(2,1)} %bitcast.302, bf16[1536,1536]{1,0:T(8,128)(2,1)} %all-gather.9.cloned.1.call-done), kind=kOutput, calls=%fused_computation.16 | convolution fusion | flops 3629776896 | bytes 14155776 | tf_op jit(solution)/shard_map/dot_general | solution.py:19
  345.7 4.2 fusion.54
  349.9 3.5 convolution_convert_fusion.3
  353.4 7.9 %fusion.5 = bf16[768,1536]{1,0:T(8,128)(2,1)S(1)} fusion(f32[768,1536]{1,0:T(8,128)} %get-tuple-element.275, bf16[768,1536]{1,0:T(8,128)(2,1)} %bitcast.305, bf16[1536,1536]{1,0:T(8,128)(2,1)} %all-gather.11.cloned.1.call-done), kind=kOutput, calls=%fused_computation.6 | convolution fusion | flops 3635675136 | bytes 14155776 | tf_op jit(solution)/shard_map/dot_general | solution.py:19
  361.3 6.1 fusion.202
  372.6 4.2 fusion.51
  378.1 3.5 convolution_convert_fusion.2
  381.6 5.0 collective-permute-done.39
  390.1 3.4 convolution_convert_fusion.6
  393.5 10.8 %shard_map.332 = (bf16[2,96,1536]{2,1,0:T(8,128)(2,1)S(1)}, f32[2,64,1536]{2,1,0:T(8,128)S(1)}, f32[2,64,1536]{2,1,0:T(8,128)S(1)}) custom-call(bf16[2,96,1536]{2,1,0:T(8,128)(2,1)S(1)} %bitcast.265, bf16[2,64,1536]{2,1,0:T(8,128)(2,1)S(1)} %bitcast.257, bf16[2,64,1536]{2,1,0:T(8,128)(2,1)S(1)} %bitcast.259, bf16[2,96,1536]{2,1,0:T(8,128)(2,1)S(1)} %bitcast.270), custom_call_target="tpu_custom_call" | custom-call | flops 188743680 | bytes 2359296 | tf_op jit(solution)/shard_map/pallas_call | solution.py:406
  412.0 11.4 %collective-permute-done.40 = bf16[2,96,1536]{2,1,0:T(8,128)(2,1)S(1)} collective-permute-done((bf16[2,96,1536]{2,1,0:T(8,128)(2,1)S(1)}, bf16[2,96,1536]{2,1,0:T(8,128)(2,1)S(1)}, u32[]{:S(2)}, u32[]{:S(2)}) %collective-permute-start.40) | collective-permute-done | bytes 589856 | tf_op jit(solution)/shard_map/ppermute | solution.py:33
  437.8 4.2 collective-permute-done.48
  442.1 2.7 convolution_convert_fusion.8
  447.2 2.9 collective-permute-start.44
  450.1 18.1 %collective-permute-done.46 = bf16[384,192]{1,0:T(8,128)(2,1)S(1)} collective-permute-done((bf16[384,192]{1,0:T(8,128)(2,1)S(1)}, bf16[384,192]{1,0:T(8,128)(2,1)S(1)}, u32[]{:S(2)}, u32[]{:S(2)}) %collective-permute-start.46) | collective-permute-done | bytes 147488 | tf_op jit(solution)/shard_map/ppermute | solution.py:25
  475.7 9.8 %collective-permute-done.44 = bf16[384,192]{1,0:T(8,128)(2,1)S(1)} collective-permute-done((bf16[384,192]{1,0:T(8,128)(2,1)S(1)}, bf16[384,192]{1,0:T(8,128)(2,1)S(1)}, u32[]{:S(2)}, u32[]{:S(2)}) %collective-permute-start.44) | collective-permute-done | bytes 147488 | tf_op jit(solution)/shard_map/ppermute | solution.py:25
  486.5 3.3 collective-permute-done.50
  489.8 4.9 reduce-scatter.5.cloned.1.call-done
  494.7 5.3 add_convert_fusion
  502.7 24.7 %shard_map.333 = bf16[4,384,576]{2,1,0:T(8,128)(2,1)S(1)} custom-call(s32[2]{0:T(128)S(1)} %pad_add_fusion.place_ref, bf16[4,384,576]{2,1,0:T(8,128)(2,1)S(1)} %copy-done.1, bf16[4,384,192]{2,1,0:T(8,128)(2,1)S(1)} %copy-done.3, f32[4,3,384]{2,1,0:T(4,128)S(1)} %copy-done.8, bf16[4,384,192]{2,1,0:T(8,128)(2,1)S(1)} %copy-done.4), custom_call_target="tpu_custom_call" | custom-call | flops 2831155200 | bytes 7077888 | tf_op jit(solution)/shard_map/pallas_call | solution.py:332
  531.6 24.1 %collective-permute-done.51 = bf16[384,576]{1,0:T(8,128)(2,1)S(1)} collective-permute-done((bf16[384,576]{1,0:T(8,128)(2,1)S(1)}, bf16[384,576]{1,0:T(8,128)(2,1)S(1)}, u32[]{:S(2)}, u32[]{:S(2)}) %collective-permute-start.51) | collective-permute-done | bytes 442400 | tf_op jit(solution)/shard_map/ppermute | solution.py:25
  562.6 4.4 collective-permute-start.53
  567.0 9.6 %collective-permute-done.56 = bf16[128,768]{1,0:T(8,128)(2,1)S(1)} collective-permute-done((bf16[128,768]{1,0:T(8,128)(2,1)S(1)}, bf16[128,768]{1,0:T(8,128)(2,1)S(1)}, u32[]{:S(2)}, u32[]{:S(2)}) %collective-permute-start.56) | collective-permute-done | bytes 196640 | tf_op jit(solution)/shard_map/ppermute | solution.py:662
  580.8 7.2 collective-permute-done.54
  589.6 4.7 collective-permute-done.53
  598.8 4.6 convolution_convert_fusion.5
  603.4 5.6 fusion.203
  613.9 3.4 collective-permute-start.59
  621.8 16.7 %collective-permute-done.59 = bf16[128,768]{1,0:T(8,128)(2,1)S(1)} collective-permute-done((bf16[128,768]{1,0:T(8,128)(2,1)}, bf16[128,768]{1,0:T(8,128)(2,1)S(1)}, u32[]{:S(2)}, u32[]{:S(2)}) %collective-permute-start.59) | collective-permute-done | bytes 196640 | tf_op jit(solution)/shard_map/ppermute | solution.py:662
  640.3 3.6 fusion.42
  644.0 3.2 slice_add_fusion.1
  647.2 6.3 collective-permute-done.60
  657.2 2.8 fusion.201
  662.7 3.1 add_convert_fusion.2
  667.7 3.4 collective-permute-done.66
  677.2 6.8 fusion.204
  688.9 2.9 collective-permute-done.68
  693.1 2.8 collective-permute-done.69
  695.9 3.3 collective-permute-start.72
  711.3 10.0 %collective-permute-done.63 = bf16[2,96,1536]{2,1,0:T(8,128)(2,1)S(1)} collective-permute-done((bf16[2,96,1536]{2,1,0:T(8,128)(2,1)S(1)}, bf16[2,96,1536]{2,1,0:T(8,128)(2,1)S(1)}, u32[]{:S(2)}, u32[]{:S(2)}) %collective-permute-start.63) | collective-permute-done | bytes 589856 | tf_op jit(solution)/shard_map/ppermute | solution.py:33
  (520 shorter events, 183.4 us)
Async XLA Ops:
  7.3 92.7 %all-gather.5.cloned.1.call-start = ((), (), s32[]{:S(2)}) async-start(), calls=%async_computation.4 | async-start | bytes 2654208 | tf_op jit(solution)/shard_map/all_gather | solution.py:492
  9.2 132.1 %all-gather.7.cloned.1.call-start = ((), (), s32[]{:S(2)}) async-start(), calls=%async_computation.5 | async-start | bytes 2211840 | tf_op jit(solution)/shard_map/all_gather | solution.py:480
  11.2 326.3 %all-gather.9.cloned.1.call-start = ((), (), s32[]{:S(2)}) async-start(), calls=%async_computation.6 | async-start | bytes 5308416 | tf_op jit(solution)/shard_map/all_gather | solution.py:492
  11.4 12.8 %collective-permute-start = (bf16[8,192]{1,0:T(8,128)(2,1)S(1)}, bf16[8,192]{1,0:T(8,128)(2,1)S(1)}, u32[]{:S(2)}, u32[]{:S(2)}) collective-permute-start(bf16[8,192]{1,0:T(8,128)(2,1)S(1)} %stack.147), channel_id=1, source_target_pairs={{16,0},{0,16},{17,1},{1,17},{18,2},{2,18},{19,3},{3,19},{20,4},{4,... | collective-permute-start | bytes 9224 | tf_op jit(solution)/shard_map/ppermute | solution.py:29
  13.0 11.2 %collective-permute-start.1 = (bf16[8,192]{1,0:T(8,128)(2,1)S(1)}, bf16[8,192]{1,0:T(8,128)(2,1)S(1)}, u32[]{:S(2)}, u32[]{:S(2)}) collective-permute-start(bf16[8,192]{1,0:T(8,128)(2,1)S(1)} %stack.147), channel_id=1, source_target_pairs={{4,0},{8,4},{12,8},{0,12},{5,1},{9,5},{13,9},{1,13},{6,2},{10,6},{... | collective-permute-start | bytes 9224 | tf_op jit(solution)/shard_map/ppermute | solution.py:25
  13.5 12.3 %collective-permute-start.3 = (bf16[8,192]{1,0:T(8,128)(2,1)S(1)}, bf16[8,192]{1,0:T(8,128)(2,1)S(1)}, u32[]{:S(2)}, u32[]{:S(2)}) collective-permute-start(bf16[8,192]{1,0:T(8,128)(2,1)S(1)} %stack.147), channel_id=1, source_target_pairs={{12,0},{0,4},{4,8},{8,12},{13,1},{1,5},{5,9},{9,13},{14,2},{2,6},{... | collective-permute-start | bytes 9224 | tf_op jit(solution)/shard_map/ppermute | solution.py:25
  15.0 19.5 %collective-permute-start.5 = (bf16[8,192]{1,0:T(8,128)(2,1)S(1)}, bf16[8,192]{1,0:T(8,128)(2,1)S(1)}, u32[]{:S(2)}, u32[]{:S(2)}) collective-permute-start(bf16[8,192]{1,0:T(8,128)(2,1)S(1)} %stack.147), channel_id=1, source_target_pairs={{8,0},{12,4},{0,8},{4,12},{9,1},{13,5},{1,9},{5,13},{10,2},{14,6},... | collective-permute-start | bytes 9224 | tf_op jit(solution)/shard_map/ppermute | solution.py:25
  19.9 23.6 %collective-permute-start.10 = (bf16[192,1152]{1,0:T(8,128)(2,1)S(1)}, bf16[192,1152]{1,0:T(8,128)(2,1)S(1)}, u32[]{:S(2)}, u32[]{:S(2)}) collective-permute-start(bf16[192,1152]{1,0:T(8,128)(2,1)S(1)} %concatenate.81), channel_id=1, source_target_pairs={{16,0},{0,16},{17,1},{1,17},{18,2},{2,18},{19,3},{3,19},{20,4},{4,... | collective-permute-start | bytes 1327112 | tf_op jit(solution)/shard_map/ppermute | solution.py:29
  20.5 332.9 %all-gather.11.cloned.1.call-start = ((), (), s32[]{:S(2)}) async-start(), calls=%async_computation.7 | async-start | bytes 5308416 | tf_op jit(solution)/shard_map/all_gather | solution.py:492
  24.2 37.3 %collective-permute-start.11 = (bf16[192,1152]{1,0:T(8,128)(2,1)S(1)}, bf16[192,1152]{1,0:T(8,128)(2,1)S(1)}, u32[]{:S(2)}, u32[]{:S(2)}) collective-permute-start(bf16[192,1152]{1,0:T(8,128)(2,1)S(1)} %concatenate.81), channel_id=1, source_target_pairs={{4,0},{8,4},{12,8},{0,12},{5,1},{9,5},{13,9},{1,13},{6,2},{10,6},{... | collective-permute-start | bytes 1327112 | tf_op jit(solution)/shard_map/ppermute | solution.py:25
  25.8 35.8 %collective-permute-start.13 = (bf16[192,1152]{1,0:T(8,128)(2,1)S(1)}, bf16[192,1152]{1,0:T(8,128)(2,1)S(1)}, u32[]{:S(2)}, u32[]{:S(2)}) collective-permute-start(bf16[192,1152]{1,0:T(8,128)(2,1)S(1)} %concatenate.81), channel_id=1, source_target_pairs={{12,0},{0,4},{4,8},{8,12},{13,1},{1,5},{5,9},{9,13},{14,2},{2,6},{... | collective-permute-start | bytes 1327112 | tf_op jit(solution)/shard_map/ppermute | solution.py:25
  34.5 52.6 %collective-permute-start.15 = (bf16[192,1152]{1,0:T(8,128)(2,1)S(1)}, bf16[192,1152]{1,0:T(8,128)(2,1)S(1)}, u32[]{:S(2)}, u32[]{:S(2)}) collective-permute-start(bf16[192,1152]{1,0:T(8,128)(2,1)S(1)} %concatenate.81), channel_id=1, source_target_pairs={{8,0},{12,4},{0,8},{4,12},{9,1},{13,5},{1,9},{5,13},{10,2},{14,6},... | collective-permute-start | bytes 1327112 | tf_op jit(solution)/shard_map/ppermute | solution.py:25
  42.0 48.2 %collective-permute-start.7 = (bf16[2,96,1536]{2,1,0:T(8,128)(2,1)S(1)}, bf16[2,96,1536]{2,1,0:T(8,128)(2,1)S(1)}, u32[]{:S(2)}, u32[]{:S(2)}) collective-permute-start(bf16[2,96,1536]{2,1,0:T(8,128)(2,1)S(1)} %fusion.34), channel_id=1, source_target_pairs={{0,2},{1,3},{2,0},{3,1},{4,6},{5,7},{6,4},{7,5},{8,10},{9,11},{10,... | collective-permute-start | bytes 1769480 | tf_op jit(solution)/shard_map/ppermute | solution.py:33
  43.6 56.2 %collective-permute-start.8 = (bf16[2,96,1536]{2,1,0:T(8,128)(2,1)S(1)}, bf16[2,96,1536]{2,1,0:T(8,128)(2,1)S(1)}, u32[]{:S(2)}, u32[]{:S(2)}) collective-permute-start(bf16[2,96,1536]{2,1,0:T(8,128)(2,1)S(1)} %fusion.34), channel_id=1, source_target_pairs={{0,1},{1,0},{2,3},{3,2},{4,5},{5,4},{6,7},{7,6},{8,9},{9,8},{10,11... | collective-permute-start | bytes 1769480 | tf_op jit(solution)/shard_map/ppermute | solution.py:33
  61.6 28.7 %collective-permute-start.12 = (bf16[192,1152]{1,0:T(8,128)(2,1)S(1)}, bf16[192,1152]{1,0:T(8,128)(2,1)S(1)}, u32[]{:S(2)}, u32[]{:S(2)}) collective-permute-start(bf16[192,1152]{1,0:T(8,128)(2,1)S(1)} %collective-permute-done.11), channel_id=1, source_target_pairs={{16,0},{0,16},{17,1},{1,17},{18,2},{2,18},{19,3},{3,19},{20,4},{4,... | collective-permute-start | bytes 1327112 | tf_op jit(solution)/shard_map/ppermute | solution.py:29
  61.6 30.3 %collective-permute-start.14 = (bf16[192,1152]{1,0:T(8,128)(2,1)S(1)}, bf16[192,1152]{1,0:T(8,128)(2,1)S(1)}, u32[]{:S(2)}, u32[]{:S(2)}) collective-permute-start(bf16[192,1152]{1,0:T(8,128)(2,1)S(1)} %collective-permute-done.13), channel_id=1, source_target_pairs={{16,0},{0,16},{17,1},{1,17},{18,2},{2,18},{19,3},{3,19},{20,4},{4,... | collective-permute-start | bytes 1327112 | tf_op jit(solution)/shard_map/ppermute | solution.py:29
  87.1 11.9 %collective-permute-start.16 = (bf16[192,1152]{1,0:T(8,128)(2,1)S(1)}, bf16[192,1152]{1,0:T(8,128)(2,1)S(1)}, u32[]{:S(2)}, u32[]{:S(2)}) collective-permute-start(bf16[192,1152]{1,0:T(8,128)(2,1)S(1)} %collective-permute-done.15), channel_id=1, source_target_pairs={{16,0},{0,16},{17,1},{1,17},{18,2},{2,18},{19,3},{3,19},{20,4},{4,... | collective-permute-start | bytes 1327112 | tf_op jit(solution)/shard_map/ppermute | solution.py:29
  100.0 99.8 %collective-permute-start.20 = (bf16[1536,768]{1,0:T(8,128)(2,1)}, bf16[1536,768]{1,0:T(8,128)(2,1)}, u32[]{:S(2)}, u32[]{:S(2)}) collective-permute-start(bf16[1536,768]{1,0:T(8,128)(2,1)} %all-gather.5.cloned.1.call-done), channel_id=1, source_target_pairs={{0,2},{1,3},{2,0},{3,1},{4,6},{5,7},{6,4},{7,5},{8,10},{9,11},{10,... | collective-permute-start | bytes 7077896 | tf_op jit(solution)/shard_map/ppermute | solution.py:33
  108.7 32.7 %collective-permute-start.17 = (bf16[384,576]{1,0:T(8,128)(2,1)S(1)}, bf16[384,576]{1,0:T(8,128)(2,1)}, u32[]{:S(2)}, u32[]{:S(2)}) collective-permute-start(bf16[384,576]{1,0:T(8,128)(2,1)S(1)} %get-tuple-element.216), channel_id=1, source_target_pairs={{12,0},{0,4},{4,8},{8,12},{13,1},{1,5},{5,9},{9,13},{14,2},{2,6},{... | collective-permute-start | bytes 1327112 | tf_op jit(solution)/shard_map/ppermute | solution.py:25
  141.4 76.5 %collective-permute-start.21 = (bf16[768,1152]{1,0:T(8,128)(2,1)}, bf16[768,1152]{1,0:T(8,128)(2,1)S(1)}, u32[]{:S(2)}, u32[]{:S(2)}) collective-permute-start(bf16[768,1152]{1,0:T(8,128)(2,1)} %all-gather.7.cloned.1.call-done), channel_id=1, source_target_pairs={{16,0},{0,16},{17,1},{1,17},{18,2},{2,18},{19,3},{3,19},{20,4},{4,... | collective-permute-start | bytes 5308424 | tf_op jit(solution)/shard_map/ppermute | solution.py:29
  142.8 27.3 %collective-permute-start.19 = (bf16[384,576]{1,0:T(8,128)(2,1)}, bf16[384,576]{1,0:T(8,128)(2,1)}, u32[]{:S(2)}, u32[]{:S(2)}) collective-permute-start(bf16[384,576]{1,0:T(8,128)(2,1)} %get-tuple-element.214), channel_id=1, source_target_pairs={{4,0},{8,4},{12,8},{0,12},{5,1},{9,5},{13,9},{1,13},{6,2},{10,6},{... | collective-permute-start | bytes 1327112 | tf_op jit(solution)/shard_map/ppermute | solution.py:25
  144.6 51.0 %collective-permute-start.18 = (bf16[384,576]{1,0:T(8,128)(2,1)}, bf16[384,576]{1,0:T(8,128)(2,1)}, u32[]{:S(2)}, u32[]{:S(2)}) collective-permute-start(bf16[384,576]{1,0:T(8,128)(2,1)} %get-tuple-element.215), channel_id=1, source_target_pairs={{8,0},{12,4},{0,8},{4,12},{9,1},{13,5},{1,9},{5,13},{10,2},{14,6},... | collective-permute-start | bytes 1327112 | tf_op jit(solution)/shard_map/ppermute | solution.py:25
  219.9 39.2 %collective-permute-start.25 = (bf16[128,768]{0,1:T(8,128)(2,1)S(1)}, bf16[128,768]{0,1:T(8,128)(2,1)S(1)}, u32[]{:S(2)}, u32[]{:S(2)}) collective-permute-start(bf16[128,768]{0,1:T(8,128)(2,1)S(1)} %fusion.67), channel_id=1, source_target_pairs={{0,2},{1,3},{2,0},{3,1},{4,6},{5,7},{6,4},{7,5},{8,10},{9,11},{10,... | collective-permute-start | bytes 589832 | tf_op jit(solution)/shard_map/ppermute | solution.py:33
  221.6 37.6 %collective-permute-start.26 = (bf16[128,768]{0,1:T(8,128)(2,1)S(1)}, bf16[128,768]{0,1:T(8,128)(2,1)S(1)}, u32[]{:S(2)}, u32[]{:S(2)}) collective-permute-start(bf16[128,768]{0,1:T(8,128)(2,1)S(1)} %fusion.67), channel_id=1, source_target_pairs={{0,1},{1,0},{2,3},{3,2},{4,5},{5,4},{6,7},{7,6},{8,9},{9,8},{10,11... | collective-permute-start | bytes 589832 | tf_op jit(solution)/shard_map/ppermute | solution.py:33
  221.7 13.8 %collective-permute-start.24 = (bf16[384,192]{1,0:T(8,128)(2,1)S(1)}, bf16[384,192]{1,0:T(8,128)(2,1)S(1)}, u32[]{:S(2)}, u32[]{:S(2)}) collective-permute-start(bf16[384,192]{1,0:T(8,128)(2,1)S(1)} %get-tuple-element.230), channel_id=1, source_target_pairs={{12,0},{0,4},{4,8},{8,12},{13,1},{1,5},{5,9},{9,13},{14,2},{2,6},{... | collective-permute-start | bytes 442376 | tf_op jit(solution)/shard_map/ppermute | solution.py:25
  221.7 34.1 %collective-permute-start.23 = (bf16[384,192]{1,0:T(8,128)(2,1)S(1)}, bf16[384,192]{1,0:T(8,128)(2,1)S(1)}, u32[]{:S(2)}, u32[]{:S(2)}) collective-permute-start(bf16[384,192]{1,0:T(8,128)(2,1)S(1)} %get-tuple-element.231), channel_id=1, source_target_pairs={{8,0},{12,4},{0,8},{4,12},{9,1},{13,5},{1,9},{5,13},{10,2},{14,6},... | collective-permute-start | bytes 442376 | tf_op jit(solution)/shard_map/ppermute | solution.py:25
  225.2 33.1 %collective-permute-start.22 = (bf16[384,192]{1,0:T(8,128)(2,1)S(1)}, bf16[384,192]{1,0:T(8,128)(2,1)S(1)}, u32[]{:S(2)}, u32[]{:S(2)}) collective-permute-start(bf16[384,192]{1,0:T(8,128)(2,1)S(1)} %get-tuple-element.232), channel_id=1, source_target_pairs={{4,0},{8,4},{12,8},{0,12},{5,1},{9,5},{13,9},{1,13},{6,2},{10,6},{... | collective-permute-start | bytes 442376 | tf_op jit(solution)/shard_map/ppermute | solution.py:25
  267.2 50.4 %collective-permute-start.32 = (bf16[2,96,1536]{2,1,0:T(8,128)(2,1)}, bf16[2,96,1536]{2,1,0:T(8,128)(2,1)}, u32[]{:S(2)}, u32[]{:S(2)}) collective-permute-start(bf16[2,96,1536]{2,1,0:T(8,128)(2,1)} %bitcast.252), channel_id=1, source_target_pairs={{0,2},{1,3},{2,0},{3,1},{4,6},{5,7},{6,4},{7,5},{8,10},{9,11},{10,... | collective-permute-start | bytes 1769480 | tf_op jit(solution)/shard_map/ppermute | solution.py:33
  268.7 226.0 %reduce-scatter.5.cloned.1.call-start = ((), (), s32[]{:S(2)}) async-start(), calls=%async_computation.8 | async-start | bytes 2949120 | tf_op jit(solution)/shard_map/reduce_scatter | solution.py:581
  269.1 27.4 %collective-permute-start.31 = (bf16[1536,768]{1,0:T(8,128)(2,1)}, bf16[1536,768]{1,0:T(8,128)(2,1)S(1)}, u32[]{:S(2)}, u32[]{:S(2)}) collective-permute-start(bf16[1536,768]{1,0:T(8,128)(2,1)} %collective-permute-done.20), channel_id=1, source_target_pairs={{0,1},{1,0},{2,3},{3,2},{4,5},{5,4},{6,7},{7,6},{8,9},{9,8},{10,11... | collective-permute-start | bytes 7077896 | tf_op jit(solution)/shard_map/ppermute | solution.py:33
  271.5 24.1 %collective-permute-start.29 = (bf16[2,96,1536]{2,1,0:T(8,128)(2,1)S(1)}, bf16[2,96,1536]{2,1,0:T(8,128)(2,1)S(1)}, u32[]{:S(2)}, u32[]{:S(2)}) collective-permute-start(bf16[2,96,1536]{2,1,0:T(8,128)(2,1)S(1)} %slice.906), channel_id=1, source_target_pairs={{0,2},{1,3},{2,0},{3,1},{4,6},{5,7},{6,4},{7,5},{8,10},{9,11},{10,... | collective-permute-start | bytes 1769480 | tf_op jit(solution)/shard_map/ppermute | solution.py:33
  275.1 21.8 %collective-permute-start.30 = (bf16[1536,768]{1,0:T(8,128)(2,1)S(1)}, bf16[1536,768]{1,0:T(8,128)(2,1)S(1)}, u32[]{:S(2)}, u32[]{:S(2)}) collective-permute-start(bf16[1536,768]{1,0:T(8,128)(2,1)S(1)} %copy-done.32), channel_id=1, source_target_pairs={{0,1},{1,0},{2,3},{3,2},{4,5},{5,4},{6,7},{7,6},{8,9},{9,8},{10,11... | collective-permute-start | bytes 7077896 | tf_op jit(solution)/shard_map/ppermute | solution.py:33
  316.0 15.1 %collective-permute-start.35 = (bf16[2,96,1536]{2,1,0:T(8,128)(2,1)}, bf16[2,96,1536]{2,1,0:T(8,128)(2,1)}, u32[]{:S(2)}, u32[]{:S(2)}) collective-permute-start(bf16[2,96,1536]{2,1,0:T(8,128)(2,1)} %add_convert_fusion.6), channel_id=1, source_target_pairs={{0,2},{1,3},{2,0},{3,1},{4,6},{5,7},{6,4},{7,5},{8,10},{9,11},{10,... | collective-permute-start | bytes 1769480 | tf_op jit(solution)/shard_map/ppermute | solution.py:33
  317.5 13.5 %collective-permute-start.33 = (bf16[2,96,1536]{2,1,0:T(8,128)(2,1)}, bf16[2,96,1536]{2,1,0:T(8,128)(2,1)}, u32[]{:S(2)}, u32[]{:S(2)}) collective-permute-start(bf16[2,96,1536]{2,1,0:T(8,128)(2,1)} %bitcast.252), channel_id=1, source_target_pairs={{0,1},{1,0},{2,3},{3,2},{4,5},{5,4},{6,7},{7,6},{8,9},{9,8},{10,11... | collective-permute-start | bytes 1769480 | tf_op jit(solution)/shard_map/ppermute | solution.py:33
  317.5 13.5 %collective-permute-start.34 = (bf16[2,96,1536]{2,1,0:T(8,128)(2,1)}, bf16[2,96,1536]{2,1,0:T(8,128)(2,1)}, u32[]{:S(2)}, u32[]{:S(2)}) collective-permute-start(bf16[2,96,1536]{2,1,0:T(8,128)(2,1)} %collective-permute-done.32), channel_id=1, source_target_pairs={{0,1},{1,0},{2,3},{3,2},{4,5},{5,4},{6,7},{7,6},{8,9},{9,8},{10,11... | collective-permute-start | bytes 1769480 | tf_op jit(solution)/shard_map/ppermute | solution.py:33
  318.1 16.4 %collective-permute-start.36 = (bf16[2,96,1536]{2,1,0:T(8,128)(2,1)}, bf16[2,96,1536]{2,1,0:T(8,128)(2,1)}, u32[]{:S(2)}, u32[]{:S(2)}) collective-permute-start(bf16[2,96,1536]{2,1,0:T(8,128)(2,1)} %add_convert_fusion.6), channel_id=1, source_target_pairs={{0,1},{1,0},{2,3},{3,2},{4,5},{5,4},{6,7},{7,6},{8,9},{9,8},{10,11... | collective-permute-start | bytes 1769480 | tf_op jit(solution)/shard_map/ppermute | solution.py:33
  370.9 15.7 %collective-permute-start.39 = (bf16[2,96,1536]{2,1,0:T(8,128)(2,1)S(1)}, bf16[2,96,1536]{2,1,0:T(8,128)(2,1)S(1)}, u32[]{:S(2)}, u32[]{:S(2)}) collective-permute-start(bf16[2,96,1536]{2,1,0:T(8,128)(2,1)S(1)} %slice.905), channel_id=1, source_target_pairs={{0,2},{1,3},{2,0},{3,1},{4,6},{5,7},{6,4},{7,5},{8,10},{9,11},{10,... | collective-permute-start | bytes 1769480 | tf_op jit(solution)/shard_map/ppermute | solution.py:33
  376.8 53.5 %collective-permute-start.43 = (bf16[768,1536]{1,0:T(8,128)(2,1)}, bf16[768,1536]{1,0:T(8,128)(2,1)S(1)}, u32[]{:S(2)}, u32[]{:S(2)}) collective-permute-start(bf16[768,1536]{1,0:T(8,128)(2,1)} %convolution_convert_fusion.3), channel_id=1, source_target_pairs={{16,0},{0,16},{17,1},{1,17},{18,2},{2,18},{19,3},{3,19},{20,4},{4,... | collective-permute-start | bytes 7077896 | tf_op jit(solution)/shard_map/ppermute | solution.py:29
  408.7 14.7 %collective-permute-start.40 = (bf16[2,96,1536]{2,1,0:T(8,128)(2,1)S(1)}, bf16[2,96,1536]{2,1,0:T(8,128)(2,1)S(1)}, u32[]{:S(2)}, u32[]{:S(2)}) collective-permute-start(bf16[2,96,1536]{2,1,0:T(8,128)(2,1)S(1)} %get-tuple-element.191), channel_id=1, source_target_pairs={{0,2},{1,3},{2,0},{3,1},{4,6},{5,7},{6,4},{7,5},{8,10},{9,11},{10,... | collective-permute-start | bytes 1769480 | tf_op jit(solution)/shard_map/ppermute | solution.py:33
  410.2 16.1 %collective-permute-start.41 = (bf16[2,96,1536]{2,1,0:T(8,128)(2,1)S(1)}, bf16[2,96,1536]{2,1,0:T(8,128)(2,1)S(1)}, u32[]{:S(2)}, u32[]{:S(2)}) collective-permute-start(bf16[2,96,1536]{2,1,0:T(8,128)(2,1)S(1)} %get-tuple-element.191), channel_id=1, source_target_pairs={{0,1},{1,0},{2,3},{3,2},{4,5},{5,4},{6,7},{7,6},{8,9},{9,8},{10,11... | collective-permute-start | bytes 1769480 | tf_op jit(solution)/shard_map/ppermute | solution.py:33
  425.9 42.4 %collective-permute-start.49 = (bf16[1536,1536]{1,0:T(8,128)(2,1)}, bf16[1536,1536]{1,0:T(8,128)(2,1)}, u32[]{:S(2)}, u32[]{:S(2)}) collective-permute-start(bf16[1536,1536]{1,0:T(8,128)(2,1)} %pad_maximum_fusion.2), channel_id=1, source_target_pairs={{0,1},{1,0},{2,3},{3,2},{4,5},{5,4},{6,7},{7,6},{8,9},{9,8},{10,11... | collective-permute-start | bytes 14155784 | tf_op jit(solution)/shard_map/ppermute | solution.py:33
  432.4 166.2 %reduce-scatter.7.cloned.1.call-start = ((), (), s32[]{:S(2)}) async-start(), calls=%async_computation.9 | async-start | bytes 2949120 | tf_op jit(solution)/shard_map/reduce_scatter | solution.py:581
  436.4 53.4 %collective-permute-start.50 = (bf16[768,1536]{1,0:T(8,128)(2,1)S(1)}, bf16[768,1536]{1,0:T(8,128)(2,1)}, u32[]{:S(2)}, u32[]{:S(2)}) collective-permute-start(bf16[768,1536]{1,0:T(8,128)(2,1)S(1)} %copy-done.91), channel_id=1, source_target_pairs={{16,0},{0,16},{17,1},{1,17},{18,2},{2,18},{19,3},{3,19},{20,4},{4,... | collective-permute-start | bytes 7077896 | tf_op jit(solution)/shard_map/ppermute | solution.py:29
  445.2 23.0 %collective-permute-start.46 = (bf16[384,192]{1,0:T(8,128)(2,1)S(1)}, bf16[384,192]{1,0:T(8,128)(2,1)S(1)}, u32[]{:S(2)}, u32[]{:S(2)}) collective-permute-start(bf16[384,192]{1,0:T(8,128)(2,1)S(1)} %get-tuple-element.220), channel_id=1, source_target_pairs={{4,0},{8,4},{12,8},{0,12},{5,1},{9,5},{13,9},{1,13},{6,2},{10,6},{... | collective-permute-start | bytes 442376 | tf_op jit(solution)/shard_map/ppermute | solution.py:25
  446.1 29.6 %collective-permute-start.45 = (bf16[384,192]{1,0:T(8,128)(2,1)S(1)}, bf16[384,192]{1,0:T(8,128)(2,1)S(1)}, u32[]{:S(2)}, u32[]{:S(2)}) collective-permute-start(bf16[384,192]{1,0:T(8,128)(2,1)S(1)} %get-tuple-element.221), channel_id=1, source_target_pairs={{8,0},{12,4},{0,8},{4,12},{9,1},{13,5},{1,9},{5,13},{10,2},{14,6},... | collective-permute-start | bytes 442376 | tf_op jit(solution)/shard_map/ppermute | solution.py:25
  447.2 38.2 %collective-permute-start.44 = (bf16[384,192]{1,0:T(8,128)(2,1)S(1)}, bf16[384,192]{1,0:T(8,128)(2,1)S(1)}, u32[]{:S(2)}, u32[]{:S(2)}) collective-permute-start(bf16[384,192]{1,0:T(8,128)(2,1)S(1)} %get-tuple-element.222), channel_id=1, source_target_pairs={{12,0},{0,4},{4,8},{8,12},{13,1},{1,5},{5,9},{9,13},{14,2},{2,6},{... | collective-permute-start | bytes 442376 | tf_op jit(solution)/shard_map/ppermute | solution.py:25
  473.7 82.0 %collective-permute-start.52 = (bf16[1536,768]{1,0:T(8,128)(2,1)}, bf16[1536,768]{1,0:T(8,128)(2,1)}, u32[]{:S(2)}, u32[]{:S(2)}) collective-permute-start(bf16[1536,768]{1,0:T(8,128)(2,1)} %pad_maximum_fusion.7), channel_id=1, source_target_pairs={{0,2},{1,3},{2,0},{3,1},{4,6},{5,7},{6,4},{7,5},{8,10},{9,11},{10,... | collective-permute-start | bytes 7077896 | tf_op jit(solution)/shard_map/ppermute | solution.py:33
  500.1 147.1 %reduce-scatter.9.cloned.1.call-start = ((), (), s32[]{:S(2)}) async-start(), calls=%async_computation.10 | async-start | bytes 2211840 | tf_op jit(solution)/shard_map/reduce_scatter | solution.py:581
  527.6 28.1 %collective-permute-start.51 = (bf16[384,576]{1,0:T(8,128)(2,1)S(1)}, bf16[384,576]{1,0:T(8,128)(2,1)S(1)}, u32[]{:S(2)}, u32[]{:S(2)}) collective-permute-start(bf16[384,576]{1,0:T(8,128)(2,1)S(1)} %get-tuple-element.212), channel_id=1, source_target_pairs={{4,0},{8,4},{12,8},{0,12},{5,1},{9,5},{13,9},{1,13},{6,2},{10,6},{... | collective-permute-start | bytes 1327112 | tf_op jit(solution)/shard_map/ppermute | solution.py:25
  530.1 31.6 %collective-permute-start.55 = (bf16[768,384]{1,0:T(8,128)(2,1)S(1)}, bf16[768,384]{1,0:T(8,128)(2,1)S(1)}, u32[]{:S(2)}, u32[]{:S(2)}) collective-permute-start(bf16[768,384]{1,0:T(8,128)(2,1)S(1)} %convolution_convert_fusion.9), channel_id=1, source_target_pairs={{16,0},{0,16},{17,1},{1,17},{18,2},{2,18},{19,3},{3,19},{20,4},{4,... | collective-permute-start | bytes 1769480 | tf_op jit(solution)/shard_map/ppermute | solution.py:29
  560.1 27.9 %collective-permute-start.54 = (bf16[768,768]{1,0:T(8,128)(2,1)S(1)}, bf16[768,768]{1,0:T(8,128)(2,1)S(1)}, u32[]{:S(2)}, u32[]{:S(2)}) collective-permute-start(bf16[768,768]{1,0:T(8,128)(2,1)S(1)} %pad_maximum_fusion.14), channel_id=1, source_target_pairs={{16,0},{0,16},{17,1},{1,17},{18,2},{2,18},{19,3},{3,19},{20,4},{4,... | collective-permute-start | bytes 3538952 | tf_op jit(solution)/shard_map/ppermute | solution.py:29
  561.6 15.0 %collective-permute-start.56 = (bf16[128,768]{1,0:T(8,128)(2,1)S(1)}, bf16[128,768]{1,0:T(8,128)(2,1)S(1)}, u32[]{:S(2)}, u32[]{:S(2)}) collective-permute-start(bf16[128,768]{1,0:T(8,128)(2,1)S(1)} %convert_element_type.261), channel_id=1, source_target_pairs={{0,4},{4,0},{8,12},{12,8},{1,5},{5,1},{9,13},{13,9},{2,6},{6,2},{1... | collective-permute-start | bytes 589832 | tf_op jit(solution)/shard_map/ppermute | solution.py:662
  562.6 31.7 %collective-permute-start.57 = (bf16[384,576]{1,0:T(8,128)(2,1)S(1)}, bf16[384,576]{1,0:T(8,128)(2,1)S(1)}, u32[]{:S(2)}, u32[]{:S(2)}) collective-permute-start(bf16[384,576]{1,0:T(8,128)(2,1)S(1)} %get-tuple-element.210), channel_id=1, source_target_pairs={{12,0},{0,4},{4,8},{8,12},{13,1},{1,5},{5,9},{9,13},{14,2},{2,6},{... | collective-permute-start | bytes 1327112 | tf_op jit(solution)/shard_map/ppermute | solution.py:25
  562.6 31.7 %collective-permute-start.53 = (bf16[384,576]{1,0:T(8,128)(2,1)S(1)}, bf16[384,576]{1,0:T(8,128)(2,1)}, u32[]{:S(2)}, u32[]{:S(2)}) collective-permute-start(bf16[384,576]{1,0:T(8,128)(2,1)S(1)} %get-tuple-element.211), channel_id=1, source_target_pairs={{8,0},{12,4},{0,8},{4,12},{9,1},{13,5},{1,9},{5,13},{10,2},{14,6},... | collective-permute-start | bytes 1327112 | tf_op jit(solution)/shard_map/ppermute | solution.py:25
  595.9 127.1 %reduce-scatter.11.cloned.1.call-start = ((), (), s32[]{:S(2)}) async-start(), calls=%async_computation.11 | async-start | bytes 2211840 | tf_op jit(solution)/shard_map/reduce_scatter | solution.py:581
  612.2 31.7 %collective-permute-start.58 = (bf16[2,192,1536]{2,1,0:T(8,128)(2,1)}, bf16[2,192,1536]{2,1,0:T(8,128)(2,1)}, u32[]{:S(2)}, u32[]{:S(2)}) collective-permute-start(bf16[2,192,1536]{2,1,0:T(8,128)(2,1)} %slice.900), channel_id=1, source_target_pairs={{0,1},{1,0},{2,3},{3,2},{4,5},{5,4},{6,7},{7,6},{8,9},{9,8},{10,11... | collective-permute-start | bytes 3538952 | tf_op jit(solution)/shard_map/ppermute | solution.py:33
  612.2 41.3 %collective-permute-start.60 = (bf16[768,1152]{1,0:T(8,128)(2,1)}, bf16[768,1152]{1,0:T(8,128)(2,1)}, u32[]{:S(2)}, u32[]{:S(2)}) collective-permute-start(bf16[768,1152]{1,0:T(8,128)(2,1)} %convolution_convert_fusion.5), channel_id=1, source_target_pairs={{16,0},{0,16},{17,1},{1,17},{18,2},{2,18},{19,3},{3,19},{20,4},{4,... | collective-permute-start | bytes 5308424 | tf_op jit(solution)/shard_map/ppermute | solution.py:29
  613.9 24.5 %collective-permute-start.59 = (bf16[128,768]{1,0:T(8,128)(2,1)}, bf16[128,768]{1,0:T(8,128)(2,1)S(1)}, u32[]{:S(2)}, u32[]{:S(2)}) collective-permute-start(bf16[128,768]{1,0:T(8,128)(2,1)} %convert_element_type.267), channel_id=1, source_target_pairs={{0,8},{4,12},{8,0},{12,4},{1,9},{5,13},{9,1},{13,5},{2,10},{6,14},... | collective-permute-start | bytes 589832 | tf_op jit(solution)/shard_map/ppermute | solution.py:662
  655.7 19.4 %collective-permute-start.61 = (bf16[2,96,1536]{2,1,0:T(8,128)(2,1)}, bf16[2,96,1536]{2,1,0:T(8,128)(2,1)}, u32[]{:S(2)}, u32[]{:S(2)}) collective-permute-start(bf16[2,96,1536]{2,1,0:T(8,128)(2,1)} %slice.904), channel_id=1, source_target_pairs={{0,2},{1,3},{2,0},{3,1},{4,6},{5,7},{6,4},{7,5},{8,10},{9,11},{10,... | collective-permute-start | bytes 1769480 | tf_op jit(solution)/shard_map/ppermute | solution.py:33
  660.0 13.4 %collective-permute-start.64 = (bf16[128,1536]{1,0:T(8,128)(2,1)}, bf16[128,1536]{1,0:T(8,128)(2,1)S(1)}, u32[]{:S(2)}, u32[]{:S(2)}) collective-permute-start(bf16[128,1536]{1,0:T(8,128)(2,1)} %get-tuple-element.277), channel_id=1, source_target_pairs={{0,1},{1,0},{2,3},{3,2},{4,5},{5,4},{6,7},{7,6},{8,9},{9,8},{10,11... | collective-permute-start | bytes 1179656 | tf_op jit(solution)/shard_map/ppermute | solution.py:33
  674.3 35.4 %collective-permute-start.65 = (bf16[128,1536]{1,0:T(8,128)(2,1)}, bf16[128,1536]{1,0:T(8,128)(2,1)S(1)}, u32[]{:S(2)}, u32[]{:S(2)}) collective-permute-start(bf16[128,1536]{1,0:T(8,128)(2,1)} %fusion.93), channel_id=1, source_target_pairs={{0,2},{1,3},{2,0},{3,1},{4,6},{5,7},{6,4},{7,5},{8,10},{9,11},{10,... | collective-permute-start | bytes 1179656 | tf_op jit(solution)/shard_map/ppermute | solution.py:33
  677.1 10.5 %collective-permute-start.67 = (f32[6,1536]{1,0:T(8,128)S(1)}, f32[6,1536]{1,0:T(8,128)S(1)}, u32[]{:S(2)}, u32[]{:S(2)}) collective-permute-start(f32[6,1536]{1,0:T(8,128)S(1)} %stack.179), channel_id=1, source_target_pairs={{0,1},{1,0},{2,3},{3,2},{4,5},{5,4},{6,7},{7,6},{8,9},{9,8},{10,11... | collective-permute-start | bytes 110600 | tf_op jit(solution)/shard_map/ppermute | solution.py:33
  687.2 19.1 %collective-permute-start.62 = (bf16[2,192,1536]{2,1,0:T(8,128)(2,1)}, bf16[2,192,1536]{2,1,0:T(8,128)(2,1)}, u32[]{:S(2)}, u32[]{:S(2)}) collective-permute-start(bf16[2,192,1536]{2,1,0:T(8,128)(2,1)} %slice.899), channel_id=1, source_target_pairs={{0,1},{1,0},{2,3},{3,2},{4,5},{5,4},{6,7},{7,6},{8,9},{9,8},{10,11... | collective-permute-start | bytes 3538952 | tf_op jit(solution)/shard_map/ppermute | solution.py:33
  708.0 13.3 %collective-permute-start.63 = (bf16[2,96,1536]{2,1,0:T(8,128)(2,1)S(1)}, bf16[2,96,1536]{2,1,0:T(8,128)(2,1)S(1)}, u32[]{:S(2)}, u32[]{:S(2)}) collective-permute-start(bf16[2,96,1536]{2,1,0:T(8,128)(2,1)S(1)} %slice.903), channel_id=1, source_target_pairs={{0,2},{1,3},{2,0},{3,1},{4,6},{5,7},{6,4},{7,5},{8,10},{9,11},{10,... | collective-permute-start | bytes 1769480 | tf_op jit(solution)/shard_map/ppermute | solution.py:33
  (120 other events, 1230.7 us)
Sparse Core Ops, SparseCore 0:
  10.8 76.3 all-gather.4
  89.3 52.0 all-gather.6
  143.4 113.0 all-gather.8
  268.9 77.0 all-gather.10
  432.5 62.1 reduce-scatter.4
  500.2 54.4 reduce-scatter.6
  596.1 48.1 reduce-scatter.8
  665.9 39.4 reduce-scatter.10

commit v4 on v3

--- a/solution.py
+++ b/solution.py
@@ -713,10 +713,13 @@
     grad_projected, *qkv_blocks = after(grad_projected, *qkv_blocks)
     qkv_blocks = exchange([own] + qkv_blocks)
     grad_normed = scatter_step(by_clip(dot(grad_projected, qkv_all, 1, 1)), 1, nt)
+    grad_normed = scatter_rows(grad_normed, nt, 2)
     grad_normed, middle_grad, text_grads, *qkv_blocks = after(
         grad_normed, middle_grad, text_grads, *qkv_blocks
     )
-    qkv_grad = grad_finish(qkv_blocks).astype(wide)
+    qkv_total = block_sum(qkv_blocks).astype(low)
+    qkv_total, grad_normed, text_grads, active = after(qkv_total, grad_normed, text_grads, active)
+    qkv_grad = grad_scatter(qkv_total)
     text_low = text_grads.astype(low)
 
     def text_block(step):
@@ -732,8 +735,6 @@
         text_part = text_part + swap_tensor(text_part.astype(low), mask, nt).astype(wide)
         mask *= 2
 
-    grad_normed = scatter_rows(grad_normed, nt, 2)
-    grad_normed, active = after(grad_normed, active)
 
     layer_out = after_cross + scatter_rows(by_clip(dot(active, feed_out_all, 1, 1)), nt)
     layer_out = layer_out.astype(low).transpose(1, 0, 2)
@@ -753,6 +754,8 @@
     while mask < nt:
         norm_grads = norm_grads + swap_tensor(norm_grads, mask, nt)
         mask *= 2
+    norm_grads, qkv_grad, layer_out = after(norm_grads, qkv_grad, layer_out)
+    qkv_grad = qkv_grad.astype(wide)
     norm_parts = norm_grads.reshape(6, nf * nc, block).transpose(1, 0, 2)
     norm_result = reduce_group(norm_parts, *group)
 

time: 743 us -> 741 us (level)
  waiting for transfers between devices: 358 us -> 373 us
    ppermute x21, waiting for transfers between devices: 178 us -> 189 us  [from_context(): lax.ppermute(values, 'context', [((i + step) % size, i) for i in range(si...]
    unnamed x213 -> x207, local copies, waits for them, and re-layouts: 22.8 us -> 19.1 us
  transfers between devices with their start and end apart: 81 -> 81, of which waited for: 35 -> 37; matrix products, arithmetic and copies ran while one was open for 24% -> 23% of each run, Pallas kernels for 9% -> 9%
where the time goes in v4:
time: 741 us; the launch traced here: 732 us
  waiting for transfers between devices  373 us (50%)
  matrix products  101 us (14%)
  starting transfers between devices  74.2 us (10%)
  Pallas kernels  63.4 us (9%)
  other arithmetic  58 us (8%)
  local copies, waits for them, and re-layouts  45.5 us (6%)
  between operations  16.8 us (2%)
    ppermute x21, waiting for transfers between devices, from_context(): lax.ppermute(values, 'context', [((i + step) % size, i) for i in range(si...  189 us
    dot_general x32, matrix products, dot(): lax.dot_general(left, right, (((left_dim,), (right_dim,)), ((), ())), pre...  101 us
    ppermute x34, waiting for transfers between devices, swap_tensor(): return lax.ppermute(values, 'tensor', [(i, i ^ mask) for i in range(size)])  78.3 us
    ppermute x16, waiting for transfers between devices, from_fsdp(): lax.ppermute(values, 'fsdp', [((i + step) % size, i) for i in range(size)])  43.2 us
    all_gather x1, waiting for transfers between devices, gather_near(): return lax.all_gather(shard, 'context', axis=0, tiled=True)  32.7 us
    ppermute x21, starting transfers between devices, from_context(): lax.ppermute(values, 'context', [((i + step) % size, i) for i in range(si...  27.2 us
    ppermute x2, waiting for transfers between devices, text_sum(): lax.ppermute(values.astype(low), 'context', [(i, i ^ mask) for i in range...  26.2 us
    pallas_call x1, Pallas kernels, self_backward(): pl.pallas_call(functools.partial(self_backward_kernel, frames, order), ou...  24.7 us
  transfers between devices with their start and end apart: 81, of which 37 were waited for; matrix products, arithmetic and copies ran while one was open for 23% of the time, Pallas kernels for 9%

profile of v4, /device:TPU:8, one launch (start us, length us, event | category | flops | bytes accessed | tf_op | source)
XLA Modules:
  0.0 731.8 jit_solution(2113625122625446044)
XLA Ops:
  15.0 4.4 collective-permute-start.5
  21.1 2.3 broadcast_in_dim.93
  27.8 6.3 collective-permute-done.2
  34.8 2.8 collective-permute-done.4
  38.1 3.1 collective-permute-done.6
  43.6 18.0 %collective-permute-done.11 = bf16[192,1152]{1,0:T(8,128)(2,1)S(1)} collective-permute-done((bf16[192,1152]{1,0:T(8,128)(2,1)S(1)}, bf16[192,1152]{1,0:T(8,128)(2,1)S(1)}, u32[]{:S(2)}, u32[]{:S(2)}) %collective-permute-start.11) | collective-permute-done | bytes 442400 | tf_op jit(solution)/shard_map/ppermute | solution.py:25
  63.6 23.5 %collective-permute-done.15 = bf16[192,1152]{1,0:T(8,128)(2,1)S(1)} collective-permute-done((bf16[192,1152]{1,0:T(8,128)(2,1)S(1)}, bf16[192,1152]{1,0:T(8,128)(2,1)S(1)}, u32[]{:S(2)}, u32[]{:S(2)}) %collective-permute-start.15) | collective-permute-done | bytes 442400 | tf_op jit(solution)/shard_map/ppermute | solution.py:25
  93.5 5.5 collective-permute-done.16
  101.5 5.2 convolution_convert_fusion.4
  108.7 32.7 %all-gather.7.cloned.1.call-done = bf16[768,1152]{1,0:T(8,128)(2,1)} async-done(((bf16[192,1152]{1,0:T(8,128)(2,1)}), bf16[768,1152]{1,0:T(8,128)(2,1)}) %all-gather.7.cloned.1.call-update) | async-done | bytes 1769488 | tf_op jit(solution)/shard_map/all_gather | solution.py:480
  147.0 23.2 %collective-permute-done.19 = bf16[384,576]{1,0:T(8,128)(2,1)} collective-permute-done((bf16[384,576]{1,0:T(8,128)(2,1)}, bf16[384,576]{1,0:T(8,128)(2,1)}, u32[]{:S(2)}, u32[]{:S(2)}) %collective-permute-start.19) | collective-permute-done | bytes 442400 | tf_op jit(solution)/shard_map/ppermute | solution.py:25
  170.2 25.5 %collective-permute-done.18 = bf16[384,576]{1,0:T(8,128)(2,1)} collective-permute-done((bf16[384,576]{1,0:T(8,128)(2,1)}, bf16[384,576]{1,0:T(8,128)(2,1)}, u32[]{:S(2)}, u32[]{:S(2)}) %collective-permute-start.18) | collective-permute-done | bytes 442400 | tf_op jit(solution)/shard_map/ppermute | solution.py:25
  199.8 18.0 %shard_map.330 = (bf16[4,384,192]{2,1,0:T(8,128)(2,1)S(1)}, f32[4,3,384]{2,1,0:T(4,128)S(1)}) custom-call(s32[2]{0:T(128)S(1)} %pad_add_fusion.place_ref, bf16[4,384,576]{2,1,0:T(8,128)(2,1)S(1)} %pad_maximum_fusion.9.rows_ref), custom_call_target="tpu_custom_call" | custom-call | flops 1132462080 | bytes 3538944 | tf_op jit(solution)/shard_map/pallas_call | solution.py:311
  221.8 3.5 collective-permute-start.23
  227.2 8.4 %collective-permute-done.24 = bf16[384,192]{1,0:T(8,128)(2,1)S(1)} collective-permute-done((bf16[384,192]{1,0:T(8,128)(2,1)S(1)}, bf16[384,192]{1,0:T(8,128)(2,1)S(1)}, u32[]{:S(2)}, u32[]{:S(2)}) %collective-permute-start.24) | collective-permute-done | bytes 147488 | tf_op jit(solution)/shard_map/ppermute | solution.py:25
  235.6 20.3 %collective-permute-done.23 = bf16[384,192]{1,0:T(8,128)(2,1)S(1)} collective-permute-done((bf16[384,192]{1,0:T(8,128)(2,1)S(1)}, bf16[384,192]{1,0:T(8,128)(2,1)S(1)}, u32[]{:S(2)}, u32[]{:S(2)}) %collective-permute-start.23) | collective-permute-done | bytes 147488 | tf_op jit(solution)/shard_map/ppermute | solution.py:25
  255.8 2.5 collective-permute-done.22
  261.1 2.7 fusion.79
  269.2 2.3 slice_add_fusion.3
  275.4 20.2 %collective-permute-done.29 = bf16[2,96,1536]{2,1,0:T(8,128)(2,1)S(1)} collective-permute-done((bf16[2,96,1536]{2,1,0:T(8,128)(2,1)S(1)}, bf16[2,96,1536]{2,1,0:T(8,128)(2,1)S(1)}, u32[]{:S(2)}, u32[]{:S(2)}) %collective-permute-start.29) | collective-permute-done | bytes 589856 | tf_op jit(solution)/shard_map/ppermute | solution.py:33
  297.9 3.6 convolution_convert_fusion.7
  301.5 10.0 %shard_map.331 = bf16[2,96,1536]{2,1,0:T(8,128)(2,1)S(1)} custom-call(bf16[2,96,1536]{2,1,0:T(8,128)(2,1)S(1)} %bitcast.264, bf16[2,64,1536]{2,1,0:T(8,128)(2,1)S(1)} %bitcast.256, bf16[2,64,1536]{2,1,0:T(8,128)(2,1)S(1)} %bitcast.258), custom_call_target="tpu_custom_call" | custom-call | flops 75497472 | bytes 1179648 | tf_op jit(solution)/shard_map/pallas_call | solution.py:391
  311.5 3.1 fusion.203
  318.1 13.0 %collective-permute-done.35 = bf16[2,96,1536]{2,1,0:T(8,128)(2,1)} collective-permute-done((bf16[2,96,1536]{2,1,0:T(8,128)(2,1)}, bf16[2,96,1536]{2,1,0:T(8,128)(2,1)}, u32[]{:S(2)}, u32[]{:S(2)}) %collective-permute-start.35) | collective-permute-done | bytes 589856 | tf_op jit(solution)/shard_map/ppermute | solution.py:33
  331.1 3.3 pad_maximum_fusion.4
  334.5 3.2 pad_maximum_fusion.5
  337.7 8.3 %multiply_convert_fusion = (bf16[768,1536]{1,0:T(8,128)(2,1)S(1)}, f32[768,1536]{1,0:T(8,128)}) fusion(bf16[768,1536]{1,0:T(8,128)(2,1)} %bitcast.300, bf16[1536,1536]{1,0:T(8,128)(2,1)} %all-gather.9.cloned.1.call-done), kind=kOutput, calls=%fused_computation.16 | convolution fusion | flops 3629776896 | bytes 14155776 | tf_op jit(solution)/shard_map/dot_general | solution.py:19
  346.0 4.2 fusion.54
  350.2 3.4 convolution_convert_fusion.3
  353.7 7.9 %fusion.5 = bf16[768,1536]{1,0:T(8,128)(2,1)S(1)} fusion(f32[768,1536]{1,0:T(8,128)} %get-tuple-element.285, bf16[768,1536]{1,0:T(8,128)(2,1)} %bitcast.303, bf16[1536,1536]{1,0:T(8,128)(2,1)} %all-gather.11.cloned.1.call-done), kind=kOutput, calls=%fused_computation.6 | convolution fusion | flops 3635675136 | bytes 14155776 | tf_op jit(solution)/shard_map/dot_general | solution.py:19
  361.6 6.2 fusion.205
  368.3 2.5 collective-permute-done.38
  372.8 4.2 fusion.51
  378.4 3.5 convolution_convert_fusion.2
  381.9 4.9 collective-permute-done.39
  390.4 3.4 convolution_convert_fusion.6
  393.8 10.8 %shard_map.332 = (bf16[2,96,1536]{2,1,0:T(8,128)(2,1)S(1)}, f32[2,64,1536]{2,1,0:T(8,128)S(1)}, f32[2,64,1536]{2,1,0:T(8,128)S(1)}) custom-call(bf16[2,96,1536]{2,1,0:T(8,128)(2,1)S(1)} %bitcast.265, bf16[2,64,1536]{2,1,0:T(8,128)(2,1)S(1)} %bitcast.257, bf16[2,64,1536]{2,1,0:T(8,128)(2,1)S(1)} %bitcast.259, bf16[2,96,1536]{2,1,0:T(8,128)(2,1)S(1)} %bitcast.270), custom_call_target="tpu_custom_call" | custom-call | flops 188743680 | bytes 2359296 | tf_op jit(solution)/shard_map/pallas_call | solution.py:406
  404.8 2.4 multiply_reduce_fusion.1
  412.2 11.4 %collective-permute-done.40 = bf16[2,96,1536]{2,1,0:T(8,128)(2,1)S(1)} collective-permute-done((bf16[2,96,1536]{2,1,0:T(8,128)(2,1)S(1)}, bf16[2,96,1536]{2,1,0:T(8,128)(2,1)S(1)}, u32[]{:S(2)}, u32[]{:S(2)}) %collective-permute-start.40) | collective-permute-done | bytes 589856 | tf_op jit(solution)/shard_map/ppermute | solution.py:33
  423.7 2.4 pad_maximum_fusion.2
  438.1 4.2 collective-permute-done.48
  442.4 2.7 convolution_convert_fusion.8
  446.3 15.6 %collective-permute-done.46 = bf16[384,192]{1,0:T(8,128)(2,1)S(1)} collective-permute-done((bf16[384,192]{1,0:T(8,128)(2,1)S(1)}, bf16[384,192]{1,0:T(8,128)(2,1)S(1)}, u32[]{:S(2)}, u32[]{:S(2)}) %collective-permute-start.46) | collective-permute-done | bytes 147488 | tf_op jit(solution)/shard_map/ppermute | solution.py:25
  469.6 15.7 %collective-permute-done.45 = bf16[384,192]{1,0:T(8,128)(2,1)S(1)} collective-permute-done((bf16[384,192]{1,0:T(8,128)(2,1)S(1)}, bf16[384,192]{1,0:T(8,128)(2,1)S(1)}, u32[]{:S(2)}, u32[]{:S(2)}) %collective-permute-start.45) | collective-permute-done | bytes 147488 | tf_op jit(solution)/shard_map/ppermute | solution.py:25
  485.3 6.3 collective-permute-done.44
  494.7 5.3 add_convert_fusion
  502.7 24.7 %shard_map.333 = bf16[4,384,576]{2,1,0:T(8,128)(2,1)S(1)} custom-call(s32[2]{0:T(128)S(1)} %pad_add_fusion.place_ref, bf16[4,384,576]{2,1,0:T(8,128)(2,1)S(1)} %copy-done.1, bf16[4,384,192]{2,1,0:T(8,128)(2,1)S(1)} %copy-done.3, f32[4,3,384]{2,1,0:T(4,128)S(1)} %copy-done.8, bf16[4,384,192]{2,1,0:T(8,128)(2,1)S(1)} %copy-done.4), custom_call_target="tpu_custom_call" | custom-call | flops 2831155200 | bytes 7077888 | tf_op jit(solution)/shard_map/pallas_call | solution.py:332
  531.7 24.0 %collective-permute-done.51 = bf16[384,576]{1,0:T(8,128)(2,1)S(1)} collective-permute-done((bf16[384,576]{1,0:T(8,128)(2,1)S(1)}, bf16[384,576]{1,0:T(8,128)(2,1)S(1)}, u32[]{:S(2)}, u32[]{:S(2)}) %collective-permute-start.51) | collective-permute-done | bytes 442400 | tf_op jit(solution)/shard_map/ppermute | solution.py:25
  562.6 4.4 collective-permute-start.53
  566.9 9.6 %collective-permute-done.56 = bf16[128,768]{1,0:T(8,128)(2,1)S(1)} collective-permute-done((bf16[128,768]{1,0:T(8,128)(2,1)S(1)}, bf16[128,768]{1,0:T(8,128)(2,1)S(1)}, u32[]{:S(2)}, u32[]{:S(2)}) %collective-permute-start.56) | collective-permute-done | bytes 196640 | tf_op jit(solution)/shard_map/ppermute | solution.py:662
  580.6 7.2 collective-permute-done.54
  589.5 4.7 collective-permute-done.53
  598.5 4.6 convolution_convert_fusion.5
  603.1 5.2 fusion.206
  615.2 3.5 collective-permute-start.60
  619.8 2.3 slice_add_fusion.1
  623.8 16.6 %collective-permute-done.60 = bf16[128,768]{1,0:T(8,128)(2,1)S(1)} collective-permute-done((bf16[128,768]{1,0:T(8,128)(2,1)S(1)}, bf16[128,768]{1,0:T(8,128)(2,1)S(1)}, u32[]{:S(2)}, u32[]{:S(2)}) %collective-permute-start.60) | collective-permute-done | bytes 196640 | tf_op jit(solution)/shard_map/ppermute | solution.py:662
  641.6 3.6 fusion.42
  646.5 13.3 %collective-permute-done.61 = bf16[768,1152]{1,0:T(8,128)(2,1)} collective-permute-done((bf16[768,1152]{1,0:T(8,128)(2,1)}, bf16[768,1152]{1,0:T(8,128)(2,1)}, u32[]{:S(2)}, u32[]{:S(2)}) %collective-permute-start.61) | collective-permute-done | bytes 1769504 | tf_op jit(solution)/shard_map/ppermute | solution.py:29
  659.8 4.1 add_convert_fusion.2
  665.3 6.9 fusion.207
  689.9 8.6 %collective-permute-done.67 = bf16[128,1536]{1,0:T(8,128)(2,1)S(1)} collective-permute-done((bf16[128,1536]{1,0:T(8,128)(2,1)S(1)}, bf16[128,1536]{1,0:T(8,128)(2,1)S(1)}, u32[]{:S(2)}, u32[]{:S(2)}) %collective-permute-start.67) | collective-permute-done | bytes 393248 | tf_op jit(solution)/shard_map/ppermute | solution.py:33
  700.2 9.8 %collective-permute-done.65 = bf16[2,96,1536]{2,1,0:T(8,128)(2,1)S(1)} collective-permute-done((bf16[2,96,1536]{2,1,0:T(8,128)(2,1)S(1)}, bf16[2,96,1536]{2,1,0:T(8,128)(2,1)S(1)}, u32[]{:S(2)}, u32[]{:S(2)}) %collective-permute-start.65) | collective-permute-done | bytes 589856 | tf_op jit(solution)/shard_map/ppermute | solution.py:33
  716.5 3.8 collective-permute-start.71
  (513 shorter events, 166.5 us)
Async XLA Ops:
  7.3 92.7 %all-gather.5.cloned.1.call-start = ((), (), s32[]{:S(2)}) async-start(), calls=%async_computation.4 | async-start | bytes 2654208 | tf_op jit(solution)/shard_map/all_gather | solution.py:492
  9.2 132.1 %all-gather.7.cloned.1.call-start = ((), (), s32[]{:S(2)}) async-start(), calls=%async_computation.5 | async-start | bytes 2211840 | tf_op jit(solution)/shard_map/all_gather | solution.py:480
  11.2 326.5 %all-gather.9.cloned.1.call-start = ((), (), s32[]{:S(2)}) async-start(), calls=%async_computation.6 | async-start | bytes 5308416 | tf_op jit(solution)/shard_map/all_gather | solution.py:492
  11.4 12.8 %collective-permute-start = (bf16[8,192]{1,0:T(8,128)(2,1)S(1)}, bf16[8,192]{1,0:T(8,128)(2,1)S(1)}, u32[]{:S(2)}, u32[]{:S(2)}) collective-permute-start(bf16[8,192]{1,0:T(8,128)(2,1)S(1)} %stack.147), channel_id=1, source_target_pairs={{16,0},{0,16},{17,1},{1,17},{18,2},{2,18},{19,3},{3,19},{20,4},{4,... | collective-permute-start | bytes 9224 | tf_op jit(solution)/shard_map/ppermute | solution.py:29
  13.0 11.2 %collective-permute-start.1 = (bf16[8,192]{1,0:T(8,128)(2,1)S(1)}, bf16[8,192]{1,0:T(8,128)(2,1)S(1)}, u32[]{:S(2)}, u32[]{:S(2)}) collective-permute-start(bf16[8,192]{1,0:T(8,128)(2,1)S(1)} %stack.147), channel_id=1, source_target_pairs={{4,0},{8,4},{12,8},{0,12},{5,1},{9,5},{13,9},{1,13},{6,2},{10,6},{... | collective-permute-start | bytes 9224 | tf_op jit(solution)/shard_map/ppermute | solution.py:25
  13.5 12.3 %collective-permute-start.3 = (bf16[8,192]{1,0:T(8,128)(2,1)S(1)}, bf16[8,192]{1,0:T(8,128)(2,1)S(1)}, u32[]{:S(2)}, u32[]{:S(2)}) collective-permute-start(bf16[8,192]{1,0:T(8,128)(2,1)S(1)} %stack.147), channel_id=1, source_target_pairs={{12,0},{0,4},{4,8},{8,12},{13,1},{1,5},{5,9},{9,13},{14,2},{2,6},{... | collective-permute-start | bytes 9224 | tf_op jit(solution)/shard_map/ppermute | solution.py:25
  15.0 19.5 %collective-permute-start.5 = (bf16[8,192]{1,0:T(8,128)(2,1)S(1)}, bf16[8,192]{1,0:T(8,128)(2,1)S(1)}, u32[]{:S(2)}, u32[]{:S(2)}) collective-permute-start(bf16[8,192]{1,0:T(8,128)(2,1)S(1)} %stack.147), channel_id=1, source_target_pairs={{8,0},{12,4},{0,8},{4,12},{9,1},{13,5},{1,9},{5,13},{10,2},{14,6},... | collective-permute-start | bytes 9224 | tf_op jit(solution)/shard_map/ppermute | solution.py:25
  19.9 23.6 %collective-permute-start.10 = (bf16[192,1152]{1,0:T(8,128)(2,1)S(1)}, bf16[192,1152]{1,0:T(8,128)(2,1)S(1)}, u32[]{:S(2)}, u32[]{:S(2)}) collective-permute-start(bf16[192,1152]{1,0:T(8,128)(2,1)S(1)} %concatenate.81), channel_id=1, source_target_pairs={{16,0},{0,16},{17,1},{1,17},{18,2},{2,18},{19,3},{3,19},{20,4},{4,... | collective-permute-start | bytes 1327112 | tf_op jit(solution)/shard_map/ppermute | solution.py:29
  20.5 333.2 %all-gather.11.cloned.1.call-start = ((), (), s32[]{:S(2)}) async-start(), calls=%async_computation.7 | async-start | bytes 5308416 | tf_op jit(solution)/shard_map/all_gather | solution.py:492
  24.2 37.4 %collective-permute-start.11 = (bf16[192,1152]{1,0:T(8,128)(2,1)S(1)}, bf16[192,1152]{1,0:T(8,128)(2,1)S(1)}, u32[]{:S(2)}, u32[]{:S(2)}) collective-permute-start(bf16[192,1152]{1,0:T(8,128)(2,1)S(1)} %concatenate.81), channel_id=1, source_target_pairs={{4,0},{8,4},{12,8},{0,12},{5,1},{9,5},{13,9},{1,13},{6,2},{10,6},{... | collective-permute-start | bytes 1327112 | tf_op jit(solution)/shard_map/ppermute | solution.py:25
  24.2 9.8 %collective-permute-start.2 = (bf16[8,192]{1,0:T(8,128)(2,1)S(1)}, bf16[8,192]{1,0:T(8,128)(2,1)S(1)}, u32[]{:S(2)}, u32[]{:S(2)}) collective-permute-start(bf16[8,192]{1,0:T(8,128)(2,1)S(1)} %collective-permute-done.1), channel_id=1, source_target_pairs={{16,0},{0,16},{17,1},{1,17},{18,2},{2,18},{19,3},{3,19},{20,4},{4,... | collective-permute-start | bytes 9224 | tf_op jit(solution)/shard_map/ppermute | solution.py:29
  25.8 35.8 %collective-permute-start.13 = (bf16[192,1152]{1,0:T(8,128)(2,1)S(1)}, bf16[192,1152]{1,0:T(8,128)(2,1)S(1)}, u32[]{:S(2)}, u32[]{:S(2)}) collective-permute-start(bf16[192,1152]{1,0:T(8,128)(2,1)S(1)} %concatenate.81), channel_id=1, source_target_pairs={{12,0},{0,4},{4,8},{8,12},{13,1},{1,5},{5,9},{9,13},{14,2},{2,6},{... | collective-permute-start | bytes 1327112 | tf_op jit(solution)/shard_map/ppermute | solution.py:25
  34.5 52.6 %collective-permute-start.15 = (bf16[192,1152]{1,0:T(8,128)(2,1)S(1)}, bf16[192,1152]{1,0:T(8,128)(2,1)S(1)}, u32[]{:S(2)}, u32[]{:S(2)}) collective-permute-start(bf16[192,1152]{1,0:T(8,128)(2,1)S(1)} %concatenate.81), channel_id=1, source_target_pairs={{8,0},{12,4},{0,8},{4,12},{9,1},{13,5},{1,9},{5,13},{10,2},{14,6},... | collective-permute-start | bytes 1327112 | tf_op jit(solution)/shard_map/ppermute | solution.py:25
  42.0 48.3 %collective-permute-start.7 = (bf16[2,96,1536]{2,1,0:T(8,128)(2,1)S(1)}, bf16[2,96,1536]{2,1,0:T(8,128)(2,1)S(1)}, u32[]{:S(2)}, u32[]{:S(2)}) collective-permute-start(bf16[2,96,1536]{2,1,0:T(8,128)(2,1)S(1)} %fusion.34), channel_id=1, source_target_pairs={{0,2},{1,3},{2,0},{3,1},{4,6},{5,7},{6,4},{7,5},{8,10},{9,11},{10,... | collective-permute-start | bytes 1769480 | tf_op jit(solution)/shard_map/ppermute | solution.py:33
  43.6 56.2 %collective-permute-start.8 = (bf16[2,96,1536]{2,1,0:T(8,128)(2,1)S(1)}, bf16[2,96,1536]{2,1,0:T(8,128)(2,1)S(1)}, u32[]{:S(2)}, u32[]{:S(2)}) collective-permute-start(bf16[2,96,1536]{2,1,0:T(8,128)(2,1)S(1)} %fusion.34), channel_id=1, source_target_pairs={{0,1},{1,0},{2,3},{3,2},{4,5},{5,4},{6,7},{7,6},{8,9},{9,8},{10,11... | collective-permute-start | bytes 1769480 | tf_op jit(solution)/shard_map/ppermute | solution.py:33
  61.6 28.7 %collective-permute-start.12 = (bf16[192,1152]{1,0:T(8,128)(2,1)S(1)}, bf16[192,1152]{1,0:T(8,128)(2,1)S(1)}, u32[]{:S(2)}, u32[]{:S(2)}) collective-permute-start(bf16[192,1152]{1,0:T(8,128)(2,1)S(1)} %collective-permute-done.11), channel_id=1, source_target_pairs={{16,0},{0,16},{17,1},{1,17},{18,2},{2,18},{19,3},{3,19},{20,4},{4,... | collective-permute-start | bytes 1327112 | tf_op jit(solution)/shard_map/ppermute | solution.py:29
  61.6 30.3 %collective-permute-start.14 = (bf16[192,1152]{1,0:T(8,128)(2,1)S(1)}, bf16[192,1152]{1,0:T(8,128)(2,1)S(1)}, u32[]{:S(2)}, u32[]{:S(2)}) collective-permute-start(bf16[192,1152]{1,0:T(8,128)(2,1)S(1)} %collective-permute-done.13), channel_id=1, source_target_pairs={{16,0},{0,16},{17,1},{1,17},{18,2},{2,18},{19,3},{3,19},{20,4},{4,... | collective-permute-start | bytes 1327112 | tf_op jit(solution)/shard_map/ppermute | solution.py:29
  87.1 11.9 %collective-permute-start.16 = (bf16[192,1152]{1,0:T(8,128)(2,1)S(1)}, bf16[192,1152]{1,0:T(8,128)(2,1)S(1)}, u32[]{:S(2)}, u32[]{:S(2)}) collective-permute-start(bf16[192,1152]{1,0:T(8,128)(2,1)S(1)} %collective-permute-done.15), channel_id=1, source_target_pairs={{16,0},{0,16},{17,1},{1,17},{18,2},{2,18},{19,3},{3,19},{20,4},{4,... | collective-permute-start | bytes 1327112 | tf_op jit(solution)/shard_map/ppermute | solution.py:29
  100.0 99.8 %collective-permute-start.20 = (bf16[1536,768]{1,0:T(8,128)(2,1)}, bf16[1536,768]{1,0:T(8,128)(2,1)}, u32[]{:S(2)}, u32[]{:S(2)}) collective-permute-start(bf16[1536,768]{1,0:T(8,128)(2,1)} %all-gather.5.cloned.1.call-done), channel_id=1, source_target_pairs={{0,2},{1,3},{2,0},{3,1},{4,6},{5,7},{6,4},{7,5},{8,10},{9,11},{10,... | collective-permute-start | bytes 7077896 | tf_op jit(solution)/shard_map/ppermute | solution.py:33
  108.7 32.7 %collective-permute-start.17 = (bf16[384,576]{1,0:T(8,128)(2,1)S(1)}, bf16[384,576]{1,0:T(8,128)(2,1)}, u32[]{:S(2)}, u32[]{:S(2)}) collective-permute-start(bf16[384,576]{1,0:T(8,128)(2,1)S(1)} %get-tuple-element.226), channel_id=1, source_target_pairs={{12,0},{0,4},{4,8},{8,12},{13,1},{1,5},{5,9},{9,13},{14,2},{2,6},{... | collective-permute-start | bytes 1327112 | tf_op jit(solution)/shard_map/ppermute | solution.py:25
  141.4 76.5 %collective-permute-start.21 = (bf16[768,1152]{1,0:T(8,128)(2,1)}, bf16[768,1152]{1,0:T(8,128)(2,1)S(1)}, u32[]{:S(2)}, u32[]{:S(2)}) collective-permute-start(bf16[768,1152]{1,0:T(8,128)(2,1)} %all-gather.7.cloned.1.call-done), channel_id=1, source_target_pairs={{16,0},{0,16},{17,1},{1,17},{18,2},{2,18},{19,3},{3,19},{20,4},{4,... | collective-permute-start | bytes 5308424 | tf_op jit(solution)/shard_map/ppermute | solution.py:29
  142.8 27.3 %collective-permute-start.19 = (bf16[384,576]{1,0:T(8,128)(2,1)}, bf16[384,576]{1,0:T(8,128)(2,1)}, u32[]{:S(2)}, u32[]{:S(2)}) collective-permute-start(bf16[384,576]{1,0:T(8,128)(2,1)} %get-tuple-element.224), channel_id=1, source_target_pairs={{4,0},{8,4},{12,8},{0,12},{5,1},{9,5},{13,9},{1,13},{6,2},{10,6},{... | collective-permute-start | bytes 1327112 | tf_op jit(solution)/shard_map/ppermute | solution.py:25
  144.6 51.0 %collective-permute-start.18 = (bf16[384,576]{1,0:T(8,128)(2,1)}, bf16[384,576]{1,0:T(8,128)(2,1)}, u32[]{:S(2)}, u32[]{:S(2)}) collective-permute-start(bf16[384,576]{1,0:T(8,128)(2,1)} %get-tuple-element.225), channel_id=1, source_target_pairs={{8,0},{12,4},{0,8},{4,12},{9,1},{13,5},{1,9},{5,13},{10,2},{14,6},... | collective-permute-start | bytes 1327112 | tf_op jit(solution)/shard_map/ppermute | solution.py:25
  219.9 39.1 %collective-permute-start.25 = (bf16[128,768]{0,1:T(8,128)(2,1)S(1)}, bf16[128,768]{0,1:T(8,128)(2,1)S(1)}, u32[]{:S(2)}, u32[]{:S(2)}) collective-permute-start(bf16[128,768]{0,1:T(8,128)(2,1)S(1)} %fusion.67), channel_id=1, source_target_pairs={{0,2},{1,3},{2,0},{3,1},{4,6},{5,7},{6,4},{7,5},{8,10},{9,11},{10,... | collective-permute-start | bytes 589832 | tf_op jit(solution)/shard_map/ppermute | solution.py:33
  221.6 37.6 %collective-permute-start.26 = (bf16[128,768]{0,1:T(8,128)(2,1)S(1)}, bf16[128,768]{0,1:T(8,128)(2,1)S(1)}, u32[]{:S(2)}, u32[]{:S(2)}) collective-permute-start(bf16[128,768]{0,1:T(8,128)(2,1)S(1)} %fusion.67), channel_id=1, source_target_pairs={{0,1},{1,0},{2,3},{3,2},{4,5},{5,4},{6,7},{7,6},{8,9},{9,8},{10,11... | collective-permute-start | bytes 589832 | tf_op jit(solution)/shard_map/ppermute | solution.py:33
  221.7 13.8 %collective-permute-start.24 = (bf16[384,192]{1,0:T(8,128)(2,1)S(1)}, bf16[384,192]{1,0:T(8,128)(2,1)S(1)}, u32[]{:S(2)}, u32[]{:S(2)}) collective-permute-start(bf16[384,192]{1,0:T(8,128)(2,1)S(1)} %get-tuple-element.240), channel_id=1, source_target_pairs={{12,0},{0,4},{4,8},{8,12},{13,1},{1,5},{5,9},{9,13},{14,2},{2,6},{... | collective-permute-start | bytes 442376 | tf_op jit(solution)/shard_map/ppermute | solution.py:25
  221.8 34.0 %collective-permute-start.23 = (bf16[384,192]{1,0:T(8,128)(2,1)S(1)}, bf16[384,192]{1,0:T(8,128)(2,1)S(1)}, u32[]{:S(2)}, u32[]{:S(2)}) collective-permute-start(bf16[384,192]{1,0:T(8,128)(2,1)S(1)} %get-tuple-element.241), channel_id=1, source_target_pairs={{8,0},{12,4},{0,8},{4,12},{9,1},{13,5},{1,9},{5,13},{10,2},{14,6},... | collective-permute-start | bytes 442376 | tf_op jit(solution)/shard_map/ppermute | solution.py:25
  225.2 33.1 %collective-permute-start.22 = (bf16[384,192]{1,0:T(8,128)(2,1)S(1)}, bf16[384,192]{1,0:T(8,128)(2,1)S(1)}, u32[]{:S(2)}, u32[]{:S(2)}) collective-permute-start(bf16[384,192]{1,0:T(8,128)(2,1)S(1)} %get-tuple-element.242), channel_id=1, source_target_pairs={{4,0},{8,4},{12,8},{0,12},{5,1},{9,5},{13,9},{1,13},{6,2},{10,6},{... | collective-permute-start | bytes 442376 | tf_op jit(solution)/shard_map/ppermute | solution.py:25
  267.2 50.4 %collective-permute-start.32 = (bf16[2,96,1536]{2,1,0:T(8,128)(2,1)}, bf16[2,96,1536]{2,1,0:T(8,128)(2,1)}, u32[]{:S(2)}, u32[]{:S(2)}) collective-permute-start(bf16[2,96,1536]{2,1,0:T(8,128)(2,1)} %bitcast.252), channel_id=1, source_target_pairs={{0,2},{1,3},{2,0},{3,1},{4,6},{5,7},{6,4},{7,5},{8,10},{9,11},{10,... | collective-permute-start | bytes 1769480 | tf_op jit(solution)/shard_map/ppermute | solution.py:33
  268.7 226.0 %reduce-scatter.5.cloned.1.call-start = ((), (), s32[]{:S(2)}) async-start(), calls=%async_computation.8 | async-start | bytes 2949120 | tf_op jit(solution)/shard_map/reduce_scatter | solution.py:581
  269.1 27.4 %collective-permute-start.31 = (bf16[1536,768]{1,0:T(8,128)(2,1)}, bf16[1536,768]{1,0:T(8,128)(2,1)S(1)}, u32[]{:S(2)}, u32[]{:S(2)}) collective-permute-start(bf16[1536,768]{1,0:T(8,128)(2,1)} %collective-permute-done.20), channel_id=1, source_target_pairs={{0,1},{1,0},{2,3},{3,2},{4,5},{5,4},{6,7},{7,6},{8,9},{9,8},{10,11... | collective-permute-start | bytes 7077896 | tf_op jit(solution)/shard_map/ppermute | solution.py:33
  271.6 24.1 %collective-permute-start.29 = (bf16[2,96,1536]{2,1,0:T(8,128)(2,1)S(1)}, bf16[2,96,1536]{2,1,0:T(8,128)(2,1)S(1)}, u32[]{:S(2)}, u32[]{:S(2)}) collective-permute-start(bf16[2,96,1536]{2,1,0:T(8,128)(2,1)S(1)} %slice.907), channel_id=1, source_target_pairs={{0,2},{1,3},{2,0},{3,1},{4,6},{5,7},{6,4},{7,5},{8,10},{9,11},{10,... | collective-permute-start | bytes 1769480 | tf_op jit(solution)/shard_map/ppermute | solution.py:33
  275.1 21.8 %collective-permute-start.30 = (bf16[1536,768]{1,0:T(8,128)(2,1)S(1)}, bf16[1536,768]{1,0:T(8,128)(2,1)S(1)}, u32[]{:S(2)}, u32[]{:S(2)}) collective-permute-start(bf16[1536,768]{1,0:T(8,128)(2,1)S(1)} %copy-done.28), channel_id=1, source_target_pairs={{0,1},{1,0},{2,3},{3,2},{4,5},{5,4},{6,7},{7,6},{8,9},{9,8},{10,11... | collective-permute-start | bytes 7077896 | tf_op jit(solution)/shard_map/ppermute | solution.py:33
  316.1 15.1 %collective-permute-start.35 = (bf16[2,96,1536]{2,1,0:T(8,128)(2,1)}, bf16[2,96,1536]{2,1,0:T(8,128)(2,1)}, u32[]{:S(2)}, u32[]{:S(2)}) collective-permute-start(bf16[2,96,1536]{2,1,0:T(8,128)(2,1)} %add_convert_fusion.6), channel_id=1, source_target_pairs={{0,2},{1,3},{2,0},{3,1},{4,6},{5,7},{6,4},{7,5},{8,10},{9,11},{10,... | collective-permute-start | bytes 1769480 | tf_op jit(solution)/shard_map/ppermute | solution.py:33
  317.6 13.5 %collective-permute-start.33 = (bf16[2,96,1536]{2,1,0:T(8,128)(2,1)}, bf16[2,96,1536]{2,1,0:T(8,128)(2,1)}, u32[]{:S(2)}, u32[]{:S(2)}) collective-permute-start(bf16[2,96,1536]{2,1,0:T(8,128)(2,1)} %bitcast.252), channel_id=1, source_target_pairs={{0,1},{1,0},{2,3},{3,2},{4,5},{5,4},{6,7},{7,6},{8,9},{9,8},{10,11... | collective-permute-start | bytes 1769480 | tf_op jit(solution)/shard_map/ppermute | solution.py:33
  317.6 13.5 %collective-permute-start.34 = (bf16[2,96,1536]{2,1,0:T(8,128)(2,1)}, bf16[2,96,1536]{2,1,0:T(8,128)(2,1)}, u32[]{:S(2)}, u32[]{:S(2)}) collective-permute-start(bf16[2,96,1536]{2,1,0:T(8,128)(2,1)} %collective-permute-done.32), channel_id=1, source_target_pairs={{0,1},{1,0},{2,3},{3,2},{4,5},{5,4},{6,7},{7,6},{8,9},{9,8},{10,11... | collective-permute-start | bytes 1769480 | tf_op jit(solution)/shard_map/ppermute | solution.py:33
  318.1 16.4 %collective-permute-start.36 = (bf16[2,96,1536]{2,1,0:T(8,128)(2,1)}, bf16[2,96,1536]{2,1,0:T(8,128)(2,1)}, u32[]{:S(2)}, u32[]{:S(2)}) collective-permute-start(bf16[2,96,1536]{2,1,0:T(8,128)(2,1)} %add_convert_fusion.6), channel_id=1, source_target_pairs={{0,1},{1,0},{2,3},{3,2},{4,5},{5,4},{6,7},{7,6},{8,9},{9,8},{10,11... | collective-permute-start | bytes 1769480 | tf_op jit(solution)/shard_map/ppermute | solution.py:33
  371.2 15.7 %collective-permute-start.39 = (bf16[2,96,1536]{2,1,0:T(8,128)(2,1)S(1)}, bf16[2,96,1536]{2,1,0:T(8,128)(2,1)S(1)}, u32[]{:S(2)}, u32[]{:S(2)}) collective-permute-start(bf16[2,96,1536]{2,1,0:T(8,128)(2,1)S(1)} %slice.906), channel_id=1, source_target_pairs={{0,2},{1,3},{2,0},{3,1},{4,6},{5,7},{6,4},{7,5},{8,10},{9,11},{10,... | collective-permute-start | bytes 1769480 | tf_op jit(solution)/shard_map/ppermute | solution.py:33
  377.0 53.2 %collective-permute-start.43 = (bf16[768,1536]{1,0:T(8,128)(2,1)S(1)}, bf16[768,1536]{1,0:T(8,128)(2,1)S(1)}, u32[]{:S(2)}, u32[]{:S(2)}) collective-permute-start(bf16[768,1536]{1,0:T(8,128)(2,1)S(1)} %copy-done.90), channel_id=1, source_target_pairs={{16,0},{0,16},{17,1},{1,17},{18,2},{2,18},{19,3},{3,19},{20,4},{4,... | collective-permute-start | bytes 7077896 | tf_op jit(solution)/shard_map/ppermute | solution.py:29
  408.9 14.7 %collective-permute-start.40 = (bf16[2,96,1536]{2,1,0:T(8,128)(2,1)S(1)}, bf16[2,96,1536]{2,1,0:T(8,128)(2,1)S(1)}, u32[]{:S(2)}, u32[]{:S(2)}) collective-permute-start(bf16[2,96,1536]{2,1,0:T(8,128)(2,1)S(1)} %get-tuple-element.201), channel_id=1, source_target_pairs={{0,2},{1,3},{2,0},{3,1},{4,6},{5,7},{6,4},{7,5},{8,10},{9,11},{10,... | collective-permute-start | bytes 1769480 | tf_op jit(solution)/shard_map/ppermute | solution.py:33
  410.5 16.1 %collective-permute-start.41 = (bf16[2,96,1536]{2,1,0:T(8,128)(2,1)S(1)}, bf16[2,96,1536]{2,1,0:T(8,128)(2,1)S(1)}, u32[]{:S(2)}, u32[]{:S(2)}) collective-permute-start(bf16[2,96,1536]{2,1,0:T(8,128)(2,1)S(1)} %get-tuple-element.201), channel_id=1, source_target_pairs={{0,1},{1,0},{2,3},{3,2},{4,5},{5,4},{6,7},{7,6},{8,9},{9,8},{10,11... | collective-permute-start | bytes 1769480 | tf_op jit(solution)/shard_map/ppermute | solution.py:33
  426.1 35.8 %collective-permute-start.49 = (bf16[1536,1536]{1,0:T(8,128)(2,1)}, bf16[1536,1536]{1,0:T(8,128)(2,1)}, u32[]{:S(2)}, u32[]{:S(2)}) collective-permute-start(bf16[1536,1536]{1,0:T(8,128)(2,1)} %pad_maximum_fusion.2), channel_id=1, source_target_pairs={{0,1},{1,0},{2,3},{3,2},{4,5},{5,4},{6,7},{7,6},{8,9},{9,8},{10,11... | collective-permute-start | bytes 14155784 | tf_op jit(solution)/shard_map/ppermute | solution.py:33
  432.5 166.0 %reduce-scatter.7.cloned.1.call-start = ((), (), s32[]{:S(2)}) async-start(), calls=%async_computation.9 | async-start | bytes 2949120 | tf_op jit(solution)/shard_map/reduce_scatter | solution.py:581
  436.7 56.0 %collective-permute-start.50 = (bf16[768,1536]{1,0:T(8,128)(2,1)S(1)}, bf16[768,1536]{1,0:T(8,128)(2,1)}, u32[]{:S(2)}, u32[]{:S(2)}) collective-permute-start(bf16[768,1536]{1,0:T(8,128)(2,1)S(1)} %copy-done.89), channel_id=1, source_target_pairs={{16,0},{0,16},{17,1},{1,17},{18,2},{2,18},{19,3},{3,19},{20,4},{4,... | collective-permute-start | bytes 7077896 | tf_op jit(solution)/shard_map/ppermute | solution.py:29
  445.4 16.5 %collective-permute-start.46 = (bf16[384,192]{1,0:T(8,128)(2,1)S(1)}, bf16[384,192]{1,0:T(8,128)(2,1)S(1)}, u32[]{:S(2)}, u32[]{:S(2)}) collective-permute-start(bf16[384,192]{1,0:T(8,128)(2,1)S(1)} %get-tuple-element.230), channel_id=1, source_target_pairs={{4,0},{8,4},{12,8},{0,12},{5,1},{9,5},{13,9},{1,13},{6,2},{10,6},{... | collective-permute-start | bytes 442376 | tf_op jit(solution)/shard_map/ppermute | solution.py:25
  467.4 88.3 %collective-permute-start.52 = (bf16[1536,768]{1,0:T(8,128)(2,1)}, bf16[1536,768]{1,0:T(8,128)(2,1)}, u32[]{:S(2)}, u32[]{:S(2)}) collective-permute-start(bf16[1536,768]{1,0:T(8,128)(2,1)} %pad_maximum_fusion.7), channel_id=1, source_target_pairs={{0,2},{1,3},{2,0},{3,1},{4,6},{5,7},{6,4},{7,5},{8,10},{9,11},{10,... | collective-permute-start | bytes 7077896 | tf_op jit(solution)/shard_map/ppermute | solution.py:33
  469.0 16.3 %collective-permute-start.45 = (bf16[384,192]{1,0:T(8,128)(2,1)S(1)}, bf16[384,192]{1,0:T(8,128)(2,1)S(1)}, u32[]{:S(2)}, u32[]{:S(2)}) collective-permute-start(bf16[384,192]{1,0:T(8,128)(2,1)S(1)} %get-tuple-element.231), channel_id=1, source_target_pairs={{8,0},{12,4},{0,8},{4,12},{9,1},{13,5},{1,9},{5,13},{10,2},{14,6},... | collective-permute-start | bytes 442376 | tf_op jit(solution)/shard_map/ppermute | solution.py:25
  469.0 22.6 %collective-permute-start.44 = (bf16[384,192]{1,0:T(8,128)(2,1)S(1)}, bf16[384,192]{1,0:T(8,128)(2,1)S(1)}, u32[]{:S(2)}, u32[]{:S(2)}) collective-permute-start(bf16[384,192]{1,0:T(8,128)(2,1)S(1)} %get-tuple-element.232), channel_id=1, source_target_pairs={{12,0},{0,4},{4,8},{8,12},{13,1},{1,5},{5,9},{9,13},{14,2},{2,6},{... | collective-permute-start | bytes 442376 | tf_op jit(solution)/shard_map/ppermute | solution.py:25
  500.1 146.4 %reduce-scatter.9.cloned.1.call-start = ((), (), s32[]{:S(2)}) async-start(), calls=%async_computation.10 | async-start | bytes 2211840 | tf_op jit(solution)/shard_map/reduce_scatter | solution.py:581
  527.6 28.1 %collective-permute-start.51 = (bf16[384,576]{1,0:T(8,128)(2,1)S(1)}, bf16[384,576]{1,0:T(8,128)(2,1)S(1)}, u32[]{:S(2)}, u32[]{:S(2)}) collective-permute-start(bf16[384,576]{1,0:T(8,128)(2,1)S(1)} %get-tuple-element.222), channel_id=1, source_target_pairs={{4,0},{8,4},{12,8},{0,12},{5,1},{9,5},{13,9},{1,13},{6,2},{10,6},{... | collective-permute-start | bytes 1327112 | tf_op jit(solution)/shard_map/ppermute | solution.py:25
  530.1 31.6 %collective-permute-start.55 = (bf16[768,384]{1,0:T(8,128)(2,1)S(1)}, bf16[768,384]{1,0:T(8,128)(2,1)S(1)}, u32[]{:S(2)}, u32[]{:S(2)}) collective-permute-start(bf16[768,384]{1,0:T(8,128)(2,1)S(1)} %convolution_convert_fusion.9), channel_id=1, source_target_pairs={{16,0},{0,16},{17,1},{1,17},{18,2},{2,18},{19,3},{3,19},{20,4},{4,... | collective-permute-start | bytes 1769480 | tf_op jit(solution)/shard_map/ppermute | solution.py:29
  560.0 27.9 %collective-permute-start.54 = (bf16[768,768]{1,0:T(8,128)(2,1)S(1)}, bf16[768,768]{1,0:T(8,128)(2,1)S(1)}, u32[]{:S(2)}, u32[]{:S(2)}) collective-permute-start(bf16[768,768]{1,0:T(8,128)(2,1)S(1)} %pad_maximum_fusion.14), channel_id=1, source_target_pairs={{16,0},{0,16},{17,1},{1,17},{18,2},{2,18},{19,3},{3,19},{20,4},{4,... | collective-permute-start | bytes 3538952 | tf_op jit(solution)/shard_map/ppermute | solution.py:29
  561.6 14.9 %collective-permute-start.56 = (bf16[128,768]{1,0:T(8,128)(2,1)S(1)}, bf16[128,768]{1,0:T(8,128)(2,1)S(1)}, u32[]{:S(2)}, u32[]{:S(2)}) collective-permute-start(bf16[128,768]{1,0:T(8,128)(2,1)S(1)} %convert_element_type.261), channel_id=1, source_target_pairs={{0,4},{4,0},{8,12},{12,8},{1,5},{5,1},{9,13},{13,9},{2,6},{6,2},{1... | collective-permute-start | bytes 589832 | tf_op jit(solution)/shard_map/ppermute | solution.py:662
  562.5 31.7 %collective-permute-start.57 = (bf16[384,576]{1,0:T(8,128)(2,1)S(1)}, bf16[384,576]{1,0:T(8,128)(2,1)S(1)}, u32[]{:S(2)}, u32[]{:S(2)}) collective-permute-start(bf16[384,576]{1,0:T(8,128)(2,1)S(1)} %get-tuple-element.220), channel_id=1, source_target_pairs={{12,0},{0,4},{4,8},{8,12},{13,1},{1,5},{5,9},{9,13},{14,2},{2,6},{... | collective-permute-start | bytes 1327112 | tf_op jit(solution)/shard_map/ppermute | solution.py:25
  562.6 31.7 %collective-permute-start.53 = (bf16[384,576]{1,0:T(8,128)(2,1)S(1)}, bf16[384,576]{1,0:T(8,128)(2,1)}, u32[]{:S(2)}, u32[]{:S(2)}) collective-permute-start(bf16[384,576]{1,0:T(8,128)(2,1)S(1)} %get-tuple-element.221), channel_id=1, source_target_pairs={{8,0},{12,4},{0,8},{4,12},{9,1},{13,5},{1,9},{5,13},{10,2},{14,6},... | collective-permute-start | bytes 1327112 | tf_op jit(solution)/shard_map/ppermute | solution.py:25
  598.2 112.1 %reduce-scatter.11.cloned.1.call-start = ((), (), s32[]{:S(2)}) async-start(), calls=%async_computation.11 | async-start | bytes 2211840 | tf_op jit(solution)/shard_map/reduce_scatter | solution.py:581
  615.2 25.2 %collective-permute-start.60 = (bf16[128,768]{1,0:T(8,128)(2,1)S(1)}, bf16[128,768]{1,0:T(8,128)(2,1)S(1)}, u32[]{:S(2)}, u32[]{:S(2)}) collective-permute-start(bf16[128,768]{1,0:T(8,128)(2,1)S(1)} %convert_element_type.268), channel_id=1, source_target_pairs={{0,8},{4,12},{8,0},{12,4},{1,9},{5,13},{9,1},{13,5},{2,10},{6,14},... | collective-permute-start | bytes 589832 | tf_op jit(solution)/shard_map/ppermute | solution.py:662
  618.7 41.1 %collective-permute-start.61 = (bf16[768,1152]{1,0:T(8,128)(2,1)}, bf16[768,1152]{1,0:T(8,128)(2,1)}, u32[]{:S(2)}, u32[]{:S(2)}) collective-permute-start(bf16[768,1152]{1,0:T(8,128)(2,1)} %convolution_convert_fusion.5), channel_id=1, source_target_pairs={{16,0},{0,16},{17,1},{1,17},{18,2},{2,18},{19,3},{3,19},{20,4},{4,... | collective-permute-start | bytes 5308424 | tf_op jit(solution)/shard_map/ppermute | solution.py:29
  622.3 22.9 %collective-permute-start.59 = (bf16[2,96,1536]{2,1,0:T(8,128)(2,1)S(1)}, bf16[2,96,1536]{2,1,0:T(8,128)(2,1)S(1)}, u32[]{:S(2)}, u32[]{:S(2)}) collective-permute-start(bf16[2,96,1536]{2,1,0:T(8,128)(2,1)S(1)} %slice.905), channel_id=1, source_target_pairs={{0,2},{1,3},{2,0},{3,1},{4,6},{5,7},{6,4},{7,5},{8,10},{9,11},{10,... | collective-permute-start | bytes 1769480 | tf_op jit(solution)/shard_map/ppermute | solution.py:33
  665.2 11.9 %collective-permute-start.62 = (f32[6,1536]{1,0:T(8,128)}, f32[6,1536]{1,0:T(8,128)}, u32[]{:S(2)}, u32[]{:S(2)}) collective-permute-start(f32[6,1536]{1,0:T(8,128)} %stack.179), channel_id=1, source_target_pairs={{0,1},{1,0},{2,3},{3,2},{4,5},{5,4},{6,7},{7,6},{8,9},{9,8},{10,11... | collective-permute-start | bytes 110600 | tf_op jit(solution)/shard_map/ppermute | solution.py:33
  672.3 15.7 %collective-permute-start.64 = (bf16[2,192,1536]{2,1,0:T(8,128)(2,1)S(1)}, bf16[2,192,1536]{2,1,0:T(8,128)(2,1)S(1)}, u32[]{:S(2)}, u32[]{:S(2)}) collective-permute-start(bf16[2,192,1536]{2,1,0:T(8,128)(2,1)S(1)} %slice.900), channel_id=1, source_target_pairs={{0,1},{1,0},{2,3},{3,2},{4,5},{5,4},{6,7},{7,6},{8,9},{9,8},{10,11... | collective-permute-start | bytes 3538952 | tf_op jit(solution)/shard_map/ppermute | solution.py:33
  673.8 12.6 %collective-permute-start.66 = (bf16[128,1536]{1,0:T(8,128)(2,1)S(1)}, bf16[128,1536]{1,0:T(8,128)(2,1)S(1)}, u32[]{:S(2)}, u32[]{:S(2)}) collective-permute-start(bf16[128,1536]{1,0:T(8,128)(2,1)S(1)} %get-tuple-element.287), channel_id=1, source_target_pairs={{0,1},{1,0},{2,3},{3,2},{4,5},{5,4},{6,7},{7,6},{8,9},{9,8},{10,11... | collective-permute-start | bytes 1179656 | tf_op jit(solution)/shard_map/ppermute | solution.py:33
  686.5 12.1 %collective-permute-start.67 = (bf16[128,1536]{1,0:T(8,128)(2,1)S(1)}, bf16[128,1536]{1,0:T(8,128)(2,1)S(1)}, u32[]{:S(2)}, u32[]{:S(2)}) collective-permute-start(bf16[128,1536]{1,0:T(8,128)(2,1)S(1)} %fusion.93), channel_id=1, source_target_pairs={{0,2},{1,3},{2,0},{3,1},{4,6},{5,7},{6,4},{7,5},{8,10},{9,11},{10,... | collective-permute-start | bytes 1179656 | tf_op jit(solution)/shard_map/ppermute | solution.py:33
  688.5 21.5 %collective-permute-start.65 = (bf16[2,96,1536]{2,1,0:T(8,128)(2,1)S(1)}, bf16[2,96,1536]{2,1,0:T(8,128)(2,1)S(1)}, u32[]{:S(2)}, u32[]{:S(2)}) collective-permute-start(bf16[2,96,1536]{2,1,0:T(8,128)(2,1)S(1)} %slice.904), channel_id=1, source_target_pairs={{0,2},{1,3},{2,0},{3,1},{4,6},{5,7},{6,4},{7,5},{8,10},{9,11},{10,... | collective-permute-start | bytes 1769480 | tf_op jit(solution)/shard_map/ppermute | solution.py:33
  (117 other events, 1294.8 us)
Sparse Core Ops, SparseCore 0:
  10.8 76.3 all-gather.4
  89.3 52.0 all-gather.6
  143.5 113.0 all-gather.8
  268.9 77.0 all-gather.10
  432.6 62.0 reduce-scatter.4
  500.2 54.3 reduce-scatter.6
  598.3 48.1 reduce-scatter.8
  665.4 38.6 reduce-scatter.10
